TPU v7x, 256 devices: a whole 4x4x8 slice. The times are simulated.
256 devices in a mesh: role: 4 (over y), atoms: 64 (over x, z, core).
Axes of the slice: x: 4, y: 4, z: 8, core: 2. Of those that a mesh axis runs over, the one named last changes fastest.
Arguments:
- features: bfloat16 [4, 64, 256, 256], P('role', 'atoms'), may hold values from -6 to 6
- positions: float32 [4, 64, 3, 256], P('role', 'atoms'), may hold values from 0 to 1, as said below
- neighbours: int32 [4, 64, 32, 256], P('role', 'atoms'), may hold values from 0 to 2304, as said below
- images: int32 [4, 64, 32, 256], P('role', 'atoms'), may hold values from 0 to 26
- wave: int32 [3, 2048], replicated, may hold values from -8 to 8, as said below
- kgain: float32 [256], replicated, may hold values from 0.5 to 4
- w_in: bfloat16 [256, 256], replicated, may hold values from -0.375 to 0.375
- w_query: bfloat16 [256, 256], replicated, may hold values from -0.375 to 0.375
- w_rbf: bfloat16 [64, 256], replicated, may hold values from -1.5 to 1.5
- b_rbf: float32 [256], replicated, may hold values from -4 to 4
- w_filter: bfloat16 [256, 256], replicated, may hold values from -0.375 to 0.375
- w_out: bfloat16 [256, 256], replicated, may hold values from -0.375 to 0.375
Outputs:
- updated: bfloat16 [4, 64, 256, 256], P('role', 'atoms')
Inputs may be any that keep to these rules, and one draw needn't show every extreme that they name: `neighbours`: an entry (p * 3 + q) * 256 + t names atom t of the brick offset by p - 1 along the first and q - 1 along the second brick dimension, periodically; 2304 marks an empty slot. Empty slots come last; every list has 16 or more entries, and every brick has a full list. `positions`: atom coordinates of brick (a, b) lie in [a / 4, (a + 1) / 4) x [b / 64, (b + 1) / 64) x [0, 1). No wave vector has all three indices zero.
All inputs are finite; a program needn't handle non-finite values.
Results may differ from a plain program's by a relative error of at most 0.0085.
Values may be sent and summed in bfloat16 or wider, within the bound.
No kernel may reach another device: no remote copies, remote signals or barrier semaphores. Data moves between devices by JAX's collectives and lax.ppermute only.
A program may use at most 128 MiB of HBM per device.

v0:
```python
import functools
import math

import jax
import jax.numpy as jnp
from jax import lax
from jax.experimental import pallas as pl
from jax.experimental.pallas import tpu as pltpu
from jax.sharding import PartitionSpec as P

box_side = 1.0
soft_sq = 0.01
damping = 64.0
ewald_scale = 0.25
SINE = (
    3.1415925800428712,
    -5.16770687881004,
    2.550031375353375,
    -0.5980451625033413,
    0.07722010591476362,
)
VMEM = pl.BlockSpec(memory_space=pltpu.VMEM)


def call(body, out, ins, scratch=(), flops=0, nbytes=0, trans=0, name=None):
    multiple = isinstance(out, (list, tuple))
    return pl.pallas_call(
        body,
        out_shape=out,
        in_specs=[VMEM] * len(ins),
        out_specs=[VMEM] * len(out) if multiple else VMEM,
        scratch_shapes=list(scratch),
        compiler_params=pltpu.CompilerParams(vmem_limit_bytes=48 << 20),
        cost_estimate=pl.CostEstimate(flops=flops, bytes_accessed=nbytes, transcendentals=trans),
        name=name,
    )(*ins)


def dot(left, right):
    return jnp.dot(left, right, preferred_element_type=jnp.float32)


def cos_turns(turns):
    rest = turns - jnp.round(turns)
    square = rest * rest
    poly = SINE[4]
    for coef in SINE[3::-1]:
        poly = poly * square + coef
    sine = poly * rest
    return 1.0 - 2.0 * (sine * sine)


def structure_kernel(scale, *refs):
    rows_refs, (pos_ref, wave_ref, wq_ref, out_ref, table, queries) = refs[:4], refs[4:]
    atoms = rows_refs[0].shape[0]
    weight = wq_ref[...]
    for i, rows in enumerate(rows_refs):
        queries[i * atoms : (i + 1) * atoms, :] = dot(rows[...], weight).astype(jnp.bfloat16)
    step = 128

    def block(j, carry):
        part = pl.ds(pl.multiple_of(j * step, step), step)
        waves = wave_ref[part, :]
        turns = (
            waves[:, 0:1] * pos_ref[0:1, :]
            + waves[:, 1:2] * pos_ref[1:2, :]
            + waves[:, 2:3] * pos_ref[2:3, :]
            - waves[:, 3:4]
        )
        table[part, :] = cos_turns(turns).astype(jnp.bfloat16)
        out_ref[part, :] = (dot(table[part, :], queries[...]) * scale).astype(jnp.bfloat16)
        return carry

    lax.fori_loop(0, wave_ref.shape[0] // step, block, 0)


def table_kernel(pos_ref, wave_ref, out_ref):
    step = 128

    def block(j, carry):
        part = pl.ds(pl.multiple_of(j * step, step), step)
        pos = pos_ref[part, :]
        turns = (
            pos[:, 0:1] * wave_ref[0:1, :]
            + pos[:, 1:2] * wave_ref[1:2, :]
            + pos[:, 2:3] * wave_ref[2:3, :]
            - wave_ref[3:4, :]
        )
        out_ref[part, :] = cos_turns(turns).astype(jnp.bfloat16)
        return carry

    lax.fori_loop(0, pos_ref.shape[0] // step, block, 0)


def ewald_kernel(table_ref, filtered_ref, out_ref):
    bricks, atoms, _ = out_ref.shape
    for i in range(bricks):
        part = table_ref[i * atoms : (i + 1) * atoms, :]
        out_ref[i] = dot(part, filtered_ref[...]).astype(jnp.bfloat16)


def final_kernel(rows_ref, short_ref, e0_ref, e1_ref, e2_ref, e3_ref, wout_ref, out_ref):
    total = short_ref[...]
    for ref in (e0_ref, e1_ref, e2_ref, e3_ref):
        total = total + ref[...].astype(jnp.float32)
    moved = dot(total.astype(jnp.bfloat16), wout_ref[...])
    out_ref[...] = (rows_ref[...].astype(jnp.float32) + moved).astype(jnp.bfloat16)


def short_kernel(scale, *refs):
    rows_refs = refs[:9]
    pos_ref, slots_ref, images_ref, own_ref, win_ref, wrbf_ref, brbf_ref, wf_ref = refs[9:17]
    out_ref, hidden, turned, dist_cols, brick_cols, atom_cols, hot = refs[17:]
    slots, atoms = slots_ref.shape
    basis_count = wrbf_ref.shape[0]
    width = wf_ref.shape[1]
    weight = win_ref[...]
    for i, rows in enumerate(rows_refs):
        hidden[i * atoms : (i + 1) * atoms, :] = dot(rows[...], weight).astype(jnp.bfloat16)
    zoom = (basis_count / 4.0) * math.sqrt(math.log2(math.e))
    lane = 128
    for half in range(atoms // lane):
        cut = slice(half * lane, (half + 1) * lane)
        index = slots_ref[:, cut]
        image = images_ref[:, cut]
        place = index & (lane - 1)
        group = index >> 7
        near = [jnp.zeros((slots, lane), jnp.float32) for _ in range(3)]
        for r in range(9 * atoms // lane):
            here = group == r
            for c in range(3):
                table = jnp.broadcast_to(
                    pos_ref[c : c + 1, r * lane : (r + 1) * lane], (slots, lane)
                )
                taken = jnp.take_along_axis(table, place, axis=1, mode="promise_in_bounds")
                near[c] = jnp.where(here, taken, near[c])
        first = (image >= 9).astype(jnp.int32) + (image >= 18).astype(jnp.int32)
        inside = image - 9 * first
        second = (inside >= 3).astype(jnp.int32) + (inside >= 6).astype(jnp.int32)
        third = inside - 3 * second
        square = jnp.zeros((slots, lane), jnp.float32)
        for c, offset in enumerate((first, second, third)):
            delta = near[c] + (offset - 1).astype(jnp.float32) * box_side - own_ref[c : c + 1, cut]
            square = square + delta * delta
        turned[0:slots, cut] = jnp.sqrt(square + soft_sq) * zoom
        turned[slots : 2 * slots, cut] = (index >> 8).astype(jnp.float32)
        turned[2 * slots : 3 * slots, cut] = (index & (atoms - 1)).astype(jnp.float32)
        turned[3 * slots : 4 * slots, cut] = jnp.zeros((slots, lane), jnp.float32)
    columns = turned[...].T
    low = lax.broadcasted_iota(jnp.int32, (atoms, lane), 1) < basis_count
    for s in range(slots):
        brick_cols[s] = jnp.broadcast_to(
            columns[:, slots + s : slots + s + 1], (atoms, lane)
        ).astype(jnp.bfloat16)
        atom_cols[s] = jnp.broadcast_to(
            columns[:, 2 * slots + s : 2 * slots + s + 1], (atoms, lane)
        ).astype(jnp.bfloat16)
    for j in range(slots // 2):
        dist_cols[j] = jnp.where(
            low,
            jnp.broadcast_to(columns[:, 2 * j : 2 * j + 1], (atoms, lane)),
            jnp.broadcast_to(columns[:, 2 * j + 1 : 2 * j + 2], (atoms, lane)),
        )
    out_ref[...] = jnp.zeros_like(out_ref)
    centers = (
        (lax.broadcasted_iota(jnp.int32, (1, lane), 1) & (basis_count - 1)).astype(jnp.float32)
        * (4.0 / (basis_count - 1))
        * zoom
    )
    numbers = lax.broadcasted_iota(jnp.int32, (atoms, lane), 1).astype(jnp.float32)
    one = jnp.ones((atoms, lane), jnp.bfloat16)
    zero = jnp.zeros((atoms, lane), jnp.bfloat16)
    numbers_low = numbers.astype(jnp.bfloat16)
    numbers_high = (numbers + float(lane)).astype(jnp.bfloat16)
    none = jnp.full((atoms, lane), -1.0, jnp.bfloat16)
    bias = brbf_ref[...]

    def pair(j, carry):
        offset = dist_cols[j] - centers
        basis = jnp.exp2(-(offset * offset)).astype(jnp.bfloat16)
        for k in range(2):
            s = 2 * j + k
            part = basis[:, k * basis_count : (k + 1) * basis_count]
            value = dot(part, wrbf_ref[...]) + bias
            inner = (jnp.log(1.0 + jnp.exp(value)) - math.log(2.0)).astype(jnp.bfloat16)
            filters = dot(inner, wf_ref[...])
            brick = brick_cols[s]
            atom = atom_cols[s]
            for b in range(9):
                mine = jnp.where(brick == jnp.bfloat16(b), atom, none)
                hot[:, b * atoms : b * atoms + lane] = jnp.where(mine == numbers_low, one, zero)
                hot[:, b * atoms + lane : (b + 1) * atoms] = jnp.where(
                    mine == numbers_high, one, zero
                )
            gathered = dot(hot[...], hidden[...])
            out_ref[...] += filters * gathered
        return carry

    lax.fori_loop(0, slots // 2, pair, 0)
    out_ref[...] = out_ref[...] * scale


def local(
    features,
    positions,
    neighbours,
    images,
    wave,
    kgain,
    w_in,
    w_query,
    w_rbf,
    b_rbf,
    w_filter,
    w_out,
):
    f32, bf16 = jnp.float32, jnp.bfloat16
    rows = features[0, 0]
    place = positions[0, 0]
    atoms, width = rows.shape
    slots = neighbours.shape[2]
    roles = lax.axis_size("role")
    columns = lax.axis_size("atoms")
    atom_total = atoms * roles * columns
    waves = wave.shape[1]
    share = waves // roles
    piece = share // columns
    role = lax.axis_index("role")
    column = lax.axis_index("atoms")

    def from_role(block, shift):
        return lax.ppermute(block, "role", [((i + shift) % roles, i) for i in range(roles)])

    def from_column(block, shift):
        return lax.ppermute(
            block, "atoms", [((i + shift) % columns, i) for i in range(columns)]
        )

    shifts = (1, roles - 1, 2)
    place_of = {0: place, **{d: from_role(place, d) for d in shifts}}
    rows_of = {0: rows, **{d: from_role(rows, d) for d in shifts}}
    order = (0,) + shifts

    own_waves = lax.dynamic_slice_in_dim(wave, role * share, share, axis=1).astype(f32)
    phase = jnp.broadcast_to(
        jnp.asarray([0.0, 0.25], f32)[None, None, :, None], (1, columns, 2, piece)
    ).reshape(1, 2 * share)
    doubled = jnp.broadcast_to(
        own_waves.reshape(3, columns, 1, piece), (3, columns, 2, piece)
    ).reshape(3, 2 * share)
    wave_rows = jnp.concatenate([doubled, phase], axis=0)
    wave_cols = wave_rows.T
    group_pos = jnp.concatenate([place_of[d] for d in order], axis=1)

    partial = call(
        functools.partial(structure_kernel, atom_total ** (-0.5)),
        jax.ShapeDtypeStruct((2 * share, width), bf16),
        [rows_of[d] for d in order] + [group_pos, wave_cols, w_query],
        scratch=[
            pltpu.VMEM((2 * share, roles * atoms), bf16),
            pltpu.VMEM((roles * atoms, width), bf16),
        ],
        flops=2 * 2 * share * roles * atoms * width,
        nbytes=4 << 20,
        name="structure",
    )
    chunks = partial.reshape(columns, 2 * piece, width)
    mine = lax.all_to_all(chunks, "atoms", 0, 0)
    total = jnp.sum(mine.astype(f32), axis=0)

    my_waves = lax.dynamic_slice_in_dim(
        wave, role * share + column * piece, piece, axis=1
    ).astype(f32)
    squares = jnp.sum(my_waves * my_waves, axis=0)
    k_filter = ewald_scale * kgain[None, :] * (jnp.exp(-squares / damping) / squares)[:, None]
    filtered = (total.reshape(2, piece, width) * k_filter[None]).astype(bf16)
    copies = jnp.broadcast_to(
        filtered.reshape(1, 2 * piece, width), (columns, 2 * piece, width)
    )
    everyone = lax.all_to_all(copies, "atoms", 0, 0).reshape(2 * share, width)

    near_rows = {}
    near_pos = {}
    triple = (roles - 1, 0, 1)
    stack_rows = jnp.stack([rows_of[d] for d in triple])
    stack_pos = jnp.stack([place_of[d] for d in triple])
    for q, step in ((0, columns - 1), (2, 1)):
        got_rows = from_column(stack_rows, step)
        got_pos = from_column(stack_pos, step)
        for p in range(3):
            near_rows[p, q] = got_rows[p]
            near_pos[p, q] = got_pos[p]
    for p, d in enumerate(triple):
        near_rows[p, 1] = rows_of[d]
        near_pos[p, 1] = place_of[d]
    window = [(p, q) for p in range(3) for q in range(3)]
    near_table = jnp.concatenate([near_pos[w] for w in window], axis=1)
    short = call(
        functools.partial(short_kernel, slots ** (-0.5)),
        jax.ShapeDtypeStruct((atoms, width), f32),
        [near_rows[w] for w in window]
        + [
            near_table,
            neighbours[0, 0],
            images[0, 0],
            place,
            w_in,
            w_rbf,
            b_rbf[None, :],
            w_filter,
        ],
        scratch=[
            pltpu.VMEM((9 * atoms, width), bf16),
            pltpu.VMEM((4 * slots, atoms), f32),
            pltpu.VMEM((slots // 2, atoms, 128), f32),
            pltpu.VMEM((slots, atoms, 128), bf16),
            pltpu.VMEM((slots, atoms, 128), bf16),
            pltpu.VMEM((atoms, 9 * atoms), bf16),
        ],
        flops=2 * slots * atoms * 9 * atoms * width,
        nbytes=4 << 20,
        name="short",
    )
    table = call(
        table_kernel,
        jax.ShapeDtypeStruct((roles * atoms, 2 * share), bf16),
        [group_pos.T, wave_rows],
        nbytes=4 << 20,
        name="table",
    )
    parts = call(
        ewald_kernel,
        jax.ShapeDtypeStruct((roles, atoms, width), bf16),
        [table, everyone],
        flops=2 * 2 * share * roles * atoms * width,
        nbytes=4 << 20,
        name="ewald",
    )
    back = [parts[0]] + [from_role(parts[1 + i], roles - d) for i, d in enumerate(shifts)]
    result = call(
        final_kernel,
        jax.ShapeDtypeStruct((atoms, width), bf16),
        [rows, short] + back + [w_out],
        flops=2 * atoms * width * width,
        nbytes=1 << 20,
        name="final",
    )
    return result[None, None]


def solution(mesh):
    in_specs = (
        P("role", "atoms", None, None),
        P("role", "atoms", None, None),
        P("role", "atoms", None, None),
        P("role", "atoms", None, None),
        P(),
        P(),
        P(),
        P(),
        P(),
        P(),
        P(),
        P(),
    )
    out_specs = P("role", "atoms", None, None)
    return jax.shard_map(local, mesh=mesh, in_specs=in_specs, out_specs=out_specs, check_vma=False)
```

profile of v0, /device:TPU:24, one launch (start us, length us, event | category | flops | bytes accessed | tf_op | source)
XLA Modules:
  0.0 123.8 jit_solution(7186985568430356967)
XLA Ops:
  0.0 0.7 copy.32
  0.7 1.2 collective-permute-start.8
  1.9 1.6 %collective-permute-start.5 = (f32[3,256]{1,0:T(4,128)S(1)}, f32[3,256]{1,0:T(4,128)S(1)}, u32[]{:S(2)}, u32[]{:S(2)}) collective-permute-start(f32[3,256]{1,0:T(4,128)S(1)} %bitcast.81), channel_id=1, source_target_pairs={{64,0},{128,64},{192,128},{0,192},{65,1},{129,65},{193,129},{1,193... | collective-permute-start | bytes 9224 | tf_op jit(solution)/shard_map/ppermute | solution.py:232
  3.5 1.7 %collective-permute-start.4 = (f32[3,256]{1,0:T(4,128)S(1)}, f32[3,256]{1,0:T(4,128)S(1)}, u32[]{:S(2)}, u32[]{:S(2)}) collective-permute-start(f32[3,256]{1,0:T(4,128)S(1)} %bitcast.82), channel_id=1, source_target_pairs={{192,0},{0,64},{64,128},{128,192},{193,1},{1,65},{65,129},{129,193... | collective-permute-start | bytes 9224 | tf_op jit(solution)/shard_map/ppermute | solution.py:232
  5.2 1.1 collective-permute-start.9
  6.2 0.7 collective-permute-start.1
  7.0 0.8 multiply_reduce_fusion
  7.8 0.7 broadcast_multiply_fusion.1
  8.5 0.7 dynamic-slice_convert_fusion
  9.2 0.7 broadcast_in_dim.32
  9.9 0.1 broadcast_in_dim.33
  10.0 0.1 broadcast_in_dim.30
  10.2 0.1 broadcast_in_dim.31
  10.2 0.0 copy-start
  10.2 0.3 reshape.65
  10.5 0.7 broadcast_multiply_fusion
  11.2 0.7 copy.25
  11.9 0.2 copy.27
  12.1 0.0 collective-permute-done.5
  12.2 2.6 %collective-permute-start = (bf16[256,256]{1,0:T(8,128)(2,1)}, bf16[256,256]{1,0:T(8,128)(2,1)S(1)}, u32[]{:S(2)}, u32[]{:S(2)}) collective-permute-start(bf16[256,256]{1,0:T(8,128)(2,1)} %bitcast.73), channel_id=1, source_target_pairs={{192,0},{0,64},{64,128},{128,192},{193,1},{1,65},{65,129},{129,193... | collective-permute-start | bytes 393224 | tf_op jit(solution)/shard_map/ppermute | solution.py:232
  14.7 0.0 collective-permute-done.4
  14.7 0.6 pad_maximum_fusion.3
  15.3 5.8 %collective-permute-start.7 = (f32[3,3,256]{2,1,0:T(4,128)}, f32[3,3,256]{2,1,0:T(4,128)}, u32[]{:S(2)}, u32[]{:S(2)}) collective-permute-start(f32[3,3,256]{2,1,0:T(4,128)} %pad_maximum_fusion.3), channel_id=1, source_target_pairs={{1,0},{2,1},{3,2},{4,3},{5,4},{6,5},{7,6},{8,7},{9,8},{10,9},{11,1... | collective-permute-start | bytes 27656 | tf_op jit(solution)/shard_map/ppermute | solution.py:235
  21.1 0.0 collective-permute-done.8
  21.1 0.0 collective-permute-start.6
  21.2 0.6 pad_maximum_fusion.1
  21.8 0.2 copy.26.pos_ref
  22.0 0.0 copy-start.4
  22.0 3.7 %table.1.table_ref = bf16[1024,1024]{1,0:T(8,128)(2,1)S(1)} custom-call(f32[1024,3]{1,0:T(8,128)S(1)} %copy.26.pos_ref, f32[4,1024]{1,0:T(4,128)S(1)} %pad_maximum_fusion.2.wave_ref), custom_call_target="tpu_custom_call" | custom-call | bytes 4194304 | tf_op jit(solution)/shard_map/table/pallas_call | solution.py:27
  25.7 0.0 copy-start.21
  25.7 2.2 %collective-permute-done.6 = f32[3,3,256]{2,1,0:T(4,128)} collective-permute-done((f32[3,3,256]{2,1,0:T(4,128)}, f32[3,3,256]{2,1,0:T(4,128)}, u32[]{:S(2)}, u32[]{:S(2)}) %collective-permute-start.6) | collective-permute-done | bytes 9248 | tf_op jit(solution)/shard_map/ppermute | solution.py:235
  27.9 0.7 constant_dynamic-update-slice_fusion.8
  28.6 0.0 copy-start.9
  28.6 0.9 copy-done.9
  29.5 6.9 %structure.1 = bf16[1024,256]{1,0:T(8,128)(2,1)} custom-call(bf16[256,256]{1,0:T(8,128)(2,1)S(1)} %bitcast.74, bf16[256,256]{1,0:T(8,128)(2,1)S(1)} %collective-permute-done.1.refs_7_.refs_1_, bf16[256,256]{1,0:T(8,128)(2,1)S(1)} %collective-permute-done.refs_1_.refs_2_, bf16[256,256]{1,0:T(8,128)(2,1)} %collective-permute-done.9.refs_3_, ...), custom_call_target="tpu_custom_call" | custom-call | flops 536870912 | bytes 4194304 | tf_op jit(solution)/shard_map/structure/pallas_call | solution.py:27
  36.4 5.3 %all-to-all-start = ((bf16[64,16,256]{2,1,0:T(8,128)(2,1)}), bf16[64,16,256]{2,1,0:T(8,128)(2,1)S(1)}, u32[]{:S(2)}, u32[]{:S(2)}) async-start(bf16[64,16,256]{2,1,0:T(8,128)(2,1)} %bitcast.24), calls=%async_computation | async-start | bytes 1048576 | tf_op jit(solution)/shard_map/all_to_all | solution.py:268
  41.8 0.7 constant_dynamic-update-slice_fusion.6
  42.4 0.7 constant_dynamic-update-slice_fusion.5
  43.1 0.7 constant_dynamic-update-slice_fusion.3
  43.8 0.8 pad_maximum_fusion
  44.6 4.9 %collective-permute-start.3 = (bf16[3,256,256]{2,1,0:T(8,128)(2,1)}, bf16[3,256,256]{2,1,0:T(8,128)(2,1)}, u32[]{:S(2)}, u32[]{:S(2)}) collective-permute-start(bf16[3,256,256]{2,1,0:T(8,128)(2,1)} %pad_maximum_fusion), channel_id=1, source_target_pairs={{1,0},{2,1},{3,2},{4,3},{5,4},{6,5},{7,6},{8,7},{9,8},{10,9},{11,1... | collective-permute-start | bytes 1179656 | tf_op jit(solution)/shard_map/ppermute | solution.py:235
  49.6 9.2 %all-to-all-done = bf16[64,16,256]{2,1,0:T(8,128)(2,1)S(1)} async-done(((bf16[64,16,256]{2,1,0:T(8,128)(2,1)}), bf16[64,16,256]{2,1,0:T(8,128)(2,1)S(1)}, u32[]{:S(2)}, u32[]{:S(2)}) %all-to-all-start) | async-done | bytes 524320 | tf_op jit(solution)/shard_map/all_to_all | solution.py:268
  58.8 0.1 convert_reduce_fusion
  58.9 0.8 broadcast_in_dim.34
  59.7 6.5 %all-to-all-start.1 = ((bf16[64,16,256]{2,1,0:T(8,128)(2,1)}), bf16[64,16,256]{2,1,0:T(8,128)(2,1)S(1)}, u32[]{:S(2)}, u32[]{:S(2)}) async-start(bf16[64,16,256]{2,1,0:T(8,128)(2,1)} %broadcast_in_dim.34), calls=%async_computation.1 | async-start | bytes 1048576 | tf_op jit(solution)/shard_map/all_to_all | solution.py:280
  66.3 1.3 %constant_dynamic-update-slice_fusion.2 = f32[3,2304]{1,0:T(4,128)} fusion(f32[3,2304]{1,0:T(4,128)} %copy-done.7, f32[3,3,256]{2,1,0:T(4,128)} %collective-permute-done.6), kind=kLoop, calls=%fused_computation.14 | loop fusion | bytes 8192
  67.5 0.6 constant_dynamic-update-slice_fusion.1
  68.1 0.1 collective-permute-start.2
  68.2 1.3 %constant_dynamic-update-slice_fusion.refs_9_ = f32[3,2304]{1,0:T(4,128)} fusion(f32[3,2304]{1,0:T(4,128)} %constant_dynamic-update-slice_fusion.1, f32[3,3,256]{2,1,0:T(4,128)} %collective-permute-done.7), kind=kLoop, calls=%fused_computation.12 | loop fusion | bytes 8192 | tf_op jit(solution)/shard_map/concatenate | solution.py:297
  69.5 1.1 slice_bitcast_fusion.4
  70.5 17.2 %collective-permute-done.2 = bf16[3,256,256]{2,1,0:T(8,128)(2,1)S(1)} collective-permute-done((bf16[3,256,256]{2,1,0:T(8,128)(2,1)}, bf16[3,256,256]{2,1,0:T(8,128)(2,1)S(1)}, u32[]{:S(2)}, u32[]{:S(2)}) %collective-permute-start.2) | collective-permute-done | bytes 393248 | tf_op jit(solution)/shard_map/ppermute | solution.py:235
  87.7 0.7 slice_bitcast_fusion.5
  88.4 0.0 copy-start.10
  88.5 0.0 copy-start.11
  88.5 0.0 copy-start.12
  88.5 0.0 copy-start.13
  88.5 0.0 copy-start.14
  88.5 0.0 copy-start.15
  88.5 0.7 ewald.1
  89.3 1.3 %collective-permute-start.12 = (bf16[256,256]{1,0:T(8,128)(2,1)S(1)}, bf16[256,256]{1,0:T(8,128)(2,1)S(1)}, u32[]{:S(2)}, u32[]{:S(2)}) collective-permute-start(bf16[256,256]{1,0:T(8,128)(2,1)S(1)} %get-tuple-element.5), channel_id=1, source_target_pairs={{128,0},{192,64},{0,128},{64,192},{129,1},{193,65},{1,129},{65,193... | collective-permute-start | bytes 393224 | tf_op jit(solution)/shard_map/ppermute | solution.py:232
  90.6 3.2 %collective-permute-start.10 = (bf16[256,256]{1,0:T(8,128)(2,1)S(1)}, bf16[256,256]{1,0:T(8,128)(2,1)S(1)}, u32[]{:S(2)}, u32[]{:S(2)}) collective-permute-start(bf16[256,256]{1,0:T(8,128)(2,1)S(1)} %get-tuple-element.7), channel_id=1, source_target_pairs={{192,0},{0,64},{64,128},{128,192},{193,1},{1,65},{65,129},{129,193... | collective-permute-start | bytes 393224 | tf_op jit(solution)/shard_map/ppermute | solution.py:232
  93.9 0.0 copy-start.1
  93.9 28.9 %short.1.short_ref = f32[256,256]{1,0:T(8,128)S(1)} custom-call(bf16[256,256]{1,0:T(8,128)(2,1)S(1)} %copy-done.3, bf16[256,256]{1,0:T(8,128)(2,1)S(1)} %collective-permute-done.refs_1_.refs_2_, bf16[256,256]{1,0:T(8,128)(2,1)S(1)} %get-tuple-element.11.refs_2_, bf16[256,256]{1,0:T(8,128)(2,1)S(1)} %copy-done.2, bf16[256,256]{1,0:T(8,128)(2,1)S(1)} %bitcast.76, ...), custom_call_target="tpu_custom_call" | custom-call | flops 9663676416 | bytes 4194304 | tf_op jit(solution)/shard_map/short/pallas_call | solution.py:27
  122.9 0.9 final.1
  (48 shorter events, 0.2 us)
Async XLA Ops:
  0.7 21.1 %copy-start.5 = (f32[1,1,3,256]{3,2,1,0:T(4,128)}, f32[1,1,3,256]{3,2,1,0:T(4,128)S(1)}, u32[]{:S(2)}) copy-start(f32[1,1,3,256]{3,2,1,0:T(4,128)S(1)} %copy.32) | copy-start | bytes 9220
  0.7 20.5 %collective-permute-start.8 = (f32[3,256]{1,0:T(4,128)S(1)}, f32[3,256]{1,0:T(4,128)S(1)}, u32[]{:S(2)}, u32[]{:S(2)}) collective-permute-start(f32[3,256]{1,0:T(4,128)S(1)} %bitcast.80), channel_id=1, source_target_pairs={{128,0},{192,64},{0,128},{64,192},{129,1},{193,65},{1,129},{65,193... | collective-permute-start | bytes 9224 | tf_op jit(solution)/shard_map/ppermute | solution.py:232
  1.9 10.2 %collective-permute-start.5 = (f32[3,256]{1,0:T(4,128)S(1)}, f32[3,256]{1,0:T(4,128)S(1)}, u32[]{:S(2)}, u32[]{:S(2)}) collective-permute-start(f32[3,256]{1,0:T(4,128)S(1)} %bitcast.81), channel_id=1, source_target_pairs={{64,0},{128,64},{192,128},{0,192},{65,1},{129,65},{193,129},{1,193... | collective-permute-start | bytes 9224 | tf_op jit(solution)/shard_map/ppermute | solution.py:232
  3.5 11.3 %collective-permute-start.4 = (f32[3,256]{1,0:T(4,128)S(1)}, f32[3,256]{1,0:T(4,128)S(1)}, u32[]{:S(2)}, u32[]{:S(2)}) collective-permute-start(f32[3,256]{1,0:T(4,128)S(1)} %bitcast.82), channel_id=1, source_target_pairs={{192,0},{0,64},{64,128},{128,192},{193,1},{1,65},{65,129},{129,193... | collective-permute-start | bytes 9224 | tf_op jit(solution)/shard_map/ppermute | solution.py:232
  5.2 23.4 %collective-permute-start.9 = (bf16[256,256]{1,0:T(8,128)(2,1)}, bf16[256,256]{1,0:T(8,128)(2,1)}, u32[]{:S(2)}, u32[]{:S(2)}) collective-permute-start(bf16[256,256]{1,0:T(8,128)(2,1)} %bitcast.71), channel_id=1, source_target_pairs={{128,0},{192,64},{0,128},{64,192},{129,1},{193,65},{1,129},{65,193... | collective-permute-start | bytes 393224 | tf_op jit(solution)/shard_map/ppermute | solution.py:232
  6.2 22.3 %collective-permute-start.1 = (bf16[256,256]{1,0:T(8,128)(2,1)}, bf16[256,256]{1,0:T(8,128)(2,1)S(1)}, u32[]{:S(2)}, u32[]{:S(2)}) collective-permute-start(bf16[256,256]{1,0:T(8,128)(2,1)} %bitcast.72), channel_id=1, source_target_pairs={{64,0},{128,64},{192,128},{0,192},{65,1},{129,65},{193,129},{1,193... | collective-permute-start | bytes 393224 | tf_op jit(solution)/shard_map/ppermute | solution.py:232
  10.2 18.4 %copy-start = (bf16[1,1,256,256]{3,2,1,0:T(8,128)(2,1)S(1)}, bf16[1,1,256,256]{3,2,1,0:T(8,128)(2,1)}, u32[]{:S(2)}) copy-start(bf16[1,1,256,256]{3,2,1,0:T(8,128)(2,1)} %param.13) | copy-start | bytes 393220
  12.1 9.6 %copy-start.16 = (f32[3,256]{1,0:T(4,128)}, f32[3,256]{1,0:T(4,128)S(1)}, u32[]{:S(2)}) copy-start(f32[3,256]{1,0:T(4,128)S(1)} %collective-permute-done.5) | copy-start | bytes 9220
  12.2 16.4 %collective-permute-start = (bf16[256,256]{1,0:T(8,128)(2,1)}, bf16[256,256]{1,0:T(8,128)(2,1)S(1)}, u32[]{:S(2)}, u32[]{:S(2)}) collective-permute-start(bf16[256,256]{1,0:T(8,128)(2,1)} %bitcast.73), channel_id=1, source_target_pairs={{192,0},{0,64},{64,128},{128,192},{193,1},{1,65},{65,129},{129,193... | collective-permute-start | bytes 393224 | tf_op jit(solution)/shard_map/ppermute | solution.py:232
  14.7 7.0 %copy-start.18 = (f32[3,256]{1,0:T(4,128)}, f32[3,256]{1,0:T(4,128)S(1)}, u32[]{:S(2)}) copy-start(f32[3,256]{1,0:T(4,128)S(1)} %collective-permute-done.4) | copy-start | bytes 9220
  15.3 26.4 %collective-permute-start.7 = (f32[3,3,256]{2,1,0:T(4,128)}, f32[3,3,256]{2,1,0:T(4,128)}, u32[]{:S(2)}, u32[]{:S(2)}) collective-permute-start(f32[3,3,256]{2,1,0:T(4,128)} %pad_maximum_fusion.3), channel_id=1, source_target_pairs={{1,0},{2,1},{3,2},{4,3},{5,4},{6,5},{7,6},{8,7},{9,8},{10,9},{11,1... | collective-permute-start | bytes 27656 | tf_op jit(solution)/shard_map/ppermute | solution.py:235
  21.1 6.8 %collective-permute-start.6 = (f32[3,3,256]{2,1,0:T(4,128)}, f32[3,3,256]{2,1,0:T(4,128)}, u32[]{:S(2)}, u32[]{:S(2)}) collective-permute-start(f32[3,3,256]{2,1,0:T(4,128)} %pad_maximum_fusion.3), channel_id=1, source_target_pairs={{63,0},{0,1},{1,2},{2,3},{3,4},{4,5},{5,6},{6,7},{7,8},{8,9},{9,10... | collective-permute-start | bytes 27656 | tf_op jit(solution)/shard_map/ppermute | solution.py:235
  22.0 6.6 %copy-start.4 = (f32[3,1024]{1,0:T(4,128)S(1)}, f32[3,1024]{1,0:T(4,128)}, u32[]{:S(2)}) copy-start(f32[3,1024]{1,0:T(4,128)} %get-tuple-element.15.refs_4_) | copy-start | bytes 36868
  25.7 16.0 %copy-start.19 = (f32[3,256]{1,0:T(4,128)S(1)}, f32[3,256]{1,0:T(4,128)}, u32[]{:S(2)}) copy-start(f32[3,256]{1,0:T(4,128)} %copy-done.18) | copy-start | bytes 9220
  25.7 17.4 %copy-start.21 = (f32[1,1,3,256]{3,1,2,0:T(1,128)S(1)}, f32[1,1,3,256]{3,1,2,0:T(1,128)}, u32[]{:S(2)}) copy-start(f32[1,1,3,256]{3,1,2,0:T(1,128)} %param.14) | copy-start | bytes 9220
  28.6 0.9 copy-start.9
  29.5 29.4 %copy-start.20 = (f32[8,256]{1,0:T(8,128)S(1)}, f32[8,256]{1,0:T(8,128)}, u32[]{:S(2)}) copy-start(f32[8,256]{1,0:T(8,128)} %broadcast_multiply_fusion) | copy-start | bytes 24580
  36.4 31.1 %copy-start.17 = (f32[3,256]{1,0:T(4,128)S(1)}, f32[3,256]{1,0:T(4,128)}, u32[]{:S(2)}) copy-start(f32[3,256]{1,0:T(4,128)} %copy-done.16) | copy-start | bytes 9220
  36.4 22.4 %all-to-all-start = ((bf16[64,16,256]{2,1,0:T(8,128)(2,1)}), bf16[64,16,256]{2,1,0:T(8,128)(2,1)S(1)}, u32[]{:S(2)}, u32[]{:S(2)}) async-start(bf16[64,16,256]{2,1,0:T(8,128)(2,1)} %bitcast.24), calls=%async_computation | async-start | bytes 1048576 | tf_op jit(solution)/shard_map/all_to_all | solution.py:268
  43.8 15.9 %copy-start.7 = (f32[3,2304]{1,0:T(4,128)}, f32[3,2304]{1,0:T(4,128)S(1)}, u32[]{:S(2)}) copy-start(f32[3,2304]{1,0:T(4,128)S(1)} %constant_dynamic-update-slice_fusion.3) | copy-start | bytes 82948
  44.6 24.8 %collective-permute-start.3 = (bf16[3,256,256]{2,1,0:T(8,128)(2,1)}, bf16[3,256,256]{2,1,0:T(8,128)(2,1)}, u32[]{:S(2)}, u32[]{:S(2)}) collective-permute-start(bf16[3,256,256]{2,1,0:T(8,128)(2,1)} %pad_maximum_fusion), channel_id=1, source_target_pairs={{1,0},{2,1},{3,2},{4,3},{5,4},{6,5},{7,6},{8,7},{9,8},{10,9},{11,1... | collective-permute-start | bytes 1179656 | tf_op jit(solution)/shard_map/ppermute | solution.py:235
  59.7 28.7 %all-to-all-start.1 = ((bf16[64,16,256]{2,1,0:T(8,128)(2,1)}), bf16[64,16,256]{2,1,0:T(8,128)(2,1)S(1)}, u32[]{:S(2)}, u32[]{:S(2)}) async-start(bf16[64,16,256]{2,1,0:T(8,128)(2,1)} %broadcast_in_dim.34), calls=%async_computation.1 | async-start | bytes 1048576 | tf_op jit(solution)/shard_map/all_to_all | solution.py:280
  68.1 19.6 %collective-permute-start.2 = (bf16[3,256,256]{2,1,0:T(8,128)(2,1)}, bf16[3,256,256]{2,1,0:T(8,128)(2,1)S(1)}, u32[]{:S(2)}, u32[]{:S(2)}) collective-permute-start(bf16[3,256,256]{2,1,0:T(8,128)(2,1)} %pad_maximum_fusion), channel_id=1, source_target_pairs={{63,0},{0,1},{1,2},{2,3},{3,4},{4,5},{5,6},{6,7},{7,8},{8,9},{9,10... | collective-permute-start | bytes 1179656 | tf_op jit(solution)/shard_map/ppermute | solution.py:235
  88.4 5.4 %copy-start.2 = (bf16[256,256]{1,0:T(8,128)(2,1)S(1)}, bf16[256,256]{1,0:T(8,128)(2,1)}, u32[]{:S(2)}) copy-start(bf16[256,256]{1,0:T(8,128)(2,1)} %get-tuple-element.13.refs_3_) | copy-start | bytes 393220
  88.4 5.4 %copy-start.3 = (bf16[256,256]{1,0:T(8,128)(2,1)S(1)}, bf16[256,256]{1,0:T(8,128)(2,1)}, u32[]{:S(2)}) copy-start(bf16[256,256]{1,0:T(8,128)(2,1)} %get-tuple-element.14.refs_0_) | copy-start | bytes 393220
  88.4 5.4 %copy-start.6 = (f32[1,1,3,256]{3,2,1,0:T(4,128)S(1)}, f32[1,1,3,256]{3,2,1,0:T(4,128)}, u32[]{:S(2)}) copy-start(f32[1,1,3,256]{3,2,1,0:T(4,128)} %copy-done.5) | copy-start | bytes 9220
  88.4 5.4 %copy-start.8 = (f32[3,2304]{1,0:T(4,128)S(1)}, f32[3,2304]{1,0:T(4,128)}, u32[]{:S(2)}) copy-start(f32[3,2304]{1,0:T(4,128)} %constant_dynamic-update-slice_fusion.refs_9_) | copy-start | bytes 82948
  88.4 5.4 %copy-start.10 = (bf16[256,256]{1,0:T(8,128)(2,1)S(1)}, bf16[256,256]{1,0:T(8,128)(2,1)}, u32[]{:S(2)}) copy-start(bf16[256,256]{1,0:T(8,128)(2,1)} %refs_13_.1) | copy-start | bytes 393220
  88.5 5.4 %copy-start.11 = (bf16[256,256]{1,0:T(8,128)(2,1)S(1)}, bf16[256,256]{1,0:T(8,128)(2,1)}, u32[]{:S(2)}) copy-start(bf16[256,256]{1,0:T(8,128)(2,1)} %refs_16_.1) | copy-start | bytes 393220
  88.5 5.4 %copy-start.12 = (s32[1,1,32,256]{3,2,1,0:T(8,128)S(1)}, s32[1,1,32,256]{3,2,1,0:T(8,128)}, u32[]{:S(2)}) copy-start(s32[1,1,32,256]{3,2,1,0:T(8,128)} %param.15) | copy-start | bytes 98308
  88.5 5.4 %copy-start.13 = (s32[1,1,32,256]{3,2,1,0:T(8,128)S(1)}, s32[1,1,32,256]{3,2,1,0:T(8,128)}, u32[]{:S(2)}) copy-start(s32[1,1,32,256]{3,2,1,0:T(8,128)} %param.16) | copy-start | bytes 98308
  88.5 5.4 %copy-start.14 = (bf16[64,256]{1,0:T(8,128)(2,1)S(1)}, bf16[64,256]{1,0:T(8,128)(2,1)}, u32[]{:S(2)}) copy-start(bf16[64,256]{1,0:T(8,128)(2,1)} %refs_14_.1) | copy-start | bytes 98308
  88.5 5.4 %copy-start.15 = (f32[256]{0:T(256)S(1)}, f32[256]{0:T(256)}, u32[]{:S(2)}) copy-start(f32[256]{0:T(256)} %param.22) | copy-start | bytes 3076
  89.3 33.6 %collective-permute-start.12 = (bf16[256,256]{1,0:T(8,128)(2,1)S(1)}, bf16[256,256]{1,0:T(8,128)(2,1)S(1)}, u32[]{:S(2)}, u32[]{:S(2)}) collective-permute-start(bf16[256,256]{1,0:T(8,128)(2,1)S(1)} %get-tuple-element.5), channel_id=1, source_target_pairs={{128,0},{192,64},{0,128},{64,192},{129,1},{193,65},{1,129},{65,193... | collective-permute-start | bytes 393224 | tf_op jit(solution)/shard_map/ppermute | solution.py:232
  90.6 32.3 %collective-permute-start.11 = (bf16[256,256]{1,0:T(8,128)(2,1)S(1)}, bf16[256,256]{1,0:T(8,128)(2,1)S(1)}, u32[]{:S(2)}, u32[]{:S(2)}) collective-permute-start(bf16[256,256]{1,0:T(8,128)(2,1)S(1)} %get-tuple-element.6), channel_id=1, source_target_pairs={{64,0},{128,64},{192,128},{0,192},{65,1},{129,65},{193,129},{1,193... | collective-permute-start | bytes 393224 | tf_op jit(solution)/shard_map/ppermute | solution.py:232
  90.6 32.3 %collective-permute-start.10 = (bf16[256,256]{1,0:T(8,128)(2,1)S(1)}, bf16[256,256]{1,0:T(8,128)(2,1)S(1)}, u32[]{:S(2)}, u32[]{:S(2)}) collective-permute-start(bf16[256,256]{1,0:T(8,128)(2,1)S(1)} %get-tuple-element.7), channel_id=1, source_target_pairs={{192,0},{0,64},{64,128},{128,192},{193,1},{1,65},{65,129},{129,193... | collective-permute-start | bytes 393224 | tf_op jit(solution)/shard_map/ppermute | solution.py:232
  93.9 29.0 %copy-start.1 = (bf16[256,256]{1,0:T(8,128)(2,1)S(1)}, bf16[256,256]{1,0:T(8,128)(2,1)}, u32[]{:S(2)}) copy-start(bf16[256,256]{1,0:T(8,128)(2,1)} %wout_ref.1) | copy-start | bytes 393220
where the time goes:
time: 124 us
  Pallas kernels  41.1 us (33%)
  starting transfers between devices  36 us (29%)
  waiting for transfers between devices  28.6 us (23%)
  local copies, waits for them, and re-layouts  12.7 us (10%)
  other arithmetic  4.98 us (4%)
    pallas_call x5, Pallas kernels, call(): pl.pallas_call(body, out_shape=out, in_specs=[VMEM] * len(ins), out_specs...  41.1 us
    ppermute x4, waiting for transfers between devices, from_column(): lax.ppermute(block, 'atoms', [((i + shift) % columns, i) for i in range(c...  19.4 us
    ppermute x9, starting transfers between devices, from_role(): lax.ppermute(block, 'role', [((i + shift) % roles, i) for i in range(role...  13.4 us
    ppermute x4, starting transfers between devices, from_column(): lax.ppermute(block, 'atoms', [((i + shift) % columns, i) for i in range(c...  10.8 us
    all_to_all x1, waiting for transfers between devices, local(): mine = lax.all_to_all(chunks, 'atoms', 0, 0)  9.21 us
    all_to_all x1, starting transfers between devices, local(): everyone = lax.all_to_all(copies, 'atoms', 0, 0).reshape(2 * share, width)  6.53 us
    unnamed x53, local copies, waits for them, and re-layouts  6.29 us
    all_to_all x1, starting transfers between devices, local(): mine = lax.all_to_all(chunks, 'atoms', 0, 0)  5.29 us
  transfers between devices with their start and end apart: 15, of which 3 were waited for; matrix products, arithmetic and copies ran while one was open for 13% of the time, Pallas kernels for 32%

commit v1 on v0

v1 whole, which is shorter than its diff:
```python
import functools
import math

import jax
import jax.numpy as jnp
from jax import lax
from jax.experimental import pallas as pl
from jax.experimental.pallas import tpu as pltpu
from jax.sharding import PartitionSpec as P

box_side = 1.0
soft_sq = 0.01
damping = 64.0
ewald_scale = 0.25
SINE = (
    3.1415925800428712,
    -5.16770687881004,
    2.550031375353375,
    -0.5980451625033413,
    0.07722010591476362,
)
COSINE = (
    0.9999999534655706,
    -4.934792858503339,
    4.058411910098915,
    -1.331880131184001,
    0.21969673041819898,
)
ZOOM = 16.0 * math.sqrt(math.log2(math.e))
VMEM = pl.BlockSpec(memory_space=pltpu.VMEM)


def call(body, out, ins, scratch=(), flops=0, nbytes=0, trans=0, name=None):
    multiple = isinstance(out, (list, tuple))
    return pl.pallas_call(
        body,
        out_shape=out,
        in_specs=[VMEM] * len(ins),
        out_specs=[VMEM] * len(out) if multiple else VMEM,
        scratch_shapes=list(scratch),
        compiler_params=pltpu.CompilerParams(vmem_limit_bytes=48 << 20),
        cost_estimate=pl.CostEstimate(flops=flops, bytes_accessed=nbytes, transcendentals=trans),
        name=name,
    )(*ins)


def dot(left, right):
    return jnp.dot(left, right, preferred_element_type=jnp.float32)


def sine_cosine(turns):
    rest = turns - jnp.round(turns)
    square = rest * rest
    odd = SINE[-1]
    for coef in SINE[-2::-1]:
        odd = odd * square + coef
    even = COSINE[-1]
    for coef in COSINE[-2::-1]:
        even = even * square + coef
    half = odd * rest
    return 2.0 * (half * even), 1.0 - 2.0 * (half * half)


def tables_kernel(*refs):
    pos_refs, (wave_ref, by_wave, by_atom, pos, cols) = refs[:4], refs[4:]
    atoms = pos_refs[0].shape[1]
    for i, ref in enumerate(pos_refs):
        pos[:, i * atoms : (i + 1) * atoms] = ref[...]
    share = by_wave.shape[0] // 2
    role = lax.axis_index("role")
    for i in range(share // 128):
        first = pl.multiple_of(role * share + i * 128, 128)
        cols[i * 128 : (i + 1) * 128, 0:3] = wave_ref[:, pl.ds(first, 128)].astype(jnp.float32).T
    step = 64
    total = pos.shape[1]

    def block(j, carry):
        waves = cols[pl.ds(pl.multiple_of(j * step, step), step), :]
        turns = (
            waves[:, 0:1] * pos[0:1, :] + waves[:, 1:2] * pos[1:2, :] + waves[:, 2:3] * pos[2:3, :]
        )
        sine, cosine = sine_cosine(turns)
        both = jnp.stack(
            [cosine.reshape(step // 8, 8, total), sine.reshape(step // 8, 8, total)], axis=1
        ).reshape(2 * step, total)
        part = pl.ds(pl.multiple_of(j * 2 * step, 2 * step), 2 * step)
        by_wave[part, :] = both.astype(jnp.bfloat16)
        by_atom[:, part] = both.T.astype(jnp.bfloat16)
        return carry

    lax.fori_loop(0, share // step, block, 0)


def structure_kernel(scale, *refs):
    rows_refs, (wq_ref, table, out_ref, queries) = refs[:4], refs[4:]
    atoms = rows_refs[0].shape[0]
    weight = wq_ref[...]
    for i, rows in enumerate(rows_refs):
        queries[i * atoms : (i + 1) * atoms, :] = dot(rows[...], weight).astype(jnp.bfloat16)
    out_ref[...] = (dot(table[...], queries[...]) * scale).astype(jnp.bfloat16)


def stack_kernel(*refs):
    rows_refs, pos_refs, (out_ref, parts) = refs[:3], refs[3:6], refs[6:]
    atoms = rows_refs[0].shape[0]
    parts[...] = jnp.zeros_like(parts)
    for i in range(3):
        out_ref[i, 0:atoms, :] = rows_refs[i][...]
        rest = pos_refs[i][...]
        for k in range(3):
            rounded = rest.astype(jnp.bfloat16).astype(jnp.float32)
            parts[8 * k : 8 * k + 3, :] = rounded
            rest = rest - rounded
        out_ref[i, atoms:, :] = parts[...].astype(jnp.bfloat16)


def reduce_kernel(mine_ref, wave_ref, kgain_ref, out_ref):
    columns, rows, width = mine_ref.shape
    piece = rows // 2
    share = columns * piece
    first = lax.axis_index("role") * share + lax.axis_index("atoms") * piece
    start = pl.multiple_of((first // 128) * 128, 128)
    waves = wave_ref[:, pl.ds(start, 128)].astype(jnp.float32)
    squares = jnp.broadcast_to(jnp.sum(waves * waves, axis=0, keepdims=True), (piece, 128))
    lanes = lax.broadcasted_iota(jnp.int32, (piece, 128), 1)
    wanted = lax.broadcasted_iota(jnp.int32, (piece, 128), 0) + (first - start)
    square = jnp.sum(jnp.where(lanes == wanted, squares, 0.0), axis=1, keepdims=True)
    k_filter = ewald_scale * kgain_ref[...] * (jnp.exp(-square / damping) / square)
    total = jnp.sum(mine_ref[...].astype(jnp.float32), axis=0)
    filtered = total * jnp.concatenate([k_filter, k_filter], axis=0)
    out_ref[...] = jnp.broadcast_to(filtered.astype(jnp.bfloat16)[None], (columns, rows, width))


def ewald_kernel(table_ref, filtered_ref, out_ref):
    bricks, atoms, _ = out_ref.shape
    for i in range(bricks):
        part = table_ref[i * atoms : (i + 1) * atoms, :]
        out_ref[i] = dot(part, filtered_ref[...]).astype(jnp.bfloat16)


def final_kernel(rows_ref, short_ref, e0_ref, e1_ref, e2_ref, e3_ref, wout_ref, out_ref):
    total = short_ref[...]
    for ref in (e0_ref, e1_ref, e2_ref, e3_ref):
        total = total + ref[...].astype(jnp.float32)
    moved = dot(total.astype(jnp.bfloat16), wout_ref[...])
    out_ref[...] = (rows_ref[...].astype(jnp.float32) + moved).astype(jnp.bfloat16)


def prepare_kernel(
    r0, r1, r2, low_ref, high_ref, p0, p1, p2, slots_ref, images_ref, win_ref, hidden, cols, pos, turned
):
    slots, atoms = slots_ref.shape
    weight = win_ref[...]
    own = (r0, r1, r2)
    for p in range(3):
        for q in range(3):
            brick = p * 3 + q
            if q == 1:
                rows, place = own[p][...], (p0, p1, p2)[p][...]
            else:
                ref = low_ref if q == 0 else high_ref
                rows = ref[p, 0:atoms, :]
                parts = ref[p, atoms:, :].astype(jnp.float32)
                place = (parts[0:3, :] + parts[8:11, :]) + parts[16:19, :]
            hidden[brick * atoms : (brick + 1) * atoms, :] = dot(rows, weight).astype(jnp.bfloat16)
            pos[0:3, brick * atoms : (brick + 1) * atoms] = place
    lane = 128
    for half in range(atoms // lane):
        cut = slice(half * lane, (half + 1) * lane)
        index = slots_ref[:, cut]
        image = images_ref[:, cut]
        place = index & (lane - 1)
        group = index >> 7
        near = [jnp.zeros((slots, lane), jnp.float32) for _ in range(3)]
        for r in range(9 * atoms // lane):
            here = group == r
            for c in range(3):
                table = jnp.broadcast_to(pos[c : c + 1, r * lane : (r + 1) * lane], (slots, lane))
                taken = jnp.take_along_axis(table, place, axis=1, mode="promise_in_bounds")
                near[c] = jnp.where(here, taken, near[c])
        first = (image >= 9).astype(jnp.int32) + (image >= 18).astype(jnp.int32)
        inside = image - 9 * first
        second = (inside >= 3).astype(jnp.int32) + (inside >= 6).astype(jnp.int32)
        third = inside - 3 * second
        square = jnp.zeros((slots, lane), jnp.float32)
        for c, offset in enumerate((first, second, third)):
            delta = near[c] + (offset - 1).astype(jnp.float32) * box_side - p1[c : c + 1, cut]
            square = square + delta * delta
        rest = jnp.sqrt(square + soft_sq) * ZOOM
        for k in range(3):
            rounded = rest.astype(jnp.bfloat16).astype(jnp.float32)
            turned[k * slots : (k + 1) * slots, cut] = rounded
            rest = rest - rounded
        turned[3 * slots : 4 * slots, cut] = ((lane + place) << group).astype(jnp.float32)
    cols[...] = turned[...].T.astype(jnp.bfloat16)


def short_kernel(first, count, scale, cols_ref, hidden, wrbf_ref, brbf_ref, wf_ref, sum_ref, out_ref, pairs, hot_a, hot_b):
    lane = 128
    atoms = cols_ref.shape[0]
    slots = cols_ref.shape[1] // 4
    basis_count, width = wrbf_ref.shape
    pairs[...] = jnp.zeros_like(pairs)
    pairs[0:basis_count, 0:width] = wrbf_ref[...]
    pairs[basis_count:, width:] = wrbf_ref[...]
    out_ref[...] = sum_ref[...]
    row = lax.broadcasted_iota(jnp.int32, (lane, 6 * lane), 0)
    column = lax.broadcasted_iota(jnp.int32, (lane, 6 * lane), 1)
    code_slot = jnp.where(row >= 3 * slots, row - 3 * slots - (column >> 7), -lane)
    dist_slot = jnp.where(row < 3 * slots, (row & (slots - 1)) - ((column - 4 * lane) >> 6), -lane)
    source = jnp.where(column < 4 * lane, code_slot, dist_slot)
    centers = (
        (lax.broadcasted_iota(jnp.int32, (1, lane), 1) & (basis_count - 1)).astype(jnp.float32)
        * (4.0 / (basis_count - 1))
        * ZOOM
    )
    lanes = lax.broadcasted_iota(jnp.int32, (16, lane), 1) + lane
    bias = brbf_ref[...] * math.log2(math.e)
    bias = jnp.concatenate([bias, bias], axis=1)
    groups = 9 * atoms // lane

    def spread(j):
        select = (source == 4 * j).astype(jnp.float32).astype(jnp.bfloat16)
        return dot(cols_ref[...], select)

    def make_hot(hot, wide):
        for i in range(4):
            code = wide[:, i * lane : (i + 1) * lane].astype(jnp.bfloat16)
            for g in range(groups):
                number = jnp.broadcast_to(
                    (lanes << g).astype(jnp.float32).astype(jnp.bfloat16)[None], (atoms // 16, 16, lane)
                ).reshape(atoms, lane)
                hot[i * atoms : (i + 1) * atoms, g * lane : (g + 1) * lane] = jnp.where(
                    code == number, jnp.bfloat16(1), jnp.bfloat16(0)
                )

    def filters_of(wide):
        inner = []
        for p in range(2):
            offset = wide[:, (4 + p) * lane : (5 + p) * lane] - centers
            basis = jnp.exp2(-(offset * offset)).astype(jnp.bfloat16)
            value = dot(basis, pairs[...]) * math.log2(math.e) + bias
            both = (jnp.log(1.0 + jnp.exp2(value)) - math.log(2.0)).astype(jnp.bfloat16)
            inner += [both[:, :width], both[:, width:]]
        return dot(jnp.concatenate(inner, axis=0), wf_ref[...])

    def add(filters, gathered):
        product = filters * gathered
        total = product[0:atoms]
        for i in range(1, 4):
            total = total + product[i * atoms : (i + 1) * atoms]
        out_ref[...] += total

    wide_first = spread(first)
    make_hot(hot_a, wide_first)

    def body(jj, carry):
        j = first + 2 * jj
        wide_b = spread(j + 1)
        make_hot(hot_b, wide_b)
        gathered_a = dot(hot_a[...], hidden[...])
        add(filters_of(spread(j)), gathered_a)
        wide_a = spread(j + 2)
        gathered_b = dot(hot_b[...], hidden[...])
        add(filters_of(wide_b), gathered_b)
        make_hot(hot_a, wide_a)
        return carry

    lax.fori_loop(0, count // 2, body, 0)
    out_ref[...] = out_ref[...] * scale


def local(
    features,
    positions,
    neighbours,
    images,
    wave,
    kgain,
    w_in,
    w_query,
    w_rbf,
    b_rbf,
    w_filter,
    w_out,
):
    f32, bf16 = jnp.float32, jnp.bfloat16
    rows = features[0, 0]
    place = positions[0, 0]
    atoms, width = rows.shape
    slots = neighbours.shape[2]
    roles = lax.axis_size("role")
    columns = lax.axis_size("atoms")
    atom_total = atoms * roles * columns
    waves = wave.shape[1]
    share = waves // roles
    piece = share // columns

    def from_role(block, shift):
        return lax.ppermute(block, "role", [((i + shift) % roles, i) for i in range(roles)])

    def from_column(block, shift):
        return lax.ppermute(
            block, "atoms", [((i + shift) % columns, i) for i in range(columns)]
        )

    shifts = (1, roles - 1, 2)
    place_of = {0: place, **{d: from_role(place, d) for d in shifts}}
    rows_of = {0: rows, **{d: from_role(rows, d) for d in shifts}}
    order = (0,) + shifts

    by_wave, by_atom = call(
        tables_kernel,
        [jax.ShapeDtypeStruct((2 * share, roles * atoms), bf16)]
        + [jax.ShapeDtypeStruct((roles * atoms, 2 * share), bf16)],
        [place_of[d] for d in order] + [wave],
        scratch=[pltpu.VMEM((3, roles * atoms), f32), pltpu.VMEM((share, 128), f32)],
        flops=40 * share * roles * atoms,
        nbytes=4 << 20,
        name="tables",
    )
    partial = call(
        functools.partial(structure_kernel, atom_total ** (-0.5)),
        jax.ShapeDtypeStruct((2 * share, width), bf16),
        [rows_of[d] for d in order] + [w_query, by_wave],
        scratch=[pltpu.VMEM((roles * atoms, width), bf16)],
        flops=2 * 2 * share * roles * atoms * width,
        nbytes=3 << 20,
        name="structure",
    )
    mine = lax.all_to_all(partial.reshape(columns, 2 * piece, width), "atoms", 0, 0)
    copies = call(
        reduce_kernel,
        jax.ShapeDtypeStruct((columns, 2 * piece, width), bf16),
        [mine, wave, kgain[None, :]],
        flops=2 * share * width,
        nbytes=1 << 20,
        name="reduce",
    )
    everyone = lax.all_to_all(copies, "atoms", 0, 0).reshape(2 * share, width)

    triple = (roles - 1, 0, 1)
    bundle = call(
        stack_kernel,
        jax.ShapeDtypeStruct((3, atoms + 32, width), bf16),
        [rows_of[d] for d in triple] + [place_of[d] for d in triple],
        scratch=[pltpu.VMEM((32, width), f32)],
        nbytes=1 << 20,
        name="stack",
    )
    low, high = from_column(bundle, columns - 1), from_column(bundle, 1)
    hidden, cols = call(
        prepare_kernel,
        [jax.ShapeDtypeStruct((9 * atoms, width), bf16), jax.ShapeDtypeStruct((atoms, 4 * slots), bf16)],
        [rows_of[d] for d in triple]
        + [low, high]
        + [place_of[d] for d in triple]
        + [neighbours[0, 0], images[0, 0], w_in],
        scratch=[pltpu.VMEM((8, 9 * atoms), f32), pltpu.VMEM((4 * slots, atoms), f32)],
        flops=2 * 9 * atoms * width * width,
        nbytes=4 << 20,
        name="prepare",
    )
    short = jnp.zeros((atoms, width), f32)
    quads = slots // 4
    for half in range(2):
        short = call(
            functools.partial(
                short_kernel, half * quads // 2, quads // 2, slots ** (-0.5) if half else 1.0
            ),
            jax.ShapeDtypeStruct((atoms, width), f32),
            [cols, hidden, w_rbf, b_rbf[None, :], w_filter, short],
            scratch=[
                pltpu.VMEM((128, 2 * width), bf16),
                pltpu.VMEM((4 * atoms, 9 * atoms), bf16),
                pltpu.VMEM((4 * atoms, 9 * atoms), bf16),
            ],
            flops=slots * atoms * 9 * atoms * width,
            nbytes=4 << 20,
            name="short%d" % half,
        )
    parts = call(
        ewald_kernel,
        jax.ShapeDtypeStruct((roles, atoms, width), bf16),
        [by_atom, everyone],
        flops=2 * 2 * share * roles * atoms * width,
        nbytes=4 << 20,
        name="ewald",
    )
    back = [parts[0]] + [from_role(parts[1 + i], roles - d) for i, d in enumerate(shifts)]
    result = call(
        final_kernel,
        jax.ShapeDtypeStruct((atoms, width), bf16),
        [rows, short] + back + [w_out],
        flops=2 * atoms * width * width,
        nbytes=1 << 20,
        name="final",
    )
    return result[None, None]


def solution(mesh):
    in_specs = (
        P("role", "atoms", None, None),
        P("role", "atoms", None, None),
        P("role", "atoms", None, None),
        P("role", "atoms", None, None),
        P(),
        P(),
        P(),
        P(),
        P(),
        P(),
        P(),
        P(),
    )
    out_specs = P("role", "atoms", None, None)
    return jax.shard_map(local, mesh=mesh, in_specs=in_specs, out_specs=out_specs, check_vma=False)
```

time: 124 us -> 106 us (0.85); the launches traced: 124 us -> 105 us
  blocking collectives: 0 us -> 28 us
  Pallas kernels: 41.1 us -> 25.8 us
  starting transfers between devices: 36 us -> 22.7 us
  local copies, waits for them, and re-layouts: 12.7 us -> 4.37 us
  waiting for transfers between devices: 28.6 us -> 23.4 us
  other arithmetic: 4.98 us -> 0 us
    all_to_all x0 -> x1, blocking collectives: none -> 28 us  [local(): lax.all_to_all(partial.reshape(columns, 2 * piece, width), 'atoms', 0, 0)]
    pallas_call x5 -> x9, Pallas kernels: 41.1 us -> 25.8 us  [call(): pl.pallas_call(body, out_shape=out, in_specs=[VMEM] * len(ins), out_specs...]
    all_to_all x1 -> x0, waiting for transfers between devices: 9.21 us -> none  [local(): mine = lax.all_to_all(chunks, 'atoms', 0, 0)]
    ppermute x9, waiting for transfers between devices: 0.02 us -> 6.75 us  [from_role(): lax.ppermute(block, 'role', [((i + shift) % roles, i) for i in range(role...]
    ppermute x4 -> x2, starting transfers between devices: 10.8 us -> 5.27 us  [from_column(): lax.ppermute(block, 'atoms', [((i + shift) % columns, i) for i in range(c...]
    all_to_all x1 -> x0, starting transfers between devices: 5.29 us -> none  [local(): mine = lax.all_to_all(chunks, 'atoms', 0, 0)]
    ppermute x4 -> x2, waiting for transfers between devices: 19.4 us -> 16.7 us  [from_column(): lax.ppermute(block, 'atoms', [((i + shift) % columns, i) for i in range(c...]
    ppermute x9, starting transfers between devices: 13.4 us -> 10.8 us  [from_role(): lax.ppermute(block, 'role', [((i + shift) % roles, i) for i in range(role...]
  transfers between devices with their start and end apart: 15 -> 12, of which waited for: 3 -> 4; matrix products, arithmetic and copies ran while one was open for 13% -> 1% of each run, Pallas kernels for 32% -> 21%
where the time goes in v1:
time: 106 us; the launch traced here: 105 us
  blocking collectives  28 us (26%)
  Pallas kernels  25.8 us (24%)
  waiting for transfers between devices  23.4 us (22%)
  starting transfers between devices  22.7 us (21%)
  local copies, waits for them, and re-layouts  4.37 us (4%)
    all_to_all x1, blocking collectives, local(): lax.all_to_all(partial.reshape(columns, 2 * piece, width), 'atoms', 0, 0)  28 us
    pallas_call x9, Pallas kernels, call(): pl.pallas_call(body, out_shape=out, in_specs=[VMEM] * len(ins), out_specs...  25.8 us
    ppermute x2, waiting for transfers between devices, from_column(): lax.ppermute(block, 'atoms', [((i + shift) % columns, i) for i in range(c...  16.7 us
    ppermute x9, starting transfers between devices, from_role(): lax.ppermute(block, 'role', [((i + shift) % roles, i) for i in range(role...  10.8 us
    ppermute x9, waiting for transfers between devices, from_role(): lax.ppermute(block, 'role', [((i + shift) % roles, i) for i in range(role...  6.75 us
    all_to_all x1, starting transfers between devices, local(): everyone = lax.all_to_all(copies, 'atoms', 0, 0).reshape(2 * share, width)  6.66 us
    ppermute x2, starting transfers between devices, from_column(): lax.ppermute(block, 'atoms', [((i + shift) % columns, i) for i in range(c...  5.27 us
    unnamed x31, local copies, waits for them, and re-layouts  4.31 us
  transfers between devices with their start and end apart: 12, of which 4 were waited for; matrix products, arithmetic and copies ran while one was open for 1% of the time, Pallas kernels for 21%

profile of v1, /device:TPU:24, one launch (start us, length us, event | category | flops | bytes accessed | tf_op | source)
XLA Modules:
  0.0 104.5 jit_solution(5724737407047800413)
XLA Ops:
  0.0 1.9 %collective-permute-start = (bf16[256,256]{1,0:T(8,128)(2,1)}, bf16[256,256]{1,0:T(8,128)(2,1)S(1)}, u32[]{:S(2)}, u32[]{:S(2)}) collective-permute-start(bf16[256,256]{1,0:T(8,128)(2,1)} %bitcast.19), channel_id=1, source_target_pairs={{192,0},{0,64},{64,128},{128,192},{193,1},{1,65},{65,129},{129,193... | collective-permute-start | bytes 393224 | tf_op jit(solution)/shard_map/ppermute | solution.py:300
  1.9 0.1 collective-permute-start.1
  2.0 1.4 %collective-permute-start.7 = (bf16[256,256]{1,0:T(8,128)(2,1)}, bf16[256,256]{1,0:T(8,128)(2,1)S(1)}, u32[]{:S(2)}, u32[]{:S(2)}) collective-permute-start(bf16[256,256]{1,0:T(8,128)(2,1)} %bitcast.21), channel_id=1, source_target_pairs={{128,0},{192,64},{0,128},{64,192},{129,1},{193,65},{1,129},{65,193... | collective-permute-start | bytes 393224 | tf_op jit(solution)/shard_map/ppermute | solution.py:300
  3.4 0.7 copy.15
  4.1 2.0 %collective-permute-start.2 = (f32[3,256]{1,0:T(4,128)S(1)}, f32[3,256]{1,0:T(4,128)S(1)}, u32[]{:S(2)}, u32[]{:S(2)}) collective-permute-start(f32[3,256]{1,0:T(4,128)S(1)} %bitcast.28), channel_id=1, source_target_pairs={{192,0},{0,64},{64,128},{128,192},{193,1},{1,65},{65,129},{129,193... | collective-permute-start | bytes 9224 | tf_op jit(solution)/shard_map/ppermute | solution.py:300
  6.1 0.6 collective-permute-start.3
  6.7 2.5 %collective-permute-done.2.refs_3_.p0.refs_2_ = f32[3,256]{1,0:T(4,128)S(1)} collective-permute-done((f32[3,256]{1,0:T(4,128)S(1)}, f32[3,256]{1,0:T(4,128)S(1)}, u32[]{:S(2)}, u32[]{:S(2)}) %collective-permute-start.2) | collective-permute-done | bytes 3104 | tf_op jit(solution)/shard_map/ppermute | solution.py:300
  9.2 0.9 collective-permute-start.6
  10.1 0.8 collective-permute-done.3.refs_5_.p2.refs_1_
  10.9 3.4 %collective-permute-done.6.refs_3_ = f32[3,256]{1,0:T(4,128)S(1)} collective-permute-done((f32[3,256]{1,0:T(4,128)S(1)}, f32[3,256]{1,0:T(4,128)S(1)}, u32[]{:S(2)}, u32[]{:S(2)}) %collective-permute-start.6) | collective-permute-done | bytes 3104 | tf_op jit(solution)/shard_map/ppermute | solution.py:300
  14.3 0.0 copy-start.5
  14.3 0.8 copy-done.5
  15.1 3.6 %tables.1 = (bf16[1024,1024]{1,0:T(8,128)(2,1)S(1)}, bf16[1024,1024]{1,0:T(8,128)(2,1)S(1)}) custom-call(f32[3,256]{1,0:T(4,128)S(1)} %bitcast.31, f32[3,256]{1,0:T(4,128)S(1)} %collective-permute-done.3.refs_5_.p2.refs_1_, f32[3,256]{1,0:T(4,128)S(1)} %collective-permute-done.2.refs_3_.p0.refs_2_, f32[3,256]{1,0:T(4,128)S(1)} %collective-permute-done.6.refs_3_, ...), custom_call_target="tpu_custom_call" | custom-call | flops 20971520 | bytes 4194304 | tf_op jit(solution)/shard_map/tables/pallas_call | solution.py:35
  18.7 0.0 collective-permute-done.refs_0_.r0.refs_2_
  18.7 0.0 collective-permute-done.1.refs_2_.r2.refs_1_
  18.7 0.0 collective-permute-done.7.refs_3_
  18.7 0.0 copy-start
  18.7 0.9 copy-done
  19.6 0.0 copy-start.2
  19.6 0.9 copy-done.2
  20.5 0.0 copy-start.6
  20.5 0.0 copy-start.9
  20.5 1.0 structure.1
  21.5 0.0 copy-start.1
  21.5 0.0 copy-start.3
  21.5 0.0 copy-start.7
  21.5 0.0 copy-start.8
  21.6 28.0 %all_to_all.10.mine_ref = bf16[64,16,256]{2,1,0:T(8,128)(2,1)S(1)} all-to-all(bf16[64,16,256]{2,1,0:T(8,128)(2,1)S(1)} %bitcast.26), channel_id=1, replica_groups=mesh['role'=4,'atoms'=64] {'atoms'}, dimensions={0} | all-to-all | bytes 1048576 | tf_op jit(solution)/shard_map/all_to_all | solution.py:331
  49.6 0.0 copy-done.6
  49.6 0.0 copy-done.9
  49.6 0.9 reduce.1
  50.6 0.0 copy-start.12
  50.6 0.0 copy-start.13
  50.6 0.0 copy-start.14
  50.6 6.7 %all-to-all-start.1 = ((bf16[64,16,256]{2,1,0:T(8,128)(2,1)}), bf16[64,16,256]{2,1,0:T(8,128)(2,1)S(1)}, u32[]{:S(2)}, u32[]{:S(2)}) async-start(bf16[64,16,256]{2,1,0:T(8,128)(2,1)} %reduce.1), calls=%async_computation.1 | async-start | bytes 1048576 | tf_op jit(solution)/shard_map/all_to_all | solution.py:340
  57.2 0.0 copy-done.1
  57.2 0.1 stack.1
  57.3 0.1 collective-permute-start.4
  57.4 5.1 %collective-permute-start.5 = (bf16[3,288,256]{2,1,0:T(8,128)(2,1)S(1)}, bf16[3,288,256]{2,1,0:T(8,128)(2,1)S(1)}, u32[]{:S(2)}, u32[]{:S(2)}) collective-permute-start(bf16[3,288,256]{2,1,0:T(8,128)(2,1)S(1)} %stack.1), channel_id=1, source_target_pairs={{1,0},{2,1},{3,2},{4,3},{5,4},{6,5},{7,6},{8,7},{9,8},{10,9},{11,1... | collective-permute-start | bytes 1327112 | tf_op jit(solution)/shard_map/ppermute | solution.py:303
  62.6 16.6 %collective-permute-done.4.low_ref = bf16[3,288,256]{2,1,0:T(8,128)(2,1)S(1)} collective-permute-done((bf16[3,288,256]{2,1,0:T(8,128)(2,1)S(1)}, bf16[3,288,256]{2,1,0:T(8,128)(2,1)S(1)}, u32[]{:S(2)}, u32[]{:S(2)}) %collective-permute-start.4) | collective-permute-done | bytes 442400 | tf_op jit(solution)/shard_map/ppermute | solution.py:303
  79.2 0.0 collective-permute-done.5.high_ref
  79.2 0.0 copy-done.3
  79.2 0.0 copy-done.7
  79.2 0.0 copy-done.8
  79.2 1.4 %prepare.1 = (bf16[2304,256]{1,0:T(8,128)(2,1)S(1)}, bf16[256,128]{1,0:T(8,128)(2,1)S(1)}) custom-call(bf16[256,256]{1,0:T(8,128)(2,1)S(1)} %collective-permute-done.refs_0_.r0.refs_2_, bf16[256,256]{1,0:T(8,128)(2,1)S(1)} %bitcast.24, bf16[256,256]{1,0:T(8,128)(2,1)S(1)} %collective-permute-done.1.refs_2_.r2.refs_1_, ...), custom_call_target="tpu_custom_call" | custom-call | flops 301989888 | bytes 4194304 | tf_op jit(solution)/shard_map/prepare/pallas_call | solution.py:35
  80.7 0.0 copy-done.12
  80.7 0.0 copy-done.13
  80.7 0.0 copy-done.14
  80.7 8.6 %short0.1.sum_ref = f32[256,256]{1,0:T(8,128)S(1)} custom-call(bf16[256,128]{1,0:T(8,128)(2,1)S(1)} %get-tuple-element.9.cols_ref, bf16[2304,256]{1,0:T(8,128)(2,1)S(1)} %get-tuple-element.10.hidden, bf16[64,256]{1,0:T(8,128)(2,1)S(1)} %copy-done.13, f32[1,256]{1,0:T(1,128)S(1)} %bitcast.37, bf16[256,256]{1,0:T(8,128)(2,1)S(1)} %copy-done.12, ...), custom_call_target="tpu_custom_call" | custom-call | flops 4831838208 | bytes 4194304 | tf_op jit(solution)/shard_map/short0/pallas_call | solution.py:35
  89.3 0.0 copy-start.10
  89.3 1.0 copy-done.10
  90.4 0.0 all-to-all-done.1
  90.4 0.0 copy-start.11
  90.4 0.7 ewald.1
  91.1 1.9 %collective-permute-start.10 = (bf16[256,256]{1,0:T(8,128)(2,1)S(1)}, bf16[256,256]{1,0:T(8,128)(2,1)S(1)}, u32[]{:S(2)}, u32[]{:S(2)}) collective-permute-start(bf16[256,256]{1,0:T(8,128)(2,1)S(1)} %get-tuple-element.13), channel_id=1, source_target_pairs={{128,0},{192,64},{0,128},{64,192},{129,1},{193,65},{1,129},{65,193... | collective-permute-start | bytes 393224 | tf_op jit(solution)/shard_map/ppermute | solution.py:300
  93.0 1.5 %collective-permute-start.8 = (bf16[256,256]{1,0:T(8,128)(2,1)S(1)}, bf16[256,256]{1,0:T(8,128)(2,1)S(1)}, u32[]{:S(2)}, u32[]{:S(2)}) collective-permute-start(bf16[256,256]{1,0:T(8,128)(2,1)S(1)} %get-tuple-element.15), channel_id=1, source_target_pairs={{192,0},{0,64},{64,128},{128,192},{193,1},{1,65},{65,129},{129,193... | collective-permute-start | bytes 393224 | tf_op jit(solution)/shard_map/ppermute | solution.py:300
  94.5 0.5 collective-permute-start.9
  95.0 0.0 copy-done.11
  95.0 8.6 %short1.1.short_ref = f32[256,256]{1,0:T(8,128)S(1)} custom-call(bf16[256,128]{1,0:T(8,128)(2,1)S(1)} %get-tuple-element.9.cols_ref, bf16[2304,256]{1,0:T(8,128)(2,1)S(1)} %copy-done.11, bf16[64,256]{1,0:T(8,128)(2,1)S(1)} %copy-done.13, f32[1,256]{1,0:T(1,128)S(1)} %bitcast.38, bf16[256,256]{1,0:T(8,128)(2,1)S(1)} %copy-done.12, f32[256,256]{1,0:T(8,128)S(1)} %short0.1.sum_ref), custom_call_target="tpu_custom_call" | custom-call | flops 4831838208 | bytes 4194304 | tf_op jit(solution)/shard_map/short1/pallas_call | solution.py:35
  103.6 0.0 collective-permute-done.10.e3_ref
  103.6 0.0 collective-permute-done.8.e1_ref
  103.6 0.0 collective-permute-done.9.e2_ref
  103.7 0.0 copy-done.4
  103.7 0.9 final.1
  (3 shorter events, 0.1 us)
Async XLA Ops:
  0.0 18.7 %collective-permute-start = (bf16[256,256]{1,0:T(8,128)(2,1)}, bf16[256,256]{1,0:T(8,128)(2,1)S(1)}, u32[]{:S(2)}, u32[]{:S(2)}) collective-permute-start(bf16[256,256]{1,0:T(8,128)(2,1)} %bitcast.19), channel_id=1, source_target_pairs={{192,0},{0,64},{64,128},{128,192},{193,1},{1,65},{65,129},{129,193... | collective-permute-start | bytes 393224 | tf_op jit(solution)/shard_map/ppermute | solution.py:300
  1.9 16.8 %collective-permute-start.1 = (bf16[256,256]{1,0:T(8,128)(2,1)}, bf16[256,256]{1,0:T(8,128)(2,1)S(1)}, u32[]{:S(2)}, u32[]{:S(2)}) collective-permute-start(bf16[256,256]{1,0:T(8,128)(2,1)} %bitcast.20), channel_id=1, source_target_pairs={{64,0},{128,64},{192,128},{0,192},{65,1},{129,65},{193,129},{1,193... | collective-permute-start | bytes 393224 | tf_op jit(solution)/shard_map/ppermute | solution.py:300
  2.0 16.7 %collective-permute-start.7 = (bf16[256,256]{1,0:T(8,128)(2,1)}, bf16[256,256]{1,0:T(8,128)(2,1)S(1)}, u32[]{:S(2)}, u32[]{:S(2)}) collective-permute-start(bf16[256,256]{1,0:T(8,128)(2,1)} %bitcast.21), channel_id=1, source_target_pairs={{128,0},{192,64},{0,128},{64,192},{129,1},{193,65},{1,129},{65,193... | collective-permute-start | bytes 393224 | tf_op jit(solution)/shard_map/ppermute | solution.py:300
  4.1 5.1 %collective-permute-start.2 = (f32[3,256]{1,0:T(4,128)S(1)}, f32[3,256]{1,0:T(4,128)S(1)}, u32[]{:S(2)}, u32[]{:S(2)}) collective-permute-start(f32[3,256]{1,0:T(4,128)S(1)} %bitcast.28), channel_id=1, source_target_pairs={{192,0},{0,64},{64,128},{128,192},{193,1},{1,65},{65,129},{129,193... | collective-permute-start | bytes 9224 | tf_op jit(solution)/shard_map/ppermute | solution.py:300
  6.1 4.8 %collective-permute-start.3 = (f32[3,256]{1,0:T(4,128)S(1)}, f32[3,256]{1,0:T(4,128)S(1)}, u32[]{:S(2)}, u32[]{:S(2)}) collective-permute-start(f32[3,256]{1,0:T(4,128)S(1)} %bitcast.29), channel_id=1, source_target_pairs={{64,0},{128,64},{192,128},{0,192},{65,1},{129,65},{193,129},{1,193... | collective-permute-start | bytes 9224 | tf_op jit(solution)/shard_map/ppermute | solution.py:300
  9.2 5.1 %collective-permute-start.6 = (f32[3,256]{1,0:T(4,128)S(1)}, f32[3,256]{1,0:T(4,128)S(1)}, u32[]{:S(2)}, u32[]{:S(2)}) collective-permute-start(f32[3,256]{1,0:T(4,128)S(1)} %bitcast.30), channel_id=1, source_target_pairs={{128,0},{192,64},{0,128},{64,192},{129,1},{193,65},{1,129},{65,193... | collective-permute-start | bytes 9224 | tf_op jit(solution)/shard_map/ppermute | solution.py:300
  14.3 0.8 copy-start.5
  18.7 0.9 copy-start
  19.6 0.9 copy-start.2
  20.5 29.1 %copy-start.6 = (s32[3,2048]{1,0:T(4,128)S(1)}, s32[3,2048]{1,0:T(4,128)}, u32[]{:S(2)}) copy-start(s32[3,2048]{1,0:T(4,128)} %wave_ref.1) | copy-start | bytes 73732
  20.5 29.1 %copy-start.9 = (f32[256]{0:T(256)S(1)}, f32[256]{0:T(256)}, u32[]{:S(2)}) copy-start(f32[256]{0:T(256)} %param.17) | copy-start | bytes 3076
  21.5 35.7 %copy-start.1 = (bf16[1,1,256,256]{3,2,1,0:T(8,128)(2,1)S(1)}, bf16[1,1,256,256]{3,2,1,0:T(8,128)(2,1)}, u32[]{:S(2)}) copy-start(bf16[1,1,256,256]{3,2,1,0:T(8,128)(2,1)} %param.12) | copy-start | bytes 393220
  21.5 57.7 %copy-start.3 = (bf16[256,256]{1,0:T(8,128)(2,1)S(1)}, bf16[256,256]{1,0:T(8,128)(2,1)}, u32[]{:S(2)}) copy-start(bf16[256,256]{1,0:T(8,128)(2,1)} %win_ref.1) | copy-start | bytes 393220
  21.5 57.7 %copy-start.7 = (s32[1,1,32,256]{3,2,1,0:T(8,128)S(1)}, s32[1,1,32,256]{3,2,1,0:T(8,128)}, u32[]{:S(2)}) copy-start(s32[1,1,32,256]{3,2,1,0:T(8,128)} %param.14) | copy-start | bytes 98308
  21.5 57.7 %copy-start.8 = (s32[1,1,32,256]{3,2,1,0:T(8,128)S(1)}, s32[1,1,32,256]{3,2,1,0:T(8,128)}, u32[]{:S(2)}) copy-start(s32[1,1,32,256]{3,2,1,0:T(8,128)} %param.15) | copy-start | bytes 98308
  50.6 30.1 %copy-start.12 = (bf16[256,256]{1,0:T(8,128)(2,1)S(1)}, bf16[256,256]{1,0:T(8,128)(2,1)}, u32[]{:S(2)}) copy-start(bf16[256,256]{1,0:T(8,128)(2,1)} %wf_ref.3) | copy-start | bytes 393220
  50.6 30.2 %copy-start.13 = (bf16[64,256]{1,0:T(8,128)(2,1)S(1)}, bf16[64,256]{1,0:T(8,128)(2,1)}, u32[]{:S(2)}) copy-start(bf16[64,256]{1,0:T(8,128)(2,1)} %wrbf_ref.3) | copy-start | bytes 98308
  50.6 30.2 %copy-start.14 = (f32[256]{0:T(256)S(1)}, f32[256]{0:T(256)}, u32[]{:S(2)}) copy-start(f32[256]{0:T(256)} %param.21) | copy-start | bytes 3076
  50.6 39.8 %all-to-all-start.1 = ((bf16[64,16,256]{2,1,0:T(8,128)(2,1)}), bf16[64,16,256]{2,1,0:T(8,128)(2,1)S(1)}, u32[]{:S(2)}, u32[]{:S(2)}) async-start(bf16[64,16,256]{2,1,0:T(8,128)(2,1)} %reduce.1), calls=%async_computation.1 | async-start | bytes 1048576 | tf_op jit(solution)/shard_map/all_to_all | solution.py:340
  57.3 21.9 %collective-permute-start.4 = (bf16[3,288,256]{2,1,0:T(8,128)(2,1)S(1)}, bf16[3,288,256]{2,1,0:T(8,128)(2,1)S(1)}, u32[]{:S(2)}, u32[]{:S(2)}) collective-permute-start(bf16[3,288,256]{2,1,0:T(8,128)(2,1)S(1)} %stack.1), channel_id=1, source_target_pairs={{63,0},{0,1},{1,2},{2,3},{3,4},{4,5},{5,6},{6,7},{7,8},{8,9},{9,10... | collective-permute-start | bytes 1327112 | tf_op jit(solution)/shard_map/ppermute | solution.py:303
  57.4 21.8 %collective-permute-start.5 = (bf16[3,288,256]{2,1,0:T(8,128)(2,1)S(1)}, bf16[3,288,256]{2,1,0:T(8,128)(2,1)S(1)}, u32[]{:S(2)}, u32[]{:S(2)}) collective-permute-start(bf16[3,288,256]{2,1,0:T(8,128)(2,1)S(1)} %stack.1), channel_id=1, source_target_pairs={{1,0},{2,1},{3,2},{4,3},{5,4},{6,5},{7,6},{8,7},{9,8},{10,9},{11,1... | collective-permute-start | bytes 1327112 | tf_op jit(solution)/shard_map/ppermute | solution.py:303
  89.3 1.0 copy-start.10
  90.4 4.6 %copy-start.11 = (bf16[2304,256]{1,0:T(8,128)(2,1)S(1)}, bf16[2304,256]{1,0:T(8,128)(2,1)}, u32[]{:S(2)}) copy-start(bf16[2304,256]{1,0:T(8,128)(2,1)} %copy-done.10) | copy-start | bytes 3538948
  91.1 12.5 %collective-permute-start.10 = (bf16[256,256]{1,0:T(8,128)(2,1)S(1)}, bf16[256,256]{1,0:T(8,128)(2,1)S(1)}, u32[]{:S(2)}, u32[]{:S(2)}) collective-permute-start(bf16[256,256]{1,0:T(8,128)(2,1)S(1)} %get-tuple-element.13), channel_id=1, source_target_pairs={{128,0},{192,64},{0,128},{64,192},{129,1},{193,65},{1,129},{65,193... | collective-permute-start | bytes 393224 | tf_op jit(solution)/shard_map/ppermute | solution.py:300
  93.0 10.7 %collective-permute-start.8 = (bf16[256,256]{1,0:T(8,128)(2,1)S(1)}, bf16[256,256]{1,0:T(8,128)(2,1)S(1)}, u32[]{:S(2)}, u32[]{:S(2)}) collective-permute-start(bf16[256,256]{1,0:T(8,128)(2,1)S(1)} %get-tuple-element.15), channel_id=1, source_target_pairs={{192,0},{0,64},{64,128},{128,192},{193,1},{1,65},{65,129},{129,193... | collective-permute-start | bytes 393224 | tf_op jit(solution)/shard_map/ppermute | solution.py:300
  94.5 9.2 %copy-start.4 = (bf16[256,256]{1,0:T(8,128)(2,1)S(1)}, bf16[256,256]{1,0:T(8,128)(2,1)}, u32[]{:S(2)}) copy-start(bf16[256,256]{1,0:T(8,128)(2,1)} %wout_ref.1) | copy-start | bytes 393220
  94.5 9.2 %collective-permute-start.9 = (bf16[256,256]{1,0:T(8,128)(2,1)S(1)}, bf16[256,256]{1,0:T(8,128)(2,1)S(1)}, u32[]{:S(2)}, u32[]{:S(2)}) collective-permute-start(bf16[256,256]{1,0:T(8,128)(2,1)S(1)} %get-tuple-element.14), channel_id=1, source_target_pairs={{64,0},{128,64},{192,128},{0,192},{65,1},{129,65},{193,129},{1,193... | collective-permute-start | bytes 393224 | tf_op jit(solution)/shard_map/ppermute | solution.py:300

commit v2 on v1

--- a/solution.py
+++ b/solution.py
@@ -7,6 +7,7 @@
 from jax.experimental import pallas as pl
 from jax.experimental.pallas import tpu as pltpu
 from jax.sharding import PartitionSpec as P
+
 
 box_side = 1.0
 soft_sq = 0.01
@@ -30,7 +31,7 @@
 VMEM = pl.BlockSpec(memory_space=pltpu.VMEM)
 
 
-def call(body, out, ins, scratch=(), flops=0, nbytes=0, trans=0, name=None):
+def call(body, out, ins, scratch=(), flops=0, nbytes=0, trans=0, grant=16):
     multiple = isinstance(out, (list, tuple))
     return pl.pallas_call(
         body,
@@ -38,9 +39,8 @@
         in_specs=[VMEM] * len(ins),
         out_specs=[VMEM] * len(out) if multiple else VMEM,
         scratch_shapes=list(scratch),
-        compiler_params=pltpu.CompilerParams(vmem_limit_bytes=48 << 20),
+        compiler_params=pltpu.CompilerParams(vmem_limit_bytes=grant << 20),
         cost_estimate=pl.CostEstimate(flops=flops, bytes_accessed=nbytes, transcendentals=trans),
-        name=name,
     )(*ins)
 
 
@@ -61,16 +61,22 @@
     return 2.0 * (half * even), 1.0 - 2.0 * (half * half)
 
 
+def begin_kernel(wave_ref, rows_ref, wq_ref, cols, rows_out, wq_out):
+    share = cols.shape[0]
+    role = lax.axis_index("role")
+    for i in range(share // 128):
+        first = pl.multiple_of(role * share + i * 128, 128)
+        cols[i * 128 : (i + 1) * 128, 0:3] = wave_ref[:, pl.ds(first, 128)].astype(jnp.float32).T
+    rows_out[...] = rows_ref[...]
+    wq_out[...] = wq_ref[...]
+
+
 def tables_kernel(*refs):
-    pos_refs, (wave_ref, by_wave, by_atom, pos, cols) = refs[:4], refs[4:]
+    pos_refs, (cols, by_wave, by_atom, pos) = refs[:4], refs[4:]
     atoms = pos_refs[0].shape[1]
     for i, ref in enumerate(pos_refs):
         pos[:, i * atoms : (i + 1) * atoms] = ref[...]
     share = by_wave.shape[0] // 2
-    role = lax.axis_index("role")
-    for i in range(share // 128):
-        first = pl.multiple_of(role * share + i * 128, 128)
-        cols[i * 128 : (i + 1) * 128, 0:3] = wave_ref[:, pl.ds(first, 128)].astype(jnp.float32).T
     step = 64
     total = pos.shape[1]
 
@@ -195,7 +201,7 @@
     cols[...] = turned[...].T.astype(jnp.bfloat16)
 
 
-def short_kernel(first, count, scale, cols_ref, hidden, wrbf_ref, brbf_ref, wf_ref, sum_ref, out_ref, pairs, hot_a, hot_b):
+def short_kernel(first, count, scale, cols_ref, hidden, wrbf_ref, brbf_ref, wf_ref, sum_ref, out_ref, pairs):
     lane = 128
     atoms = cols_ref.shape[0]
     slots = cols_ref.shape[1] // 4
@@ -223,16 +229,19 @@
         select = (source == 4 * j).astype(jnp.float32).astype(jnp.bfloat16)
         return dot(cols_ref[...], select)
 
-    def make_hot(hot, wide):
-        for i in range(4):
-            code = wide[:, i * lane : (i + 1) * lane].astype(jnp.bfloat16)
-            for g in range(groups):
-                number = jnp.broadcast_to(
-                    (lanes << g).astype(jnp.float32).astype(jnp.bfloat16)[None], (atoms // 16, 16, lane)
-                ).reshape(atoms, lane)
-                hot[i * atoms : (i + 1) * atoms, g * lane : (g + 1) * lane] = jnp.where(
-                    code == number, jnp.bfloat16(1), jnp.bfloat16(0)
-                )
+    def hot_of(wide):
+        codes = [
+            wide[:, i * lane : (i + 1) * lane].astype(jnp.bfloat16) for i in range(4)
+        ]
+        code = jnp.concatenate(codes, axis=0)
+        parts = []
+        for g in range(groups):
+            number = jnp.broadcast_to(
+                (lanes << g).astype(jnp.float32).astype(jnp.bfloat16)[None],
+                (4 * atoms // 16, 16, lane),
+            ).reshape(4 * atoms, lane)
+            parts.append(jnp.where(code == number, jnp.bfloat16(1), jnp.bfloat16(0)))
+        return jnp.concatenate(parts, axis=1)
 
     def filters_of(wide):
         inner = []
@@ -251,26 +260,17 @@
             total = total + product[i * atoms : (i + 1) * atoms]
         out_ref[...] += total
 
-    wide_first = spread(first)
-    make_hot(hot_a, wide_first)
-
-    def body(jj, carry):
-        j = first + 2 * jj
-        wide_b = spread(j + 1)
-        make_hot(hot_b, wide_b)
-        gathered_a = dot(hot_a[...], hidden[...])
-        add(filters_of(spread(j)), gathered_a)
-        wide_a = spread(j + 2)
-        gathered_b = dot(hot_b[...], hidden[...])
-        add(filters_of(wide_b), gathered_b)
-        make_hot(hot_a, wide_a)
+    def body(j, carry):
+        wide = spread(first + j)
+        gathered = dot(hot_of(wide), hidden[...])
+        add(filters_of(wide), gathered)
         return carry
 
-    lax.fori_loop(0, count // 2, body, 0)
+    lax.fori_loop(0, count, body, 0)
     out_ref[...] = out_ref[...] * scale
 
 
-def local(
+def block(
     features,
     positions,
     neighbours,
@@ -307,26 +307,34 @@
     shifts = (1, roles - 1, 2)
     place_of = {0: place, **{d: from_role(place, d) for d in shifts}}
     rows_of = {0: rows, **{d: from_role(rows, d) for d in shifts}}
+    wave_cols, near_own, near_query = call(
+        begin_kernel,
+        [
+            jax.ShapeDtypeStruct((share, 128), f32),
+            jax.ShapeDtypeStruct((atoms, width), bf16),
+            jax.ShapeDtypeStruct((width, width), bf16),
+        ],
+        [wave, rows, w_query],
+        nbytes=1 << 19,
+    )
     order = (0,) + shifts
 
     by_wave, by_atom = call(
         tables_kernel,
         [jax.ShapeDtypeStruct((2 * share, roles * atoms), bf16)]
         + [jax.ShapeDtypeStruct((roles * atoms, 2 * share), bf16)],
-        [place_of[d] for d in order] + [wave],
-        scratch=[pltpu.VMEM((3, roles * atoms), f32), pltpu.VMEM((share, 128), f32)],
+        [place_of[d] for d in order] + [wave_cols],
+        scratch=[pltpu.VMEM((3, roles * atoms), f32)],
         flops=40 * share * roles * atoms,
         nbytes=4 << 20,
-        name="tables",
     )
     partial = call(
         functools.partial(structure_kernel, atom_total ** (-0.5)),
         jax.ShapeDtypeStruct((2 * share, width), bf16),
-        [rows_of[d] for d in order] + [w_query, by_wave],
+        [near_own] + [rows_of[d] for d in shifts] + [near_query, by_wave],
         scratch=[pltpu.VMEM((roles * atoms, width), bf16)],
         flops=2 * 2 * share * roles * atoms * width,
         nbytes=3 << 20,
-        name="structure",
     )
     mine = lax.all_to_all(partial.reshape(columns, 2 * piece, width), "atoms", 0, 0)
     copies = call(
@@ -335,7 +343,6 @@
         [mine, wave, kgain[None, :]],
         flops=2 * share * width,
         nbytes=1 << 20,
-        name="reduce",
     )
     everyone = lax.all_to_all(copies, "atoms", 0, 0).reshape(2 * share, width)
 
@@ -343,23 +350,21 @@
     bundle = call(
         stack_kernel,
         jax.ShapeDtypeStruct((3, atoms + 32, width), bf16),
-        [rows_of[d] for d in triple] + [place_of[d] for d in triple],
+        [rows_of[roles - 1], near_own, rows_of[1]] + [place_of[d] for d in triple],
         scratch=[pltpu.VMEM((32, width), f32)],
         nbytes=1 << 20,
-        name="stack",
     )
     low, high = from_column(bundle, columns - 1), from_column(bundle, 1)
     hidden, cols = call(
         prepare_kernel,
         [jax.ShapeDtypeStruct((9 * atoms, width), bf16), jax.ShapeDtypeStruct((atoms, 4 * slots), bf16)],
-        [rows_of[d] for d in triple]
+        [rows_of[roles - 1], near_own, rows_of[1]]
         + [low, high]
         + [place_of[d] for d in triple]
         + [neighbours[0, 0], images[0, 0], w_in],
         scratch=[pltpu.VMEM((8, 9 * atoms), f32), pltpu.VMEM((4 * slots, atoms), f32)],
         flops=2 * 9 * atoms * width * width,
         nbytes=4 << 20,
-        name="prepare",
     )
     short = jnp.zeros((atoms, width), f32)
     quads = slots // 4
@@ -370,14 +375,10 @@
             ),
             jax.ShapeDtypeStruct((atoms, width), f32),
             [cols, hidden, w_rbf, b_rbf[None, :], w_filter, short],
-            scratch=[
-                pltpu.VMEM((128, 2 * width), bf16),
-                pltpu.VMEM((4 * atoms, 9 * atoms), bf16),
-                pltpu.VMEM((4 * atoms, 9 * atoms), bf16),
-            ],
+            scratch=[pltpu.VMEM((128, 2 * width), bf16)],
+            grant=32,
             flops=slots * atoms * 9 * atoms * width,
             nbytes=4 << 20,
-            name="short%d" % half,
         )
     parts = call(
         ewald_kernel,
@@ -385,7 +386,6 @@
         [by_atom, everyone],
         flops=2 * 2 * share * roles * atoms * width,
         nbytes=4 << 20,
-        name="ewald",
     )
     back = [parts[0]] + [from_role(parts[1 + i], roles - d) for i, d in enumerate(shifts)]
     result = call(
@@ -394,7 +394,6 @@
         [rows, short] + back + [w_out],
         flops=2 * atoms * width * width,
         nbytes=1 << 20,
-        name="final",
     )
     return result[None, None]
 
@@ -415,4 +414,4 @@
         P(),
     )
     out_specs = P("role", "atoms", None, None)
-    return jax.shard_map(local, mesh=mesh, in_specs=in_specs, out_specs=out_specs, check_vma=False)
+    return jax.shard_map(block, mesh=mesh, in_specs=in_specs, out_specs=out_specs, check_vma=False)

time: 106 us -> 101 us (0.953)
  waiting for transfers between devices: 23.4 us -> 20.7 us
  Pallas kernels: 25.8 us -> 23.5 us
    ppermute x9, waiting for transfers between devices: 6.75 us -> 4.02 us  [from_role(): lax.ppermute(block, 'role', [((i + shift) % roles, i) for i in range(role...]
    pallas_call x9 -> x10, Pallas kernels: 25.8 us -> 23.5 us  [call(): pl.pallas_call(body, out_shape=out, in_specs=[VMEM] * len(ins), out_specs...]
    unnamed x31 -> x29, local copies, waits for them, and re-layouts: 4.31 us -> 4.31 us
  transfers between devices with their start and end apart: 12 -> 12, of which waited for: 4 -> 3; matrix products, arithmetic and copies ran while one was open for 1% -> 1% of each run, Pallas kernels for 21% -> 20%
where the time goes in v2:
time: 101 us; the launch traced here: 99.6 us
  blocking collectives  28 us (28%)
  Pallas kernels  23.5 us (23%)
  starting transfers between devices  22.8 us (23%)
  waiting for transfers between devices  20.7 us (20%)
  local copies, waits for them, and re-layouts  4.37 us (4%)
    all_to_all x1, blocking collectives, block(): lax.all_to_all(partial.reshape(columns, 2 * piece, width), 'atoms', 0, 0)  28 us
    pallas_call x10, Pallas kernels, call(): pl.pallas_call(body, out_shape=out, in_specs=[VMEM] * len(ins), out_specs...  23.5 us
    ppermute x2, waiting for transfers between devices, from_column(): lax.ppermute(block, 'atoms', [((i + shift) % columns, i) for i in range(c...  16.7 us
    ppermute x9, starting transfers between devices, from_role(): lax.ppermute(block, 'role', [((i + shift) % roles, i) for i in range(role...  10.8 us
    all_to_all x1, starting transfers between devices, block(): everyone = lax.all_to_all(copies, 'atoms', 0, 0).reshape(2 * share, width)  6.66 us
    ppermute x2, starting transfers between devices, from_column(): lax.ppermute(block, 'atoms', [((i + shift) % columns, i) for i in range(c...  5.27 us
    unnamed x29, local copies, waits for them, and re-layouts  4.31 us
    ppermute x9, waiting for transfers between devices, from_role(): lax.ppermute(block, 'role', [((i + shift) % roles, i) for i in range(role...  4.02 us
  transfers between devices with their start and end apart: 12, of which 3 were waited for; matrix products, arithmetic and copies ran while one was open for 1% of the time, Pallas kernels for 20%

profile of v2, /device:TPU:24, one launch (start us, length us, event | category | flops | bytes accessed | tf_op | source)
XLA Modules:
  0.0 99.6 jit_solution(10864955309723291998)
XLA Ops:
  0.0 1.9 %collective-permute-start = (bf16[256,256]{1,0:T(8,128)(2,1)}, bf16[256,256]{1,0:T(8,128)(2,1)S(1)}, u32[]{:S(2)}, u32[]{:S(2)}) collective-permute-start(bf16[256,256]{1,0:T(8,128)(2,1)} %bitcast.21), channel_id=1, source_target_pairs={{192,0},{0,64},{64,128},{128,192},{193,1},{1,65},{65,129},{129,193... | collective-permute-start | bytes 393224 | tf_op jit(solution)/shard_map/ppermute | solution.py:300
  1.9 0.1 collective-permute-start.1
  2.0 1.4 %collective-permute-start.7 = (bf16[256,256]{1,0:T(8,128)(2,1)}, bf16[256,256]{1,0:T(8,128)(2,1)S(1)}, u32[]{:S(2)}, u32[]{:S(2)}) collective-permute-start(bf16[256,256]{1,0:T(8,128)(2,1)} %bitcast.23), channel_id=1, source_target_pairs={{128,0},{192,64},{0,128},{64,192},{129,1},{193,65},{1,129},{65,193... | collective-permute-start | bytes 393224 | tf_op jit(solution)/shard_map/ppermute | solution.py:300
  3.4 0.7 copy.15
  4.1 2.0 %collective-permute-start.2 = (f32[3,256]{1,0:T(4,128)S(1)}, f32[3,256]{1,0:T(4,128)S(1)}, u32[]{:S(2)}, u32[]{:S(2)}) collective-permute-start(f32[3,256]{1,0:T(4,128)S(1)} %bitcast.26), channel_id=1, source_target_pairs={{192,0},{0,64},{64,128},{128,192},{193,1},{1,65},{65,129},{129,193... | collective-permute-start | bytes 9224 | tf_op jit(solution)/shard_map/ppermute | solution.py:300
  6.1 0.6 collective-permute-start.3
  6.7 2.5 %collective-permute-done.2.refs_3_.p0.refs_2_ = f32[3,256]{1,0:T(4,128)S(1)} collective-permute-done((f32[3,256]{1,0:T(4,128)S(1)}, f32[3,256]{1,0:T(4,128)S(1)}, u32[]{:S(2)}, u32[]{:S(2)}) %collective-permute-start.2) | collective-permute-done | bytes 3104 | tf_op jit(solution)/shard_map/ppermute | solution.py:300
  9.2 0.9 collective-permute-start.6
  10.1 0.0 copy-start
  10.1 0.9 copy-done
  11.0 0.0 copy-start.4
  11.0 0.8 copy-done.4
  11.8 0.0 copy-start.5
  11.8 0.9 copy-done.5
  12.7 0.1 shard_map.118
  12.8 0.0 collective-permute-done.3.refs_5_.p2.refs_1_
  12.8 1.5 %collective-permute-done.6.refs_3_ = f32[3,256]{1,0:T(4,128)S(1)} collective-permute-done((f32[3,256]{1,0:T(4,128)S(1)}, f32[3,256]{1,0:T(4,128)S(1)}, u32[]{:S(2)}, u32[]{:S(2)}) %collective-permute-start.6) | collective-permute-done | bytes 3104 | tf_op jit(solution)/shard_map/ppermute | solution.py:300
  14.3 3.5 %shard_map.123 = (bf16[1024,1024]{1,0:T(8,128)(2,1)S(1)}, bf16[1024,1024]{1,0:T(8,128)(2,1)S(1)}) custom-call(f32[3,256]{1,0:T(4,128)S(1)} %bitcast.29, f32[3,256]{1,0:T(4,128)S(1)} %collective-permute-done.3.refs_5_.p2.refs_1_, f32[3,256]{1,0:T(4,128)S(1)} %collective-permute-done.2.refs_3_.p0.refs_2_, f32[3,256]{1,0:T(4,128)S(1)} %collective-permute-done.6.refs_3_, ...), custom_call_target="tpu_custom_call" | custom-call | flops 20971520 | bytes 4194304 | tf_op jit(solution)/shard_map/pallas_call | solution.py:36
  17.8 0.0 collective-permute-done.refs_0_.r0.refs_2_
  17.8 0.0 collective-permute-done.1.refs_2_.r2.refs_1_
  17.8 0.0 collective-permute-done.7.refs_3_
  17.8 0.0 copy-start.8
  17.8 1.0 shard_map.124
  18.8 0.0 copy-start.2
  18.8 0.0 copy-start.6
  18.8 0.0 copy-start.7
  18.8 28.0 %all_to_all.10.mine_ref = bf16[64,16,256]{2,1,0:T(8,128)(2,1)S(1)} all-to-all(bf16[64,16,256]{2,1,0:T(8,128)(2,1)S(1)} %bitcast.19), channel_id=1, replica_groups=mesh['role'=4,'atoms'=64] {'atoms'}, dimensions={0} | all-to-all | bytes 1048576 | tf_op jit(solution)/shard_map/all_to_all | solution.py:339
  46.9 0.0 copy-done.8
  46.9 0.9 shard_map.125
  47.8 0.0 copy-start.11
  47.8 0.0 copy-start.12
  47.8 0.0 copy-start.13
  47.8 6.7 %all-to-all-start.1 = ((bf16[64,16,256]{2,1,0:T(8,128)(2,1)}), bf16[64,16,256]{2,1,0:T(8,128)(2,1)S(1)}, u32[]{:S(2)}, u32[]{:S(2)}) async-start(bf16[64,16,256]{2,1,0:T(8,128)(2,1)} %shard_map.125), calls=%async_computation.1 | async-start | bytes 1048576 | tf_op jit(solution)/shard_map/all_to_all | solution.py:347
  54.5 0.1 shard_map.119
  54.6 0.1 collective-permute-start.4
  54.7 5.1 %collective-permute-start.5 = (bf16[3,288,256]{2,1,0:T(8,128)(2,1)S(1)}, bf16[3,288,256]{2,1,0:T(8,128)(2,1)S(1)}, u32[]{:S(2)}, u32[]{:S(2)}) collective-permute-start(bf16[3,288,256]{2,1,0:T(8,128)(2,1)S(1)} %shard_map.119), channel_id=1, source_target_pairs={{1,0},{2,1},{3,2},{4,3},{5,4},{6,5},{7,6},{8,7},{9,8},{10,9},{11,1... | collective-permute-start | bytes 1327112 | tf_op jit(solution)/shard_map/ppermute | solution.py:303
  59.8 16.7 %collective-permute-done.4.low_ref = bf16[3,288,256]{2,1,0:T(8,128)(2,1)S(1)} collective-permute-done((bf16[3,288,256]{2,1,0:T(8,128)(2,1)S(1)}, bf16[3,288,256]{2,1,0:T(8,128)(2,1)S(1)}, u32[]{:S(2)}, u32[]{:S(2)}) %collective-permute-start.4) | collective-permute-done | bytes 442400 | tf_op jit(solution)/shard_map/ppermute | solution.py:303
  76.5 0.0 collective-permute-done.5.high_ref
  76.5 0.0 copy-done.2
  76.5 0.0 copy-done.6
  76.5 0.0 copy-done.7
  76.5 1.4 %shard_map.120 = (bf16[2304,256]{1,0:T(8,128)(2,1)S(1)}, bf16[256,128]{1,0:T(8,128)(2,1)S(1)}) custom-call(bf16[256,256]{1,0:T(8,128)(2,1)S(1)} %collective-permute-done.refs_0_.r0.refs_2_, bf16[256,256]{1,0:T(8,128)(2,1)S(1)} %get-tuple-element.12.refs_1_.r1.refs_0_, bf16[256,256]{1,0:T(8,128)(2,1)S(1)} %collective-permute-done.1.refs_2_.r2.refs_1_, ...), custom_call_target="tpu_custom_call" | custom-call | flops 301989888 | bytes 4194304 | tf_op jit(solution)/shard_map/pallas_call | solution.py:36
  78.0 0.0 copy-done.11
  78.0 0.0 copy-done.12
  78.0 0.0 copy-done.13
  78.0 7.4 %shard_map.121.sum_ref = f32[256,256]{1,0:T(8,128)S(1)} custom-call(bf16[256,128]{1,0:T(8,128)(2,1)S(1)} %get-tuple-element.13.cols_ref, bf16[2304,256]{1,0:T(8,128)(2,1)S(1)} %get-tuple-element.14.hidden, bf16[64,256]{1,0:T(8,128)(2,1)S(1)} %copy-done.12, f32[1,256]{1,0:T(1,128)S(1)} %bitcast.35, bf16[256,256]{1,0:T(8,128)(2,1)S(1)} %copy-done.11, ...), custom_call_target="tpu_custom_call" | custom-call | flops 4831838208 | bytes 4194304 | tf_op jit(solution)/shard_map/pallas_call | solution.py:36
  85.4 0.0 copy-start.9
  85.4 1.0 %copy-done.9 = bf16[2304,256]{1,0:T(8,128)(2,1)} copy-done((bf16[2304,256]{1,0:T(8,128)(2,1)}, bf16[2304,256]{1,0:T(8,128)(2,1)S(1)}, u32[]{:S(2)}) %copy-start.9) | copy-done | bytes 1179672
  86.5 0.0 all-to-all-done.1
  86.5 0.0 copy-start.10
  86.5 0.7 shard_map.126
  87.2 1.8 %collective-permute-start.10 = (bf16[256,256]{1,0:T(8,128)(2,1)S(1)}, bf16[256,256]{1,0:T(8,128)(2,1)S(1)}, u32[]{:S(2)}, u32[]{:S(2)}) collective-permute-start(bf16[256,256]{1,0:T(8,128)(2,1)S(1)} %get-tuple-element.19), channel_id=1, source_target_pairs={{128,0},{192,64},{0,128},{64,192},{129,1},{193,65},{1,129},{65,193... | collective-permute-start | bytes 393224 | tf_op jit(solution)/shard_map/ppermute | solution.py:300
  89.1 2.1 %collective-permute-start.8 = (bf16[256,256]{1,0:T(8,128)(2,1)S(1)}, bf16[256,256]{1,0:T(8,128)(2,1)S(1)}, u32[]{:S(2)}, u32[]{:S(2)}) collective-permute-start(bf16[256,256]{1,0:T(8,128)(2,1)S(1)} %get-tuple-element.21), channel_id=1, source_target_pairs={{192,0},{0,64},{64,128},{128,192},{193,1},{1,65},{65,129},{129,193... | collective-permute-start | bytes 393224 | tf_op jit(solution)/shard_map/ppermute | solution.py:300
  91.1 0.0 copy-start.1
  91.1 0.0 copy-start.3
  91.2 0.0 collective-permute-start.9
  91.2 0.0 copy-done.10
  91.2 7.5 %shard_map.122.short_ref = f32[256,256]{1,0:T(8,128)S(1)} custom-call(bf16[256,128]{1,0:T(8,128)(2,1)S(1)} %get-tuple-element.13.cols_ref, bf16[2304,256]{1,0:T(8,128)(2,1)S(1)} %copy-done.10, bf16[64,256]{1,0:T(8,128)(2,1)S(1)} %copy-done.12, f32[1,256]{1,0:T(1,128)S(1)} %bitcast.36, bf16[256,256]{1,0:T(8,128)(2,1)S(1)} %copy-done.11, ...), custom_call_target="tpu_custom_call" | custom-call | flops 4831838208 | bytes 4194304 | tf_op jit(solution)/shard_map/pallas_call | solution.py:36
  98.6 0.0 collective-permute-done.10.e3_ref
  98.7 0.0 collective-permute-done.8.e1_ref
  98.7 0.0 collective-permute-done.9.e2_ref
  98.7 0.0 copy-done.1
  98.7 0.0 copy-done.3
  98.7 0.9 shard_map.127
  (2 shorter events, 0.1 us)
Async XLA Ops:
  0.0 17.8 %collective-permute-start = (bf16[256,256]{1,0:T(8,128)(2,1)}, bf16[256,256]{1,0:T(8,128)(2,1)S(1)}, u32[]{:S(2)}, u32[]{:S(2)}) collective-permute-start(bf16[256,256]{1,0:T(8,128)(2,1)} %bitcast.21), channel_id=1, source_target_pairs={{192,0},{0,64},{64,128},{128,192},{193,1},{1,65},{65,129},{129,193... | collective-permute-start | bytes 393224 | tf_op jit(solution)/shard_map/ppermute | solution.py:300
  1.9 15.9 %collective-permute-start.1 = (bf16[256,256]{1,0:T(8,128)(2,1)}, bf16[256,256]{1,0:T(8,128)(2,1)S(1)}, u32[]{:S(2)}, u32[]{:S(2)}) collective-permute-start(bf16[256,256]{1,0:T(8,128)(2,1)} %bitcast.22), channel_id=1, source_target_pairs={{64,0},{128,64},{192,128},{0,192},{65,1},{129,65},{193,129},{1,193... | collective-permute-start | bytes 393224 | tf_op jit(solution)/shard_map/ppermute | solution.py:300
  2.0 15.8 %collective-permute-start.7 = (bf16[256,256]{1,0:T(8,128)(2,1)}, bf16[256,256]{1,0:T(8,128)(2,1)S(1)}, u32[]{:S(2)}, u32[]{:S(2)}) collective-permute-start(bf16[256,256]{1,0:T(8,128)(2,1)} %bitcast.23), channel_id=1, source_target_pairs={{128,0},{192,64},{0,128},{64,192},{129,1},{193,65},{1,129},{65,193... | collective-permute-start | bytes 393224 | tf_op jit(solution)/shard_map/ppermute | solution.py:300
  4.1 5.1 %collective-permute-start.2 = (f32[3,256]{1,0:T(4,128)S(1)}, f32[3,256]{1,0:T(4,128)S(1)}, u32[]{:S(2)}, u32[]{:S(2)}) collective-permute-start(f32[3,256]{1,0:T(4,128)S(1)} %bitcast.26), channel_id=1, source_target_pairs={{192,0},{0,64},{64,128},{128,192},{193,1},{1,65},{65,129},{129,193... | collective-permute-start | bytes 9224 | tf_op jit(solution)/shard_map/ppermute | solution.py:300
  6.1 6.7 %collective-permute-start.3 = (f32[3,256]{1,0:T(4,128)S(1)}, f32[3,256]{1,0:T(4,128)S(1)}, u32[]{:S(2)}, u32[]{:S(2)}) collective-permute-start(f32[3,256]{1,0:T(4,128)S(1)} %bitcast.27), channel_id=1, source_target_pairs={{64,0},{128,64},{192,128},{0,192},{65,1},{129,65},{193,129},{1,193... | collective-permute-start | bytes 9224 | tf_op jit(solution)/shard_map/ppermute | solution.py:300
  9.2 5.1 %collective-permute-start.6 = (f32[3,256]{1,0:T(4,128)S(1)}, f32[3,256]{1,0:T(4,128)S(1)}, u32[]{:S(2)}, u32[]{:S(2)}) collective-permute-start(f32[3,256]{1,0:T(4,128)S(1)} %bitcast.28), channel_id=1, source_target_pairs={{128,0},{192,64},{0,128},{64,192},{129,1},{193,65},{1,129},{65,193... | collective-permute-start | bytes 9224 | tf_op jit(solution)/shard_map/ppermute | solution.py:300
  10.1 0.9 copy-start
  11.0 0.8 copy-start.4
  11.8 0.9 copy-start.5
  17.8 29.1 %copy-start.8 = (f32[256]{0:T(256)S(1)}, f32[256]{0:T(256)}, u32[]{:S(2)}) copy-start(f32[256]{0:T(256)} %param.17) | copy-start | bytes 3076
  18.8 57.7 %copy-start.2 = (bf16[256,256]{1,0:T(8,128)(2,1)S(1)}, bf16[256,256]{1,0:T(8,128)(2,1)}, u32[]{:S(2)}) copy-start(bf16[256,256]{1,0:T(8,128)(2,1)} %win_ref.1) | copy-start | bytes 393220
  18.8 57.7 %copy-start.6 = (s32[1,1,32,256]{3,2,1,0:T(8,128)S(1)}, s32[1,1,32,256]{3,2,1,0:T(8,128)}, u32[]{:S(2)}) copy-start(s32[1,1,32,256]{3,2,1,0:T(8,128)} %param.14) | copy-start | bytes 98308
  18.8 57.7 %copy-start.7 = (s32[1,1,32,256]{3,2,1,0:T(8,128)S(1)}, s32[1,1,32,256]{3,2,1,0:T(8,128)}, u32[]{:S(2)}) copy-start(s32[1,1,32,256]{3,2,1,0:T(8,128)} %param.15) | copy-start | bytes 98308
  47.8 30.1 %copy-start.11 = (bf16[256,256]{1,0:T(8,128)(2,1)S(1)}, bf16[256,256]{1,0:T(8,128)(2,1)}, u32[]{:S(2)}) copy-start(bf16[256,256]{1,0:T(8,128)(2,1)} %wf_ref.3) | copy-start | bytes 393220
  47.8 30.2 %copy-start.12 = (bf16[64,256]{1,0:T(8,128)(2,1)S(1)}, bf16[64,256]{1,0:T(8,128)(2,1)}, u32[]{:S(2)}) copy-start(bf16[64,256]{1,0:T(8,128)(2,1)} %wrbf_ref.3) | copy-start | bytes 98308
  47.8 30.2 %copy-start.13 = (f32[256]{0:T(256)S(1)}, f32[256]{0:T(256)}, u32[]{:S(2)}) copy-start(f32[256]{0:T(256)} %param.21) | copy-start | bytes 3076
  47.8 38.6 %all-to-all-start.1 = ((bf16[64,16,256]{2,1,0:T(8,128)(2,1)}), bf16[64,16,256]{2,1,0:T(8,128)(2,1)S(1)}, u32[]{:S(2)}, u32[]{:S(2)}) async-start(bf16[64,16,256]{2,1,0:T(8,128)(2,1)} %shard_map.125), calls=%async_computation.1 | async-start | bytes 1048576 | tf_op jit(solution)/shard_map/all_to_all | solution.py:347
  54.6 21.9 %collective-permute-start.4 = (bf16[3,288,256]{2,1,0:T(8,128)(2,1)S(1)}, bf16[3,288,256]{2,1,0:T(8,128)(2,1)S(1)}, u32[]{:S(2)}, u32[]{:S(2)}) collective-permute-start(bf16[3,288,256]{2,1,0:T(8,128)(2,1)S(1)} %shard_map.119), channel_id=1, source_target_pairs={{63,0},{0,1},{1,2},{2,3},{3,4},{4,5},{5,6},{6,7},{7,8},{8,9},{9,10... | collective-permute-start | bytes 1327112 | tf_op jit(solution)/shard_map/ppermute | solution.py:303
  54.7 21.8 %collective-permute-start.5 = (bf16[3,288,256]{2,1,0:T(8,128)(2,1)S(1)}, bf16[3,288,256]{2,1,0:T(8,128)(2,1)S(1)}, u32[]{:S(2)}, u32[]{:S(2)}) collective-permute-start(bf16[3,288,256]{2,1,0:T(8,128)(2,1)S(1)} %shard_map.119), channel_id=1, source_target_pairs={{1,0},{2,1},{3,2},{4,3},{5,4},{6,5},{7,6},{8,7},{9,8},{10,9},{11,1... | collective-permute-start | bytes 1327112 | tf_op jit(solution)/shard_map/ppermute | solution.py:303
  85.4 1.0 %copy-start.9 = (bf16[2304,256]{1,0:T(8,128)(2,1)}, bf16[2304,256]{1,0:T(8,128)(2,1)S(1)}, u32[]{:S(2)}) copy-start(bf16[2304,256]{1,0:T(8,128)(2,1)S(1)} %get-tuple-element.14.hidden) | copy-start | bytes 3538948
  86.5 4.7 %copy-start.10 = (bf16[2304,256]{1,0:T(8,128)(2,1)S(1)}, bf16[2304,256]{1,0:T(8,128)(2,1)}, u32[]{:S(2)}) copy-start(bf16[2304,256]{1,0:T(8,128)(2,1)} %copy-done.9) | copy-start | bytes 3538948
  87.2 11.4 %collective-permute-start.10 = (bf16[256,256]{1,0:T(8,128)(2,1)S(1)}, bf16[256,256]{1,0:T(8,128)(2,1)S(1)}, u32[]{:S(2)}, u32[]{:S(2)}) collective-permute-start(bf16[256,256]{1,0:T(8,128)(2,1)S(1)} %get-tuple-element.19), channel_id=1, source_target_pairs={{128,0},{192,64},{0,128},{64,192},{129,1},{193,65},{1,129},{65,193... | collective-permute-start | bytes 393224 | tf_op jit(solution)/shard_map/ppermute | solution.py:300
  89.1 9.6 %collective-permute-start.8 = (bf16[256,256]{1,0:T(8,128)(2,1)S(1)}, bf16[256,256]{1,0:T(8,128)(2,1)S(1)}, u32[]{:S(2)}, u32[]{:S(2)}) collective-permute-start(bf16[256,256]{1,0:T(8,128)(2,1)S(1)} %get-tuple-element.21), channel_id=1, source_target_pairs={{192,0},{0,64},{64,128},{128,192},{193,1},{1,65},{65,129},{129,193... | collective-permute-start | bytes 393224 | tf_op jit(solution)/shard_map/ppermute | solution.py:300
  91.1 7.5 %copy-start.1 = (bf16[1,1,256,256]{3,2,1,0:T(8,128)(2,1)S(1)}, bf16[1,1,256,256]{3,2,1,0:T(8,128)(2,1)}, u32[]{:S(2)}) copy-start(bf16[1,1,256,256]{3,2,1,0:T(8,128)(2,1)} %param.12) | copy-start | bytes 393220
  91.1 7.5 %copy-start.3 = (bf16[256,256]{1,0:T(8,128)(2,1)S(1)}, bf16[256,256]{1,0:T(8,128)(2,1)}, u32[]{:S(2)}) copy-start(bf16[256,256]{1,0:T(8,128)(2,1)} %wout_ref.1) | copy-start | bytes 393220
  91.2 7.5 %collective-permute-start.9 = (bf16[256,256]{1,0:T(8,128)(2,1)S(1)}, bf16[256,256]{1,0:T(8,128)(2,1)S(1)}, u32[]{:S(2)}, u32[]{:S(2)}) collective-permute-start(bf16[256,256]{1,0:T(8,128)(2,1)S(1)} %get-tuple-element.20), channel_id=1, source_target_pairs={{64,0},{128,64},{192,128},{0,192},{65,1},{129,65},{193,129},{1,193... | collective-permute-start | bytes 393224 | tf_op jit(solution)/shard_map/ppermute | solution.py:300

commit v3 on v2

--- a/solution.py
+++ b/solution.py
@@ -61,31 +61,39 @@
     return 2.0 * (half * even), 1.0 - 2.0 * (half * half)
 
 
-def begin_kernel(wave_ref, rows_ref, wq_ref, cols, rows_out, wq_out):
+def begin_kernel(wave_ref, rows_ref, place_ref, wq_ref, cols, rows_out, place_out, wq_out, flat):
     share = cols.shape[0]
     role = lax.axis_index("role")
+    flat[...] = jnp.zeros_like(flat)
     for i in range(share // 128):
         first = pl.multiple_of(role * share + i * 128, 128)
-        cols[i * 128 : (i + 1) * 128, 0:3] = wave_ref[:, pl.ds(first, 128)].astype(jnp.float32).T
+        waves = wave_ref[:, pl.ds(first, 128)].astype(jnp.float32)
+        for k in range(3):
+            flat[3 * k : 3 * k + 3, :] = waves
+        cols[i * 128 : (i + 1) * 128, :] = flat[...].T.astype(jnp.bfloat16)
     rows_out[...] = rows_ref[...]
+    place_out[...] = place_ref[...]
     wq_out[...] = wq_ref[...]
 
 
 def tables_kernel(*refs):
-    pos_refs, (cols, by_wave, by_atom, pos) = refs[:4], refs[4:]
+    pos_refs, (cols, by_wave, by_atom, pos, parts) = refs[:4], refs[4:]
     atoms = pos_refs[0].shape[1]
+    total = pos.shape[1]
+    pos[...] = jnp.zeros_like(pos)
     for i, ref in enumerate(pos_refs):
-        pos[:, i * atoms : (i + 1) * atoms] = ref[...]
+        rest = ref[...]
+        for k in range(3):
+            rounded = rest.astype(jnp.bfloat16).astype(jnp.float32)
+            pos[3 * k : 3 * k + 3, i * atoms : (i + 1) * atoms] = rounded
+            rest = rest - rounded
+    parts[...] = pos[...].astype(jnp.bfloat16)
     share = by_wave.shape[0] // 2
     step = 64
-    total = pos.shape[1]
 
     def block(j, carry):
         waves = cols[pl.ds(pl.multiple_of(j * step, step), step), :]
-        turns = (
-            waves[:, 0:1] * pos[0:1, :] + waves[:, 1:2] * pos[1:2, :] + waves[:, 2:3] * pos[2:3, :]
-        )
-        sine, cosine = sine_cosine(turns)
+        sine, cosine = sine_cosine(dot(waves, parts[...]))
         both = jnp.stack(
             [cosine.reshape(step // 8, 8, total), sine.reshape(step // 8, 8, total)], axis=1
         ).reshape(2 * step, total)
@@ -97,13 +105,26 @@
     lax.fori_loop(0, share // step, block, 0)
 
 
-def structure_kernel(scale, *refs):
+def core_half(size, other):
+    core = lax.axis_index("atoms") & 1
+    core = 1 - core if other else core
+    return pl.ds(pl.multiple_of(core * size, size), size)
+
+
+def send_kernel(scale, *refs):
     rows_refs, (wq_ref, table, out_ref, queries) = refs[:4], refs[4:]
     atoms = rows_refs[0].shape[0]
     weight = wq_ref[...]
     for i, rows in enumerate(rows_refs):
         queries[i * atoms : (i + 1) * atoms, :] = dot(rows[...], weight).astype(jnp.bfloat16)
-    out_ref[...] = (dot(table[...], queries[...]) * scale).astype(jnp.bfloat16)
+    part = core_half(out_ref.shape[0], True)
+    out_ref[...] = (dot(table[part, :], queries[...]) * scale).astype(jnp.bfloat16)
+
+
+def keep_kernel(scale, queries, table, got_ref, out_ref):
+    part = core_half(out_ref.shape[0], False)
+    own = dot(table[part, :], queries[...]) * scale
+    out_ref[...] = (own + got_ref[...].astype(jnp.float32)).astype(jnp.bfloat16)
 
 
 def stack_kernel(*refs):
@@ -121,10 +142,11 @@
 
 
 def reduce_kernel(mine_ref, wave_ref, kgain_ref, out_ref):
-    columns, rows, width = mine_ref.shape
+    chips, rows, width = mine_ref.shape
     piece = rows // 2
-    share = columns * piece
-    first = lax.axis_index("role") * share + lax.axis_index("atoms") * piece
+    share = 2 * chips * piece
+    column = lax.axis_index("atoms")
+    first = lax.axis_index("role") * share + ((column & 1) * chips + (column >> 1)) * piece
     start = pl.multiple_of((first // 128) * 128, 128)
     waves = wave_ref[:, pl.ds(start, 128)].astype(jnp.float32)
     squares = jnp.broadcast_to(jnp.sum(waves * waves, axis=0, keepdims=True), (piece, 128))
@@ -134,14 +156,17 @@
     k_filter = ewald_scale * kgain_ref[...] * (jnp.exp(-square / damping) / square)
     total = jnp.sum(mine_ref[...].astype(jnp.float32), axis=0)
     filtered = total * jnp.concatenate([k_filter, k_filter], axis=0)
-    out_ref[...] = jnp.broadcast_to(filtered.astype(jnp.bfloat16)[None], (columns, rows, width))
-
-
-def ewald_kernel(table_ref, filtered_ref, out_ref):
-    bricks, atoms, _ = out_ref.shape
-    for i in range(bricks):
-        part = table_ref[i * atoms : (i + 1) * atoms, :]
-        out_ref[i] = dot(part, filtered_ref[...]).astype(jnp.bfloat16)
+    out_ref[...] = jnp.broadcast_to(filtered.astype(jnp.bfloat16)[None], (chips, rows, width))
+
+
+def ewald_kernel(table_ref, own_ref, other_ref, *out_refs):
+    atoms, _ = out_refs[0].shape
+    size = own_ref.shape[0]
+    for i, out_ref in enumerate(out_refs):
+        part = slice(i * atoms, (i + 1) * atoms)
+        total = dot(table_ref[part, core_half(size, False)], own_ref[...])
+        total = total + dot(table_ref[part, core_half(size, True)], other_ref[...])
+        out_ref[...] = total.astype(jnp.bfloat16)
 
 
 def final_kernel(rows_ref, short_ref, e0_ref, e1_ref, e2_ref, e3_ref, wout_ref, out_ref):
@@ -305,52 +330,67 @@
         )
 
     shifts = (1, roles - 1, 2)
+    order = (0,) + shifts
+    wave_cols, rows, place, near_query = call(
+        begin_kernel,
+        [
+            jax.ShapeDtypeStruct((share, 128), bf16),
+            jax.ShapeDtypeStruct((atoms, width), bf16),
+            jax.ShapeDtypeStruct((3, atoms), f32),
+            jax.ShapeDtypeStruct((width, width), bf16),
+        ],
+        [wave, rows, place, w_query],
+        scratch=[pltpu.VMEM((128, 128), f32)],
+        nbytes=1 << 19,
+    )
     place_of = {0: place, **{d: from_role(place, d) for d in shifts}}
     rows_of = {0: rows, **{d: from_role(rows, d) for d in shifts}}
-    wave_cols, near_own, near_query = call(
-        begin_kernel,
-        [
-            jax.ShapeDtypeStruct((share, 128), f32),
-            jax.ShapeDtypeStruct((atoms, width), bf16),
-            jax.ShapeDtypeStruct((width, width), bf16),
-        ],
-        [wave, rows, w_query],
-        nbytes=1 << 19,
-    )
-    order = (0,) + shifts
-
     by_wave, by_atom = call(
         tables_kernel,
         [jax.ShapeDtypeStruct((2 * share, roles * atoms), bf16)]
         + [jax.ShapeDtypeStruct((roles * atoms, 2 * share), bf16)],
         [place_of[d] for d in order] + [wave_cols],
-        scratch=[pltpu.VMEM((3, roles * atoms), f32)],
+        scratch=[pltpu.VMEM((128, roles * atoms), f32), pltpu.VMEM((128, roles * atoms), bf16)],
         flops=40 * share * roles * atoms,
         nbytes=4 << 20,
     )
-    partial = call(
-        functools.partial(structure_kernel, atom_total ** (-0.5)),
-        jax.ShapeDtypeStruct((2 * share, width), bf16),
-        [near_own] + [rows_of[d] for d in shifts] + [near_query, by_wave],
-        scratch=[pltpu.VMEM((roles * atoms, width), bf16)],
-        flops=2 * 2 * share * roles * atoms * width,
+    norm = atom_total ** (-0.5)
+    partner = [(i, i ^ 1) for i in range(columns)]
+    same_core = [list(range(c, columns, 2)) for c in range(2)]
+    sent, queries = call(
+        functools.partial(send_kernel, norm),
+        [jax.ShapeDtypeStruct((share, width), bf16), jax.ShapeDtypeStruct((roles * atoms, width), bf16)],
+        [rows_of[d] for d in order] + [near_query, by_wave],
+        flops=2 * share * roles * atoms * width,
         nbytes=3 << 20,
     )
-    mine = lax.all_to_all(partial.reshape(columns, 2 * piece, width), "atoms", 0, 0)
+    got = lax.ppermute(sent, "atoms", partner)
+    kept = call(
+        functools.partial(keep_kernel, norm),
+        jax.ShapeDtypeStruct((share, width), bf16),
+        [queries, by_wave, got],
+        flops=2 * share * roles * atoms * width,
+        nbytes=2 << 20,
+    )
+    chunks = (columns // 2, 2 * piece, width)
+    mine = lax.all_to_all(kept.reshape(chunks), "atoms", 0, 0, axis_index_groups=same_core)
     copies = call(
         reduce_kernel,
-        jax.ShapeDtypeStruct((columns, 2 * piece, width), bf16),
+        jax.ShapeDtypeStruct(chunks, bf16),
         [mine, wave, kgain[None, :]],
         flops=2 * share * width,
         nbytes=1 << 20,
     )
-    everyone = lax.all_to_all(copies, "atoms", 0, 0).reshape(2 * share, width)
+    half_own = lax.all_to_all(copies, "atoms", 0, 0, axis_index_groups=same_core).reshape(
+        share, width
+    )
+    half_other = lax.ppermute(half_own, "atoms", partner)
 
     triple = (roles - 1, 0, 1)
     bundle = call(
         stack_kernel,
         jax.ShapeDtypeStruct((3, atoms + 32, width), bf16),
-        [rows_of[roles - 1], near_own, rows_of[1]] + [place_of[d] for d in triple],
+        [rows_of[d] for d in triple] + [place_of[d] for d in triple],
         scratch=[pltpu.VMEM((32, width), f32)],
         nbytes=1 << 20,
     )
@@ -358,7 +398,7 @@
     hidden, cols = call(
         prepare_kernel,
         [jax.ShapeDtypeStruct((9 * atoms, width), bf16), jax.ShapeDtypeStruct((atoms, 4 * slots), bf16)],
-        [rows_of[roles - 1], near_own, rows_of[1]]
+        [rows_of[d] for d in triple]
         + [low, high]
         + [place_of[d] for d in triple]
         + [neighbours[0, 0], images[0, 0], w_in],
@@ -382,8 +422,8 @@
         )
     parts = call(
         ewald_kernel,
-        jax.ShapeDtypeStruct((roles, atoms, width), bf16),
-        [by_atom, everyone],
+        [jax.ShapeDtypeStruct((atoms, width), bf16)] * roles,
+        [by_atom, half_own, half_other],
         flops=2 * 2 * share * roles * atoms * width,
         nbytes=4 << 20,
     )

time: 101 us -> 95.4 us (0.945)
  the two profiles are of different devices: /device:TPU:24 before, /device:TPU:1 now
where the time goes in v3:
time: 95.4 us; the launch traced here: 95.1 us
  starting transfers between devices  29.3 us (31%)
  Pallas kernels  23.9 us (25%)
  blocking collectives  19.6 us (21%)
  waiting for transfers between devices  16.3 us (17%)
  local copies, waits for them, and re-layouts  5.6 us (6%)
    pallas_call x11, Pallas kernels, call(): pl.pallas_call(body, out_shape=out, in_specs=[VMEM] * len(ins), out_specs...  23.9 us
    all_to_all x1, blocking collectives, block(): lax.all_to_all(kept.reshape(chunks), 'atoms', 0, 0, axis_index_groups=sam...  19.6 us
    ppermute x9, starting transfers between devices, from_role(): lax.ppermute(block, 'role', [((i + shift) % roles, i) for i in range(role...  10.9 us
    ppermute x2, waiting for transfers between devices, from_column(): lax.ppermute(block, 'atoms', [((i + shift) % columns, i) for i in range(c...  9.98 us
    all_to_all x1, starting transfers between devices, block(): lax.all_to_all(copies, 'atoms', 0, 0, axis_index_groups=same_core)  6.72 us
    unnamed x29, local copies, waits for them, and re-layouts  5.58 us
    ppermute x9, waiting for transfers between devices, from_role(): lax.ppermute(block, 'role', [((i + shift) % roles, i) for i in range(role...  5.17 us
    ppermute x1, starting transfers between devices, block(): got = lax.ppermute(sent, 'atoms', partner)  4.89 us
  transfers between devices with their start and end apart: 14, of which 6 were waited for; matrix products, arithmetic and copies ran while one was open for 0% of the time, Pallas kernels for 21%

profile of v3, /device:TPU:1, one launch (start us, length us, event | category | flops | bytes accessed | tf_op | source)
XLA Modules:
  0.0 95.1 jit_solution(7350968784347511796)
XLA Ops:
  0.0 0.7 copy.15
  0.7 0.0 copy-start.2
  0.7 0.8 copy-done.2
  1.4 0.0 copy-start.4
  1.4 0.9 copy-done.4
  2.4 0.9 copy-done.5
  3.3 0.1 shard_map.118
  3.4 2.2 %collective-permute-start = (bf16[256,256]{1,0:T(8,128)(2,1)S(1)}, bf16[256,256]{1,0:T(8,128)(2,1)S(1)}, u32[]{:S(2)}, u32[]{:S(2)}) collective-permute-start(bf16[256,256]{1,0:T(8,128)(2,1)S(1)} %get-tuple-element.19.refs_1_.r1.refs_0_.rows_ref), channel_id=1, source_target_pairs={{192,0},{0,64},{64,128},{128,192},{193,1},{1,65},{65,129},{129,193... | collective-permute-start | bytes 393224 | tf_op jit(solution)/shard_map/ppermute | solution.py:325
  5.6 1.5 %collective-permute-start.1 = (bf16[256,256]{1,0:T(8,128)(2,1)S(1)}, bf16[256,256]{1,0:T(8,128)(2,1)S(1)}, u32[]{:S(2)}, u32[]{:S(2)}) collective-permute-start(bf16[256,256]{1,0:T(8,128)(2,1)S(1)} %get-tuple-element.19.refs_1_.r1.refs_0_.rows_ref), channel_id=1, source_target_pairs={{64,0},{128,64},{192,128},{0,192},{65,1},{129,65},{193,129},{1,193... | collective-permute-start | bytes 393224 | tf_op jit(solution)/shard_map/ppermute | solution.py:325
  7.1 1.6 %collective-permute-start.7 = (bf16[256,256]{1,0:T(8,128)(2,1)S(1)}, bf16[256,256]{1,0:T(8,128)(2,1)S(1)}, u32[]{:S(2)}, u32[]{:S(2)}) collective-permute-start(bf16[256,256]{1,0:T(8,128)(2,1)S(1)} %get-tuple-element.19.refs_1_.r1.refs_0_.rows_ref), channel_id=1, source_target_pairs={{128,0},{192,64},{0,128},{64,192},{129,1},{193,65},{1,129},{65,193... | collective-permute-start | bytes 393224 | tf_op jit(solution)/shard_map/ppermute | solution.py:325
  8.7 0.4 collective-permute-start.2
  9.1 2.3 %collective-permute-start.3 = (f32[3,256]{1,0:T(4,128)S(1)}, f32[3,256]{1,0:T(4,128)S(1)}, u32[]{:S(2)}, u32[]{:S(2)}) collective-permute-start(f32[3,256]{1,0:T(4,128)S(1)} %get-tuple-element.20.refs_4_.p1.refs_0_), channel_id=1, source_target_pairs={{64,0},{128,64},{192,128},{0,192},{65,1},{129,65},{193,129},{1,193... | collective-permute-start | bytes 9224 | tf_op jit(solution)/shard_map/ppermute | solution.py:325
  11.3 1.4 %collective-permute-done.2.refs_3_.p0.refs_2_ = f32[3,256]{1,0:T(4,128)S(1)} collective-permute-done((f32[3,256]{1,0:T(4,128)S(1)}, f32[3,256]{1,0:T(4,128)S(1)}, u32[]{:S(2)}, u32[]{:S(2)}) %collective-permute-start.2) | collective-permute-done | bytes 3104 | tf_op jit(solution)/shard_map/ppermute | solution.py:325
  12.8 0.2 collective-permute-start.6
  13.0 0.2 collective-permute-done.3.refs_5_.p2.refs_1_
  13.2 3.5 %collective-permute-done.6.refs_3_ = f32[3,256]{1,0:T(4,128)S(1)} collective-permute-done((f32[3,256]{1,0:T(4,128)S(1)}, f32[3,256]{1,0:T(4,128)S(1)}, u32[]{:S(2)}, u32[]{:S(2)}) %collective-permute-start.6) | collective-permute-done | bytes 3104 | tf_op jit(solution)/shard_map/ppermute | solution.py:325
  16.7 3.8 %shard_map.123 = (bf16[1024,1024]{1,0:T(8,128)(2,1)S(1)}, bf16[1024,1024]{1,0:T(8,128)(2,1)S(1)}) custom-call(f32[3,256]{1,0:T(4,128)S(1)} %get-tuple-element.20.refs_4_.p1.refs_0_, f32[3,256]{1,0:T(4,128)S(1)} %collective-permute-done.3.refs_5_.p2.refs_1_, f32[3,256]{1,0:T(4,128)S(1)} %collective-permute-done.2.refs_3_.p0.refs_2_, ...), custom_call_target="tpu_custom_call" | custom-call | flops 20971520 | bytes 4194304 | tf_op jit(solution)/shard_map/pallas_call | solution.py:36
  20.6 0.0 collective-permute-done.refs_0_.r0.refs_2_
  20.6 0.0 collective-permute-done.1.refs_2_.r2.refs_1_
  20.6 0.0 collective-permute-done.7.refs_3_
  20.6 0.7 shard_map.124
  21.3 0.0 copy-start.3
  21.3 0.0 copy-start.8
  21.3 4.9 %collective-permute-start.8 = (bf16[512,256]{1,0:T(8,128)(2,1)S(1)}, bf16[512,256]{1,0:T(8,128)(2,1)S(1)}, u32[]{:S(2)}, u32[]{:S(2)}) collective-permute-start(bf16[512,256]{1,0:T(8,128)(2,1)S(1)} %get-tuple-element.28), channel_id=1, source_target_pairs={{0,1},{1,0},{2,3},{3,2},{4,5},{5,4},{6,7},{7,6},{8,9},{9,8},{10,11... | collective-permute-start | bytes 786440 | tf_op jit(solution)/shard_map/ppermute | solution.py:367
  26.2 1.2 %collective-permute-done.8.got_ref = bf16[512,256]{1,0:T(8,128)(2,1)S(1)} collective-permute-done((bf16[512,256]{1,0:T(8,128)(2,1)S(1)}, bf16[512,256]{1,0:T(8,128)(2,1)S(1)}, u32[]{:S(2)}, u32[]{:S(2)}) %collective-permute-start.8) | collective-permute-done | bytes 262176 | tf_op jit(solution)/shard_map/ppermute | solution.py:367
  27.4 0.4 shard_map.125
  27.8 0.0 copy-start.11
  27.8 0.0 copy-start.12
  27.9 0.0 copy-start.13
  27.9 19.6 %all_to_all.10.mine_ref = bf16[32,16,256]{2,1,0:T(8,128)(2,1)S(1)} all-to-all(bf16[32,16,256]{2,1,0:T(8,128)(2,1)S(1)} %bitcast.13), channel_id=1, replica_groups={{0,2,4,6,8,10,12,14,16,18,20,22,24,26,28,30,32,34,36,38,40,42,44,46,48,..., dimensions={0} | all-to-all | bytes 524288 | tf_op jit(solution)/shard_map/all_to_all | solution.py:376
  47.5 0.0 copy-done.3
  47.5 0.0 copy-done.8
  47.5 0.8 shard_map.126
  48.3 6.7 %all-to-all-start.1 = ((bf16[32,16,256]{2,1,0:T(8,128)(2,1)}), bf16[32,16,256]{2,1,0:T(8,128)(2,1)S(1)}, u32[]{:S(2)}, u32[]{:S(2)}) async-start(bf16[32,16,256]{2,1,0:T(8,128)(2,1)} %shard_map.126), calls=%async_computation.1 | async-start | bytes 524288 | tf_op jit(solution)/shard_map/all_to_all | solution.py:384
  55.1 0.1 shard_map.119
  55.1 2.9 %collective-permute-start.4 = (bf16[3,288,256]{2,1,0:T(8,128)(2,1)S(1)}, bf16[3,288,256]{2,1,0:T(8,128)(2,1)S(1)}, u32[]{:S(2)}, u32[]{:S(2)}) collective-permute-start(bf16[3,288,256]{2,1,0:T(8,128)(2,1)S(1)} %shard_map.119), channel_id=1, source_target_pairs={{63,0},{0,1},{1,2},{2,3},{3,4},{4,5},{5,6},{6,7},{7,8},{8,9},{9,10... | collective-permute-start | bytes 1327112 | tf_op jit(solution)/shard_map/ppermute | solution.py:328
  58.0 0.0 collective-permute-start.5
  58.0 8.1 %collective-permute-done.4.low_ref = bf16[3,288,256]{2,1,0:T(8,128)(2,1)S(1)} collective-permute-done((bf16[3,288,256]{2,1,0:T(8,128)(2,1)S(1)}, bf16[3,288,256]{2,1,0:T(8,128)(2,1)S(1)}, u32[]{:S(2)}, u32[]{:S(2)}) %collective-permute-start.4) | collective-permute-done | bytes 442400 | tf_op jit(solution)/shard_map/ppermute | solution.py:328
  66.1 1.9 %collective-permute-done.5.high_ref = bf16[3,288,256]{2,1,0:T(8,128)(2,1)S(1)} collective-permute-done((bf16[3,288,256]{2,1,0:T(8,128)(2,1)S(1)}, bf16[3,288,256]{2,1,0:T(8,128)(2,1)S(1)}, u32[]{:S(2)}, u32[]{:S(2)}) %collective-permute-start.5) | collective-permute-done | bytes 442400 | tf_op jit(solution)/shard_map/ppermute | solution.py:328
  68.0 0.0 copy-done
  68.0 0.0 copy-done.6
  68.0 0.0 copy-done.7
  68.0 1.4 %shard_map.120 = (bf16[2304,256]{1,0:T(8,128)(2,1)S(1)}, bf16[256,128]{1,0:T(8,128)(2,1)S(1)}) custom-call(bf16[256,256]{1,0:T(8,128)(2,1)S(1)} %collective-permute-done.refs_0_.r0.refs_2_, bf16[256,256]{1,0:T(8,128)(2,1)S(1)} %get-tuple-element.19.refs_1_.r1.refs_0_.rows_ref, bf16[256,256]{1,0:T(8,128)(2,1)S(1)} %collective-permute-done.1.refs_2_.r2.refs_1_, ...), custom_call_target="tpu_custom_call" | custom-call | flops 301989888 | bytes 4194304 | tf_op jit(solution)/shard_map/pallas_call | solution.py:36
  69.4 0.0 copy-start.9
  69.4 1.0 %copy-done.9 = bf16[2304,256]{1,0:T(8,128)(2,1)} copy-done((bf16[2304,256]{1,0:T(8,128)(2,1)}, bf16[2304,256]{1,0:T(8,128)(2,1)S(1)}, u32[]{:S(2)}) %copy-start.9) | copy-done | bytes 1179672
  70.5 0.0 all-to-all-done.1
  70.5 3.9 %collective-permute-start.9 = (bf16[512,256]{1,0:T(8,128)(2,1)S(1)}, bf16[512,256]{1,0:T(8,128)(2,1)S(1)}, u32[]{:S(2)}, u32[]{:S(2)}) collective-permute-start(bf16[512,256]{1,0:T(8,128)(2,1)S(1)} %bitcast.11), channel_id=1, source_target_pairs={{0,1},{1,0},{2,3},{3,2},{4,5},{5,4},{6,7},{7,6},{8,9},{9,8},{10,11... | collective-permute-start | bytes 786440 | tf_op jit(solution)/shard_map/ppermute | solution.py:387
  74.4 0.0 copy-done.11
  74.4 0.0 copy-done.12
  74.4 0.0 copy-done.13
  74.4 0.0 copy-start.10
  74.4 1.3 %copy-done.10 = bf16[2304,256]{1,0:T(8,128)(2,1)S(1)} copy-done((bf16[2304,256]{1,0:T(8,128)(2,1)S(1)}, bf16[2304,256]{1,0:T(8,128)(2,1)}, u32[]{:S(2)}) %copy-start.10) | copy-done | bytes 1179672
  75.7 7.5 %shard_map.121.sum_ref = f32[256,256]{1,0:T(8,128)S(1)} custom-call(bf16[256,128]{1,0:T(8,128)(2,1)S(1)} %get-tuple-element.21.cols_ref, bf16[2304,256]{1,0:T(8,128)(2,1)S(1)} %copy-done.10, bf16[64,256]{1,0:T(8,128)(2,1)S(1)} %copy-done.12, f32[1,256]{1,0:T(1,128)S(1)} %bitcast.19, bf16[256,256]{1,0:T(8,128)(2,1)S(1)} %copy-done.11, ...), custom_call_target="tpu_custom_call" | custom-call | flops 4831838208 | bytes 4194304 | tf_op jit(solution)/shard_map/pallas_call | solution.py:36
  83.2 0.0 collective-permute-done.9.other_ref
  83.2 0.7 shard_map.127
  83.9 0.1 collective-permute-start.10
  84.0 2.7 %collective-permute-start.11 = (bf16[256,256]{1,0:T(8,128)(2,1)S(1)}, bf16[256,256]{1,0:T(8,128)(2,1)S(1)}, u32[]{:S(2)}, u32[]{:S(2)}) collective-permute-start(bf16[256,256]{1,0:T(8,128)(2,1)S(1)} %get-tuple-element.31), channel_id=1, source_target_pairs={{64,0},{128,64},{192,128},{0,192},{65,1},{129,65},{193,129},{1,193... | collective-permute-start | bytes 393224 | tf_op jit(solution)/shard_map/ppermute | solution.py:325
  86.7 0.0 collective-permute-start.12
  86.7 7.5 %shard_map.122.short_ref = f32[256,256]{1,0:T(8,128)S(1)} custom-call(bf16[256,128]{1,0:T(8,128)(2,1)S(1)} %get-tuple-element.21.cols_ref, bf16[2304,256]{1,0:T(8,128)(2,1)S(1)} %copy-done.10, bf16[64,256]{1,0:T(8,128)(2,1)S(1)} %copy-done.12, f32[1,256]{1,0:T(1,128)S(1)} %bitcast.20, bf16[256,256]{1,0:T(8,128)(2,1)S(1)} %copy-done.11, ...), custom_call_target="tpu_custom_call" | custom-call | flops 4831838208 | bytes 4194304 | tf_op jit(solution)/shard_map/pallas_call | solution.py:36
  94.1 0.0 collective-permute-done.10.e1_ref
  94.1 0.0 collective-permute-done.11.e2_ref
  94.2 0.0 collective-permute-done.12.e3_ref
  94.2 0.0 copy-done.1
  94.2 0.9 shard_map.128
  (6 shorter events, 0.0 us)
Async XLA Ops:
  0.7 0.8 copy-start.2
  1.4 0.9 copy-start.4
  2.3 0.9 copy-start.5
  3.4 17.2 %collective-permute-start = (bf16[256,256]{1,0:T(8,128)(2,1)S(1)}, bf16[256,256]{1,0:T(8,128)(2,1)S(1)}, u32[]{:S(2)}, u32[]{:S(2)}) collective-permute-start(bf16[256,256]{1,0:T(8,128)(2,1)S(1)} %get-tuple-element.19.refs_1_.r1.refs_0_.rows_ref), channel_id=1, source_target_pairs={{192,0},{0,64},{64,128},{128,192},{193,1},{1,65},{65,129},{129,193... | collective-permute-start | bytes 393224 | tf_op jit(solution)/shard_map/ppermute | solution.py:325
  5.6 15.0 %collective-permute-start.1 = (bf16[256,256]{1,0:T(8,128)(2,1)S(1)}, bf16[256,256]{1,0:T(8,128)(2,1)S(1)}, u32[]{:S(2)}, u32[]{:S(2)}) collective-permute-start(bf16[256,256]{1,0:T(8,128)(2,1)S(1)} %get-tuple-element.19.refs_1_.r1.refs_0_.rows_ref), channel_id=1, source_target_pairs={{64,0},{128,64},{192,128},{0,192},{65,1},{129,65},{193,129},{1,193... | collective-permute-start | bytes 393224 | tf_op jit(solution)/shard_map/ppermute | solution.py:325
  7.1 13.5 %collective-permute-start.7 = (bf16[256,256]{1,0:T(8,128)(2,1)S(1)}, bf16[256,256]{1,0:T(8,128)(2,1)S(1)}, u32[]{:S(2)}, u32[]{:S(2)}) collective-permute-start(bf16[256,256]{1,0:T(8,128)(2,1)S(1)} %get-tuple-element.19.refs_1_.r1.refs_0_.rows_ref), channel_id=1, source_target_pairs={{128,0},{192,64},{0,128},{64,192},{129,1},{193,65},{1,129},{65,193... | collective-permute-start | bytes 393224 | tf_op jit(solution)/shard_map/ppermute | solution.py:325
  8.7 4.1 %collective-permute-start.2 = (f32[3,256]{1,0:T(4,128)S(1)}, f32[3,256]{1,0:T(4,128)S(1)}, u32[]{:S(2)}, u32[]{:S(2)}) collective-permute-start(f32[3,256]{1,0:T(4,128)S(1)} %get-tuple-element.20.refs_4_.p1.refs_0_), channel_id=1, source_target_pairs={{192,0},{0,64},{64,128},{128,192},{193,1},{1,65},{65,129},{129,193... | collective-permute-start | bytes 9224 | tf_op jit(solution)/shard_map/ppermute | solution.py:325
  9.1 4.1 %collective-permute-start.3 = (f32[3,256]{1,0:T(4,128)S(1)}, f32[3,256]{1,0:T(4,128)S(1)}, u32[]{:S(2)}, u32[]{:S(2)}) collective-permute-start(f32[3,256]{1,0:T(4,128)S(1)} %get-tuple-element.20.refs_4_.p1.refs_0_), channel_id=1, source_target_pairs={{64,0},{128,64},{192,128},{0,192},{65,1},{129,65},{193,129},{1,193... | collective-permute-start | bytes 9224 | tf_op jit(solution)/shard_map/ppermute | solution.py:325
  12.8 4.0 %collective-permute-start.6 = (f32[3,256]{1,0:T(4,128)S(1)}, f32[3,256]{1,0:T(4,128)S(1)}, u32[]{:S(2)}, u32[]{:S(2)}) collective-permute-start(f32[3,256]{1,0:T(4,128)S(1)} %get-tuple-element.20.refs_4_.p1.refs_0_), channel_id=1, source_target_pairs={{128,0},{192,64},{0,128},{64,192},{129,1},{193,65},{1,129},{65,193... | collective-permute-start | bytes 9224 | tf_op jit(solution)/shard_map/ppermute | solution.py:325
  21.3 26.2 %copy-start.3 = (s32[3,2048]{1,0:T(4,128)S(1)}, s32[3,2048]{1,0:T(4,128)}, u32[]{:S(2)}) copy-start(s32[3,2048]{1,0:T(4,128)} %wave_ref.3) | copy-start | bytes 73732
  21.3 26.2 %copy-start.8 = (f32[256]{0:T(256)S(1)}, f32[256]{0:T(256)}, u32[]{:S(2)}) copy-start(f32[256]{0:T(256)} %param.17) | copy-start | bytes 3076
  21.3 6.1 %collective-permute-start.8 = (bf16[512,256]{1,0:T(8,128)(2,1)S(1)}, bf16[512,256]{1,0:T(8,128)(2,1)S(1)}, u32[]{:S(2)}, u32[]{:S(2)}) collective-permute-start(bf16[512,256]{1,0:T(8,128)(2,1)S(1)} %get-tuple-element.28), channel_id=1, source_target_pairs={{0,1},{1,0},{2,3},{3,2},{4,5},{5,4},{6,7},{7,6},{8,9},{9,8},{10,11... | collective-permute-start | bytes 786440 | tf_op jit(solution)/shard_map/ppermute | solution.py:367
  27.4 40.6 %copy-start = (bf16[256,256]{1,0:T(8,128)(2,1)S(1)}, bf16[256,256]{1,0:T(8,128)(2,1)}, u32[]{:S(2)}) copy-start(bf16[256,256]{1,0:T(8,128)(2,1)} %win_ref.1) | copy-start | bytes 393220
  27.4 40.6 %copy-start.6 = (s32[1,1,32,256]{3,2,1,0:T(8,128)S(1)}, s32[1,1,32,256]{3,2,1,0:T(8,128)}, u32[]{:S(2)}) copy-start(s32[1,1,32,256]{3,2,1,0:T(8,128)} %param.14) | copy-start | bytes 98308
  27.4 40.6 %copy-start.7 = (s32[1,1,32,256]{3,2,1,0:T(8,128)S(1)}, s32[1,1,32,256]{3,2,1,0:T(8,128)}, u32[]{:S(2)}) copy-start(s32[1,1,32,256]{3,2,1,0:T(8,128)} %param.15) | copy-start | bytes 98308
  27.8 46.6 %copy-start.11 = (bf16[256,256]{1,0:T(8,128)(2,1)S(1)}, bf16[256,256]{1,0:T(8,128)(2,1)}, u32[]{:S(2)}) copy-start(bf16[256,256]{1,0:T(8,128)(2,1)} %wf_ref.3) | copy-start | bytes 393220
  27.8 46.6 %copy-start.12 = (bf16[64,256]{1,0:T(8,128)(2,1)S(1)}, bf16[64,256]{1,0:T(8,128)(2,1)}, u32[]{:S(2)}) copy-start(bf16[64,256]{1,0:T(8,128)(2,1)} %wrbf_ref.3) | copy-start | bytes 98308
  27.9 46.6 %copy-start.13 = (f32[256]{0:T(256)S(1)}, f32[256]{0:T(256)}, u32[]{:S(2)}) copy-start(f32[256]{0:T(256)} %param.21) | copy-start | bytes 3076
  48.3 22.1 %all-to-all-start.1 = ((bf16[32,16,256]{2,1,0:T(8,128)(2,1)}), bf16[32,16,256]{2,1,0:T(8,128)(2,1)S(1)}, u32[]{:S(2)}, u32[]{:S(2)}) async-start(bf16[32,16,256]{2,1,0:T(8,128)(2,1)} %shard_map.126), calls=%async_computation.1 | async-start | bytes 524288 | tf_op jit(solution)/shard_map/all_to_all | solution.py:384
  55.1 11.0 %collective-permute-start.4 = (bf16[3,288,256]{2,1,0:T(8,128)(2,1)S(1)}, bf16[3,288,256]{2,1,0:T(8,128)(2,1)S(1)}, u32[]{:S(2)}, u32[]{:S(2)}) collective-permute-start(bf16[3,288,256]{2,1,0:T(8,128)(2,1)S(1)} %shard_map.119), channel_id=1, source_target_pairs={{63,0},{0,1},{1,2},{2,3},{3,4},{4,5},{5,6},{6,7},{7,8},{8,9},{9,10... | collective-permute-start | bytes 1327112 | tf_op jit(solution)/shard_map/ppermute | solution.py:328
  58.0 10.0 %collective-permute-start.5 = (bf16[3,288,256]{2,1,0:T(8,128)(2,1)S(1)}, bf16[3,288,256]{2,1,0:T(8,128)(2,1)S(1)}, u32[]{:S(2)}, u32[]{:S(2)}) collective-permute-start(bf16[3,288,256]{2,1,0:T(8,128)(2,1)S(1)} %shard_map.119), channel_id=1, source_target_pairs={{1,0},{2,1},{3,2},{4,3},{5,4},{6,5},{7,6},{8,7},{9,8},{10,9},{11,1... | collective-permute-start | bytes 1327112 | tf_op jit(solution)/shard_map/ppermute | solution.py:328
  69.4 1.0 %copy-start.9 = (bf16[2304,256]{1,0:T(8,128)(2,1)}, bf16[2304,256]{1,0:T(8,128)(2,1)S(1)}, u32[]{:S(2)}) copy-start(bf16[2304,256]{1,0:T(8,128)(2,1)S(1)} %get-tuple-element.22.hidden) | copy-start | bytes 3538948
  70.5 12.7 %collective-permute-start.9 = (bf16[512,256]{1,0:T(8,128)(2,1)S(1)}, bf16[512,256]{1,0:T(8,128)(2,1)S(1)}, u32[]{:S(2)}, u32[]{:S(2)}) collective-permute-start(bf16[512,256]{1,0:T(8,128)(2,1)S(1)} %bitcast.11), channel_id=1, source_target_pairs={{0,1},{1,0},{2,3},{3,2},{4,5},{5,4},{6,7},{7,6},{8,9},{9,8},{10,11... | collective-permute-start | bytes 786440 | tf_op jit(solution)/shard_map/ppermute | solution.py:387
  74.4 1.3 %copy-start.10 = (bf16[2304,256]{1,0:T(8,128)(2,1)S(1)}, bf16[2304,256]{1,0:T(8,128)(2,1)}, u32[]{:S(2)}) copy-start(bf16[2304,256]{1,0:T(8,128)(2,1)} %copy-done.9) | copy-start | bytes 3538948
  83.9 10.2 %collective-permute-start.10 = (bf16[256,256]{1,0:T(8,128)(2,1)S(1)}, bf16[256,256]{1,0:T(8,128)(2,1)S(1)}, u32[]{:S(2)}, u32[]{:S(2)}) collective-permute-start(bf16[256,256]{1,0:T(8,128)(2,1)S(1)} %get-tuple-element.30), channel_id=1, source_target_pairs={{192,0},{0,64},{64,128},{128,192},{193,1},{1,65},{65,129},{129,193... | collective-permute-start | bytes 393224 | tf_op jit(solution)/shard_map/ppermute | solution.py:325
  84.0 10.2 %collective-permute-start.11 = (bf16[256,256]{1,0:T(8,128)(2,1)S(1)}, bf16[256,256]{1,0:T(8,128)(2,1)S(1)}, u32[]{:S(2)}, u32[]{:S(2)}) collective-permute-start(bf16[256,256]{1,0:T(8,128)(2,1)S(1)} %get-tuple-element.31), channel_id=1, source_target_pairs={{64,0},{128,64},{192,128},{0,192},{65,1},{129,65},{193,129},{1,193... | collective-permute-start | bytes 393224 | tf_op jit(solution)/shard_map/ppermute | solution.py:325
  86.6 7.5 %copy-start.1 = (bf16[256,256]{1,0:T(8,128)(2,1)S(1)}, bf16[256,256]{1,0:T(8,128)(2,1)}, u32[]{:S(2)}) copy-start(bf16[256,256]{1,0:T(8,128)(2,1)} %wout_ref.1) | copy-start | bytes 393220
  86.7 7.5 %collective-permute-start.12 = (bf16[256,256]{1,0:T(8,128)(2,1)S(1)}, bf16[256,256]{1,0:T(8,128)(2,1)S(1)}, u32[]{:S(2)}, u32[]{:S(2)}) collective-permute-start(bf16[256,256]{1,0:T(8,128)(2,1)S(1)} %get-tuple-element.32), channel_id=1, source_target_pairs={{128,0},{192,64},{0,128},{64,192},{129,1},{193,65},{1,129},{65,193... | collective-permute-start | bytes 393224 | tf_op jit(solution)/shard_map/ppermute | solution.py:325

commit v4 on v3

--- a/solution.py
+++ b/solution.py
@@ -29,17 +29,18 @@
 )
 ZOOM = 16.0 * math.sqrt(math.log2(math.e))
 VMEM = pl.BlockSpec(memory_space=pltpu.VMEM)
-
-
-def call(body, out, ins, scratch=(), flops=0, nbytes=0, trans=0, grant=16):
+HBM = pl.BlockSpec(memory_space=pltpu.HBM)
+
+
+def call(body, out, ins, scratch=(), flops=0, nbytes=0, trans=0, grant=16, spec=VMEM):
     multiple = isinstance(out, (list, tuple))
     return pl.pallas_call(
         body,
         out_shape=out,
-        in_specs=[VMEM] * len(ins),
+        in_specs=[spec] * len(ins),
         out_specs=[VMEM] * len(out) if multiple else VMEM,
         scratch_shapes=list(scratch),
-        compiler_params=pltpu.CompilerParams(vmem_limit_bytes=grant << 20),
+        compiler_params=pltpu.CompilerParams(vmem_limit_bytes=int(grant * (1 << 20))),
         cost_estimate=pl.CostEstimate(flops=flops, bytes_accessed=nbytes, transcendentals=trans),
     )(*ins)
 
@@ -61,23 +62,29 @@
     return 2.0 * (half * even), 1.0 - 2.0 * (half * half)
 
 
-def begin_kernel(wave_ref, rows_ref, place_ref, wq_ref, cols, rows_out, place_out, wq_out, flat):
+def begin_kernel(wave_hbm, place_hbm, cols, place_out, waves, place, flat, sems):
     share = cols.shape[0]
-    role = lax.axis_index("role")
+    first = pl.multiple_of(lax.axis_index("role") * share, 128)
+    copies = [
+        pltpu.make_async_copy(wave_hbm.at[:, pl.ds(first, share)], waves, sems.at[0]),
+        pltpu.make_async_copy(place_hbm, place, sems.at[1]),
+    ]
+    for copy in copies:
+        copy.start()
     flat[...] = jnp.zeros_like(flat)
+    copies[0].wait()
     for i in range(share // 128):
-        first = pl.multiple_of(role * share + i * 128, 128)
-        waves = wave_ref[:, pl.ds(first, 128)].astype(jnp.float32)
+        part = waves[:, i * 128 : (i + 1) * 128].astype(jnp.float32)
         for k in range(3):
-            flat[3 * k : 3 * k + 3, :] = waves
+            flat[3 * k : 3 * k + 3, :] = part
         cols[i * 128 : (i + 1) * 128, :] = flat[...].T.astype(jnp.bfloat16)
-    rows_out[...] = rows_ref[...]
-    place_out[...] = place_ref[...]
-    wq_out[...] = wq_ref[...]
+    copies[1].wait()
+    for c in range(3):
+        place_out[c : c + 1, :] = place[c]
 
 
 def tables_kernel(*refs):
-    pos_refs, (cols, by_wave, by_atom, pos, parts) = refs[:4], refs[4:]
+    pos_refs, (cols, by_wave, pos, parts) = refs[:4], refs[4:]
     atoms = pos_refs[0].shape[1]
     total = pos.shape[1]
     pos[...] = jnp.zeros_like(pos)
@@ -99,10 +106,15 @@
         ).reshape(2 * step, total)
         part = pl.ds(pl.multiple_of(j * 2 * step, 2 * step), 2 * step)
         by_wave[part, :] = both.astype(jnp.bfloat16)
-        by_atom[:, part] = both.T.astype(jnp.bfloat16)
         return carry
 
     lax.fori_loop(0, share // step, block, 0)
+
+
+def flip_kernel(by_wave, by_atom):
+    for j in range(by_wave.shape[0] // 128):
+        part = slice(j * 128, (j + 1) * 128)
+        by_atom[:, part] = by_wave[part, :].T
 
 
 def core_half(size, other):
@@ -121,10 +133,13 @@
     out_ref[...] = (dot(table[part, :], queries[...]) * scale).astype(jnp.bfloat16)
 
 
-def keep_kernel(scale, queries, table, got_ref, out_ref):
+def own_kernel(scale, queries, table, out_ref):
     part = core_half(out_ref.shape[0], False)
-    own = dot(table[part, :], queries[...]) * scale
-    out_ref[...] = (own + got_ref[...].astype(jnp.float32)).astype(jnp.bfloat16)
+    out_ref[...] = dot(table[part, :], queries[...]) * scale
+
+
+def keep_kernel(own_ref, got_ref, out_ref):
+    out_ref[...] = (own_ref[...] + got_ref[...].astype(jnp.float32)).astype(jnp.bfloat16)
 
 
 def stack_kernel(*refs):
@@ -178,8 +193,16 @@
 
 
 def prepare_kernel(
-    r0, r1, r2, low_ref, high_ref, p0, p1, p2, slots_ref, images_ref, win_ref, hidden, cols, pos, turned
+    r0, r1, r2, low_ref, high_ref, p0, p1, p2, slots_ref, images_ref, win_ref, wrbf_ref, brbf_ref, wf_ref,
+    hidden, cols, pairs, bias, wf_out, pos, turned,
 ):
+    basis_count, width = wrbf_ref.shape
+    pairs[...] = jnp.zeros_like(pairs)
+    pairs[0:basis_count, 0:width] = wrbf_ref[...]
+    pairs[basis_count:, width:] = wrbf_ref[...]
+    bias[:, 0:width] = brbf_ref[...] * math.log2(math.e)
+    bias[:, width:] = brbf_ref[...] * math.log2(math.e)
+    wf_out[...] = wf_ref[...]
     slots, atoms = slots_ref.shape
     weight = win_ref[...]
     own = (r0, r1, r2)
@@ -226,15 +249,13 @@
     cols[...] = turned[...].T.astype(jnp.bfloat16)
 
 
-def short_kernel(first, count, scale, cols_ref, hidden, wrbf_ref, brbf_ref, wf_ref, sum_ref, out_ref, pairs):
+def short_kernel(first, count, scale, cols_ref, hidden, pairs, bias, wf_ref, *refs):
     lane = 128
     atoms = cols_ref.shape[0]
     slots = cols_ref.shape[1] // 4
-    basis_count, width = wrbf_ref.shape
-    pairs[...] = jnp.zeros_like(pairs)
-    pairs[0:basis_count, 0:width] = wrbf_ref[...]
-    pairs[basis_count:, width:] = wrbf_ref[...]
-    out_ref[...] = sum_ref[...]
+    basis_count, width = pairs.shape[0] // 2, wf_ref.shape[1]
+    out_ref = refs[-1]
+    out_ref[...] = refs[0][...] if len(refs) > 1 else jnp.zeros_like(out_ref)
     row = lax.broadcasted_iota(jnp.int32, (lane, 6 * lane), 0)
     column = lax.broadcasted_iota(jnp.int32, (lane, 6 * lane), 1)
     code_slot = jnp.where(row >= 3 * slots, row - 3 * slots - (column >> 7), -lane)
@@ -246,8 +267,6 @@
         * ZOOM
     )
     lanes = lax.broadcasted_iota(jnp.int32, (16, lane), 1) + lane
-    bias = brbf_ref[...] * math.log2(math.e)
-    bias = jnp.concatenate([bias, bias], axis=1)
     groups = 9 * atoms // lane
 
     def spread(j):
@@ -273,7 +292,7 @@
         for p in range(2):
             offset = wide[:, (4 + p) * lane : (5 + p) * lane] - centers
             basis = jnp.exp2(-(offset * offset)).astype(jnp.bfloat16)
-            value = dot(basis, pairs[...]) * math.log2(math.e) + bias
+            value = dot(basis, pairs[...]) * math.log2(math.e) + bias[...]
             both = (jnp.log(1.0 + jnp.exp2(value)) - math.log(2.0)).astype(jnp.bfloat16)
             inner += [both[:, :width], both[:, width:]]
         return dot(jnp.concatenate(inner, axis=0), wf_ref[...])
@@ -311,7 +330,6 @@
 ):
     f32, bf16 = jnp.float32, jnp.bfloat16
     rows = features[0, 0]
-    place = positions[0, 0]
     atoms, width = rows.shape
     slots = neighbours.shape[2]
     roles = lax.axis_size("role")
@@ -331,24 +349,25 @@
 
     shifts = (1, roles - 1, 2)
     order = (0,) + shifts
-    wave_cols, rows, place, near_query = call(
+    wave_cols, place = call(
         begin_kernel,
-        [
-            jax.ShapeDtypeStruct((share, 128), bf16),
-            jax.ShapeDtypeStruct((atoms, width), bf16),
-            jax.ShapeDtypeStruct((3, atoms), f32),
-            jax.ShapeDtypeStruct((width, width), bf16),
+        [jax.ShapeDtypeStruct((share, 128), bf16), jax.ShapeDtypeStruct((3, atoms), f32)],
+        [wave, jnp.transpose(positions, (0, 2, 1, 3))[0]],
+        scratch=[
+            pltpu.VMEM((3, share), jnp.int32),
+            pltpu.VMEM((3, 1, atoms), f32),
+            pltpu.VMEM((128, 128), f32),
+            pltpu.SemaphoreType.DMA((2,)),
         ],
-        [wave, rows, place, w_query],
-        scratch=[pltpu.VMEM((128, 128), f32)],
         nbytes=1 << 19,
+        grant=63.25,
+        spec=HBM,
     )
     place_of = {0: place, **{d: from_role(place, d) for d in shifts}}
     rows_of = {0: rows, **{d: from_role(rows, d) for d in shifts}}
-    by_wave, by_atom = call(
+    by_wave = call(
         tables_kernel,
-        [jax.ShapeDtypeStruct((2 * share, roles * atoms), bf16)]
-        + [jax.ShapeDtypeStruct((roles * atoms, 2 * share), bf16)],
+        jax.ShapeDtypeStruct((2 * share, roles * atoms), bf16),
         [place_of[d] for d in order] + [wave_cols],
         scratch=[pltpu.VMEM((128, roles * atoms), f32), pltpu.VMEM((128, roles * atoms), bf16)],
         flops=40 * share * roles * atoms,
@@ -360,17 +379,30 @@
     sent, queries = call(
         functools.partial(send_kernel, norm),
         [jax.ShapeDtypeStruct((share, width), bf16), jax.ShapeDtypeStruct((roles * atoms, width), bf16)],
-        [rows_of[d] for d in order] + [near_query, by_wave],
+        [rows_of[d] for d in order] + [w_query, by_wave],
         flops=2 * share * roles * atoms * width,
         nbytes=3 << 20,
     )
     got = lax.ppermute(sent, "atoms", partner)
-    kept = call(
-        functools.partial(keep_kernel, norm),
-        jax.ShapeDtypeStruct((share, width), bf16),
-        [queries, by_wave, got],
+    own = call(
+        functools.partial(own_kernel, norm),
+        jax.ShapeDtypeStruct((share, width), f32),
+        [queries, by_wave],
         flops=2 * share * roles * atoms * width,
         nbytes=2 << 20,
+    )
+    kept = call(
+        keep_kernel,
+        jax.ShapeDtypeStruct((share, width), bf16),
+        [own, got],
+        flops=share * width,
+        nbytes=1 << 20,
+    )
+    by_atom = call(
+        flip_kernel,
+        jax.ShapeDtypeStruct((roles * atoms, 2 * share), bf16),
+        [by_wave],
+        nbytes=4 << 20,
     )
     chunks = (columns // 2, 2 * piece, width)
     mine = lax.all_to_all(kept.reshape(chunks), "atoms", 0, 0, axis_index_groups=same_core)
@@ -395,31 +427,39 @@
         nbytes=1 << 20,
     )
     low, high = from_column(bundle, columns - 1), from_column(bundle, 1)
-    hidden, cols = call(
+    hidden, cols, pairs, bias, filter_weight = call(
         prepare_kernel,
-        [jax.ShapeDtypeStruct((9 * atoms, width), bf16), jax.ShapeDtypeStruct((atoms, 4 * slots), bf16)],
+        [
+            jax.ShapeDtypeStruct((9 * atoms, width), bf16),
+            jax.ShapeDtypeStruct((atoms, 4 * slots), bf16),
+            jax.ShapeDtypeStruct((2 * w_rbf.shape[0], 2 * width), bf16),
+            jax.ShapeDtypeStruct((1, 2 * width), f32),
+            jax.ShapeDtypeStruct((width, width), bf16),
+        ],
         [rows_of[d] for d in triple]
         + [low, high]
         + [place_of[d] for d in triple]
-        + [neighbours[0, 0], images[0, 0], w_in],
+        + [neighbours[0, 0], images[0, 0], w_in, w_rbf, b_rbf[None, :], w_filter],
         scratch=[pltpu.VMEM((8, 9 * atoms), f32), pltpu.VMEM((4 * slots, atoms), f32)],
         flops=2 * 9 * atoms * width * width,
         nbytes=4 << 20,
-    )
-    short = jnp.zeros((atoms, width), f32)
-    quads = slots // 4
-    for half in range(2):
-        short = call(
-            functools.partial(
-                short_kernel, half * quads // 2, quads // 2, slots ** (-0.5) if half else 1.0
+        grant=63.25,
+    )
+    short = ()
+    ends = (0, 2, 6, slots // 4)
+    for i in range(3):
+        count = ends[i + 1] - ends[i]
+        short = (
+            call(
+                functools.partial(short_kernel, ends[i], count, 1.0 if i < 2 else slots ** (-0.5)),
+                jax.ShapeDtypeStruct((atoms, width), f32),
+                [cols, hidden, pairs, bias, filter_weight, *short],
+                flops=2 * 4 * count * atoms * 9 * atoms * width,
+                nbytes=4 << 20,
+                grant=63.25 if i < 2 else 16,
             ),
-            jax.ShapeDtypeStruct((atoms, width), f32),
-            [cols, hidden, w_rbf, b_rbf[None, :], w_filter, short],
-            scratch=[pltpu.VMEM((128, 2 * width), bf16)],
-            grant=32,
-            flops=slots * atoms * 9 * atoms * width,
-            nbytes=4 << 20,
         )
+    short = short[0]
     parts = call(
         ewald_kernel,
         [jax.ShapeDtypeStruct((atoms, width), bf16)] * roles,

time: 95.4 us -> 90.1 us (0.944)
  the two profiles are of different devices: /device:TPU:1 before, /device:TPU:24 now
where the time goes in v4:
time: 90.1 us; the launch traced here: 89.1 us
  starting transfers between devices  32.9 us (37%)
  Pallas kernels  32.5 us (36%)
  waiting for transfers between devices  18.9 us (21%)
  local copies, waits for them, and re-layouts  4.59 us (5%)
    pallas_call x14, Pallas kernels, call(): pl.pallas_call(body, out_shape=out, in_specs=[spec] * len(ins), out_specs...  32.5 us
    ppermute x9, starting transfers between devices, from_role(): lax.ppermute(block, 'role', [((i + shift) % roles, i) for i in range(role...  13 us
    all_to_all x1, starting transfers between devices, block(): lax.all_to_all(kept.reshape(chunks), 'atoms', 0, 0, axis_index_groups=sam...  10.6 us
    ppermute x9, waiting for transfers between devices, from_role(): lax.ppermute(block, 'role', [((i + shift) % roles, i) for i in range(role...  9.51 us
    all_to_all x1, waiting for transfers between devices, block(): lax.all_to_all(kept.reshape(chunks), 'atoms', 0, 0, axis_index_groups=sam...  8.37 us
    ppermute x2, starting transfers between devices, from_column(): lax.ppermute(block, 'atoms', [((i + shift) % columns, i) for i in range(c...  5.13 us
    unnamed x42, local copies, waits for them, and re-layouts  4.59 us
    all_to_all x1, starting transfers between devices, block(): lax.all_to_all(copies, 'atoms', 0, 0, axis_index_groups=same_core)  4.05 us
  transfers between devices with their start and end apart: 15, of which 6 were waited for; matrix products, arithmetic and copies ran while one was open for 0% of the time, Pallas kernels for 33%

profile of v4, /device:TPU:24, one launch (start us, length us, event | category | flops | bytes accessed | tf_op | source)
XLA Modules:
  0.0 89.1 jit_solution(12872546596061407367)
XLA Ops:
  0.0 1.9 %collective-permute-start = (bf16[256,256]{1,0:T(8,128)(2,1)}, bf16[256,256]{1,0:T(8,128)(2,1)S(1)}, u32[]{:S(2)}, u32[]{:S(2)}) collective-permute-start(bf16[256,256]{1,0:T(8,128)(2,1)} %bitcast.9), channel_id=1, source_target_pairs={{192,0},{0,64},{64,128},{128,192},{193,1},{1,65},{65,129},{129,193... | collective-permute-start | bytes 393224 | tf_op jit(solution)/shard_map/ppermute | solution.py:343
  1.9 0.1 collective-permute-start.1
  2.0 1.4 %collective-permute-start.7 = (bf16[256,256]{1,0:T(8,128)(2,1)}, bf16[256,256]{1,0:T(8,128)(2,1)S(1)}, u32[]{:S(2)}, u32[]{:S(2)}) collective-permute-start(bf16[256,256]{1,0:T(8,128)(2,1)} %bitcast.11), channel_id=1, source_target_pairs={{128,0},{192,64},{0,128},{64,192},{129,1},{193,65},{1,129},{65,193... | collective-permute-start | bytes 393224 | tf_op jit(solution)/shard_map/ppermute | solution.py:343
  3.4 1.5 %shard_map.118 = (bf16[512,128]{1,0:T(8,128)(2,1)}, f32[3,256]{1,0:T(4,128)}) custom-call(s32[3,2048]{1,0:T(4,128)} %wave_ref.1, f32[3,1,256]{2,1,0:T(1,128)} %bitcast.21), custom_call_target="tpu_custom_call" | custom-call | bytes 524288 | tf_op jit(solution)/shard_map/pallas_call | solution.py:37
  4.9 2.1 %collective-permute-start.2 = (f32[3,256]{1,0:T(4,128)}, f32[3,256]{1,0:T(4,128)S(1)}, u32[]{:S(2)}, u32[]{:S(2)}) collective-permute-start(f32[3,256]{1,0:T(4,128)} %get-tuple-element.18.refs_4_.p1.refs_0_), channel_id=1, source_target_pairs={{192,0},{0,64},{64,128},{128,192},{193,1},{1,65},{65,129},{129,193... | collective-permute-start | bytes 9224 | tf_op jit(solution)/shard_map/ppermute | solution.py:343
  7.0 0.7 collective-permute-start.3
  7.7 1.7 %collective-permute-done.2.refs_3_.p0.refs_2_ = f32[3,256]{1,0:T(4,128)S(1)} collective-permute-done((f32[3,256]{1,0:T(4,128)}, f32[3,256]{1,0:T(4,128)S(1)}, u32[]{:S(2)}, u32[]{:S(2)}) %collective-permute-start.2) | collective-permute-done | bytes 3104 | tf_op jit(solution)/shard_map/ppermute | solution.py:343
  9.4 1.8 %collective-permute-start.6 = (f32[3,256]{1,0:T(4,128)}, f32[3,256]{1,0:T(4,128)S(1)}, u32[]{:S(2)}, u32[]{:S(2)}) collective-permute-start(f32[3,256]{1,0:T(4,128)} %get-tuple-element.18.refs_4_.p1.refs_0_), channel_id=1, source_target_pairs={{128,0},{192,64},{0,128},{64,192},{129,1},{193,65},{1,129},{65,193... | collective-permute-start | bytes 9224 | tf_op jit(solution)/shard_map/ppermute | solution.py:343
  11.2 0.8 collective-permute-done.3.refs_5_.p2.refs_1_
  12.1 2.7 %collective-permute-done.6.refs_3_ = f32[3,256]{1,0:T(4,128)S(1)} collective-permute-done((f32[3,256]{1,0:T(4,128)}, f32[3,256]{1,0:T(4,128)S(1)}, u32[]{:S(2)}, u32[]{:S(2)}) %collective-permute-start.6) | collective-permute-done | bytes 3104 | tf_op jit(solution)/shard_map/ppermute | solution.py:343
  14.7 0.9 %copy-done.7 = bf16[512,128]{1,0:T(8,128)(2,1)S(1)} copy-done((bf16[512,128]{1,0:T(8,128)(2,1)S(1)}, bf16[512,128]{1,0:T(8,128)(2,1)}, u32[]{:S(2)}) %copy-start.7) | copy-done | bytes 131096
  15.6 0.7 copy-done.10
  16.3 3.0 %shard_map.124.by_wave.refs_5_.table = bf16[1024,1024]{1,0:T(8,128)(2,1)S(1)} custom-call(f32[3,256]{1,0:T(4,128)S(1)} %copy-done.10, f32[3,256]{1,0:T(4,128)S(1)} %collective-permute-done.3.refs_5_.p2.refs_1_, f32[3,256]{1,0:T(4,128)S(1)} %collective-permute-done.2.refs_3_.p0.refs_2_, f32[3,256]{1,0:T(4,128)S(1)} %collective-permute-done.6.refs_3_, ...), custom_call_target="tpu_custom_call" | custom-call | flops 20971520 | bytes 4194304 | tf_op jit(solution)/shard_map/pallas_call | solution.py:37
  19.3 0.0 collective-permute-done.refs_0_.r0.refs_2_
  19.3 0.0 copy-start.4
  19.4 0.0 collective-permute-done.1.refs_2_.r2.refs_1_
  19.4 0.0 copy-start.5
  19.4 0.0 collective-permute-done.7.refs_3_
  19.4 0.0 copy-done.2
  19.4 0.0 copy-done.9
  19.4 0.7 shard_map.126
  20.1 0.1 collective-permute-start.8
  20.2 0.0 copy-start.11
  20.2 0.0 copy-start.8
  20.2 0.0 copy-start.14
  20.2 0.4 shard_map.127.own_ref
  20.7 1.0 %collective-permute-done.8.got_ref = bf16[512,256]{1,0:T(8,128)(2,1)S(1)} collective-permute-done((bf16[512,256]{1,0:T(8,128)(2,1)S(1)}, bf16[512,256]{1,0:T(8,128)(2,1)S(1)}, u32[]{:S(2)}, u32[]{:S(2)}) %collective-permute-start.8) | collective-permute-done | bytes 262176 | tf_op jit(solution)/shard_map/ppermute | solution.py:386
  21.7 0.8 shard_map.128
  22.5 10.6 %all-to-all-start = ((bf16[32,16,256]{2,1,0:T(8,128)(2,1)}), bf16[32,16,256]{2,1,0:T(8,128)(2,1)S(1)}, u32[]{:S(2)}, u32[]{:S(2)}) async-start(bf16[32,16,256]{2,1,0:T(8,128)(2,1)} %bitcast.5), calls=%async_computation | async-start | bytes 524288 | tf_op jit(solution)/shard_map/all_to_all | solution.py:408
  33.1 0.0 copy-done.12
  33.1 0.0 copy-done.13
  33.1 0.0 copy-done.4
  33.1 0.0 copy-done.5
  33.1 0.0 copy-done.11
  33.1 0.1 shard_map.119
  33.2 0.1 collective-permute-start.4
  33.3 5.1 %collective-permute-start.5 = (bf16[3,288,256]{2,1,0:T(8,128)(2,1)S(1)}, bf16[3,288,256]{2,1,0:T(8,128)(2,1)}, u32[]{:S(2)}, u32[]{:S(2)}) collective-permute-start(bf16[3,288,256]{2,1,0:T(8,128)(2,1)S(1)} %shard_map.119), channel_id=1, source_target_pairs={{1,0},{2,1},{3,2},{4,3},{5,4},{6,5},{7,6},{8,7},{9,8},{10,9},{11,1... | collective-permute-start | bytes 1327112 | tf_op jit(solution)/shard_map/ppermute | solution.py:346
  38.3 8.4 %all-to-all-done.mine_ref = bf16[32,16,256]{2,1,0:T(8,128)(2,1)S(1)} async-done(((bf16[32,16,256]{2,1,0:T(8,128)(2,1)}), bf16[32,16,256]{2,1,0:T(8,128)(2,1)S(1)}, u32[]{:S(2)}, u32[]{:S(2)}) %all-to-all-start) | async-done | bytes 262176 | tf_op jit(solution)/shard_map/all_to_all | solution.py:408
  46.7 0.0 copy-done.14
  46.7 0.9 shard_map.129
  47.5 4.0 %all-to-all-start.1 = ((bf16[32,16,256]{2,1,0:T(8,128)(2,1)}), bf16[32,16,256]{2,1,0:T(8,128)(2,1)S(1)}, u32[]{:S(2)}, u32[]{:S(2)}) async-start(bf16[32,16,256]{2,1,0:T(8,128)(2,1)} %shard_map.129), calls=%async_computation.1 | async-start | bytes 524288 | tf_op jit(solution)/shard_map/all_to_all | solution.py:416
  51.6 0.7 shard_map.125.table_ref
  52.3 1.3 %copy-done = bf16[1024,1024]{1,0:T(8,128)(2,1)} copy-done((bf16[1024,1024]{1,0:T(8,128)(2,1)}, bf16[1024,1024]{1,0:T(8,128)(2,1)S(1)}, u32[]{:S(2)}) %copy-start) | copy-done | bytes 2097176
  53.6 0.0 collective-permute-done.4.low_ref
  53.6 0.0 collective-permute-done.5.high_ref
  53.6 3.9 %shard_map.120 = (bf16[2304,256]{1,0:T(8,128)(2,1)}, bf16[256,128]{1,0:T(8,128)(2,1)}, bf16[128,512]{1,0:T(8,128)(2,1)}, f32[1,512]{1,0:T(1,128)}, bf16[256,256]{1,0:T(8,128)(2,1)}) custom-call(bf16[256,256]{1,0:T(8,128)(2,1)} %copy-done.4, bf16[256,256]{1,0:T(8,128)(2,1)} %bitcast.12, bf16[256,256]{1,0:T(8,128)(2,1)} %copy-done.5, ...), custom_call_target="tpu_custom_call" | custom-call | flops 301989888 | bytes 4194304 | tf_op jit(solution)/shard_map/pallas_call | solution.py:37
  57.5 5.7 %shard_map.121.refs_0_ = f32[256,256]{1,0:T(8,128)} custom-call(bf16[256,128]{1,0:T(8,128)(2,1)} %get-tuple-element.19.cols_ref, bf16[2304,256]{1,0:T(8,128)(2,1)} %get-tuple-element.20.hidden, bf16[128,512]{1,0:T(8,128)(2,1)} %get-tuple-element.21.pairs, f32[1,512]{1,0:T(1,128)} %get-tuple-element.22.bias, bf16[256,256]{1,0:T(8,128)(2,1)} %get-tuple-element.23.wf_ref), custom_call_target="tpu_custom_call" | custom-call | flops 2415919104 | bytes 4194304 | tf_op jit(solution)/shard_map/pallas_call | solution.py:37
  63.3 0.0 all-to-all-done.1
  63.3 0.0 collective-permute-start.9
  63.3 9.5 %shard_map.122.refs_0_ = f32[256,256]{1,0:T(8,128)} custom-call(bf16[256,128]{1,0:T(8,128)(2,1)} %get-tuple-element.19.cols_ref, bf16[2304,256]{1,0:T(8,128)(2,1)} %get-tuple-element.20.hidden, bf16[128,512]{1,0:T(8,128)(2,1)} %get-tuple-element.21.pairs, f32[1,512]{1,0:T(1,128)} %get-tuple-element.22.bias, bf16[256,256]{1,0:T(8,128)(2,1)} %get-tuple-element.23.wf_ref, ...), custom_call_target="tpu_custom_call" | custom-call | flops 4831838208 | bytes 4194304 | tf_op jit(solution)/shard_map/pallas_call | solution.py:37
  72.8 0.0 collective-permute-done.9.other_ref
  72.8 1.6 %copy-done.1 = bf16[1024,1024]{1,0:T(8,128)(2,1)S(1)} copy-done((bf16[1024,1024]{1,0:T(8,128)(2,1)S(1)}, bf16[1024,1024]{1,0:T(8,128)(2,1)}, u32[]{:S(2)}) %copy-start.1) | copy-done | bytes 2097176
  74.4 0.7 shard_map.130
  75.1 3.5 %collective-permute-start.10 = (bf16[256,256]{1,0:T(8,128)(2,1)S(1)}, bf16[256,256]{1,0:T(8,128)(2,1)S(1)}, u32[]{:S(2)}, u32[]{:S(2)}) collective-permute-start(bf16[256,256]{1,0:T(8,128)(2,1)S(1)} %get-tuple-element.28), channel_id=1, source_target_pairs={{192,0},{0,64},{64,128},{128,192},{193,1},{1,65},{65,129},{129,193... | collective-permute-start | bytes 393224 | tf_op jit(solution)/shard_map/ppermute | solution.py:343
  78.6 0.0 collective-permute-start.11
  78.6 1.6 %collective-permute-start.12 = (bf16[256,256]{1,0:T(8,128)(2,1)S(1)}, bf16[256,256]{1,0:T(8,128)(2,1)S(1)}, u32[]{:S(2)}, u32[]{:S(2)}) collective-permute-start(bf16[256,256]{1,0:T(8,128)(2,1)S(1)} %get-tuple-element.30), channel_id=1, source_target_pairs={{128,0},{192,64},{0,128},{64,192},{129,1},{193,65},{1,129},{65,193... | collective-permute-start | bytes 393224 | tf_op jit(solution)/shard_map/ppermute | solution.py:343
  80.2 0.0 copy-done.15
  80.2 0.0 copy-done.17
  80.2 3.8 %shard_map.123.short_ref = f32[256,256]{1,0:T(8,128)S(1)} custom-call(bf16[256,128]{1,0:T(8,128)(2,1)S(1)} %copy-done.18, bf16[2304,256]{1,0:T(8,128)(2,1)S(1)} %copy-done.15, bf16[128,512]{1,0:T(8,128)(2,1)S(1)} %copy-done.16, f32[1,512]{1,0:T(1,128)S(1)} %copy-done.19, bf16[256,256]{1,0:T(8,128)(2,1)S(1)} %copy-done.17, f32[256,256]{1,0:T(8,128)S(1)} %copy-done.20), custom_call_target="tpu_custom_call" | custom-call | flops 2415919104 | bytes 4194304 | tf_op jit(solution)/shard_map/pallas_call | solution.py:37
  84.0 0.0 collective-permute-done.10.e1_ref
  84.0 4.3 %collective-permute-done.11.e2_ref = bf16[256,256]{1,0:T(8,128)(2,1)S(1)} collective-permute-done((bf16[256,256]{1,0:T(8,128)(2,1)S(1)}, bf16[256,256]{1,0:T(8,128)(2,1)S(1)}, u32[]{:S(2)}, u32[]{:S(2)}) %collective-permute-start.11) | collective-permute-done | bytes 131104 | tf_op jit(solution)/shard_map/ppermute | solution.py:343
  88.3 0.0 collective-permute-done.12.e3_ref
  88.3 0.0 copy-done.6
  88.3 0.9 shard_map.131
  (22 shorter events, 0.0 us)
Async XLA Ops:
  0.0 19.4 %copy-start.2 = (bf16[1,1,256,256]{3,2,1,0:T(8,128)(2,1)S(1)}, bf16[1,1,256,256]{3,2,1,0:T(8,128)(2,1)}, u32[]{:S(2)}) copy-start(bf16[1,1,256,256]{3,2,1,0:T(8,128)(2,1)} %param.12) | copy-start | bytes 393220
  0.0 19.3 %collective-permute-start = (bf16[256,256]{1,0:T(8,128)(2,1)}, bf16[256,256]{1,0:T(8,128)(2,1)S(1)}, u32[]{:S(2)}, u32[]{:S(2)}) collective-permute-start(bf16[256,256]{1,0:T(8,128)(2,1)} %bitcast.9), channel_id=1, source_target_pairs={{192,0},{0,64},{64,128},{128,192},{193,1},{1,65},{65,129},{129,193... | collective-permute-start | bytes 393224 | tf_op jit(solution)/shard_map/ppermute | solution.py:343
  1.9 17.4 %collective-permute-start.1 = (bf16[256,256]{1,0:T(8,128)(2,1)}, bf16[256,256]{1,0:T(8,128)(2,1)S(1)}, u32[]{:S(2)}, u32[]{:S(2)}) collective-permute-start(bf16[256,256]{1,0:T(8,128)(2,1)} %bitcast.10), channel_id=1, source_target_pairs={{64,0},{128,64},{192,128},{0,192},{65,1},{129,65},{193,129},{1,193... | collective-permute-start | bytes 393224 | tf_op jit(solution)/shard_map/ppermute | solution.py:343
  2.0 17.4 %collective-permute-start.7 = (bf16[256,256]{1,0:T(8,128)(2,1)}, bf16[256,256]{1,0:T(8,128)(2,1)S(1)}, u32[]{:S(2)}, u32[]{:S(2)}) collective-permute-start(bf16[256,256]{1,0:T(8,128)(2,1)} %bitcast.11), channel_id=1, source_target_pairs={{128,0},{192,64},{0,128},{64,192},{129,1},{193,65},{1,129},{65,193... | collective-permute-start | bytes 393224 | tf_op jit(solution)/shard_map/ppermute | solution.py:343
  4.9 4.5 %collective-permute-start.2 = (f32[3,256]{1,0:T(4,128)}, f32[3,256]{1,0:T(4,128)S(1)}, u32[]{:S(2)}, u32[]{:S(2)}) collective-permute-start(f32[3,256]{1,0:T(4,128)} %get-tuple-element.18.refs_4_.p1.refs_0_), channel_id=1, source_target_pairs={{192,0},{0,64},{64,128},{128,192},{193,1},{1,65},{65,129},{129,193... | collective-permute-start | bytes 9224 | tf_op jit(solution)/shard_map/ppermute | solution.py:343
  7.0 5.0 %collective-permute-start.3 = (f32[3,256]{1,0:T(4,128)}, f32[3,256]{1,0:T(4,128)S(1)}, u32[]{:S(2)}, u32[]{:S(2)}) collective-permute-start(f32[3,256]{1,0:T(4,128)} %get-tuple-element.18.refs_4_.p1.refs_0_), channel_id=1, source_target_pairs={{64,0},{128,64},{192,128},{0,192},{65,1},{129,65},{193,129},{1,193... | collective-permute-start | bytes 9224 | tf_op jit(solution)/shard_map/ppermute | solution.py:343
  9.4 23.7 %copy-start.12 = (f32[3,256]{1,0:T(4,128)}, f32[3,256]{1,0:T(4,128)S(1)}, u32[]{:S(2)}) copy-start(f32[3,256]{1,0:T(4,128)S(1)} %collective-permute-done.2.refs_3_.p0.refs_2_) | copy-start | bytes 9220
  9.4 5.3 %collective-permute-start.6 = (f32[3,256]{1,0:T(4,128)}, f32[3,256]{1,0:T(4,128)S(1)}, u32[]{:S(2)}, u32[]{:S(2)}) collective-permute-start(f32[3,256]{1,0:T(4,128)} %get-tuple-element.18.refs_4_.p1.refs_0_), channel_id=1, source_target_pairs={{128,0},{192,64},{0,128},{64,192},{129,1},{193,65},{1,129},{65,193... | collective-permute-start | bytes 9224 | tf_op jit(solution)/shard_map/ppermute | solution.py:343
  12.1 21.0 %copy-start.13 = (f32[3,256]{1,0:T(4,128)}, f32[3,256]{1,0:T(4,128)S(1)}, u32[]{:S(2)}) copy-start(f32[3,256]{1,0:T(4,128)S(1)} %collective-permute-done.3.refs_5_.p2.refs_1_) | copy-start | bytes 9220
  14.7 0.9 %copy-start.7 = (bf16[512,128]{1,0:T(8,128)(2,1)S(1)}, bf16[512,128]{1,0:T(8,128)(2,1)}, u32[]{:S(2)}) copy-start(bf16[512,128]{1,0:T(8,128)(2,1)} %get-tuple-element.24.refs_4_) | copy-start | bytes 393220
  15.6 0.7 copy-start.10
  16.3 3.1 %copy-start.9 = (bf16[256,256]{1,0:T(8,128)(2,1)S(1)}, bf16[256,256]{1,0:T(8,128)(2,1)}, u32[]{:S(2)}) copy-start(bf16[256,256]{1,0:T(8,128)(2,1)} %refs_4_.1) | copy-start | bytes 393220
  19.3 13.7 %copy-start.4 = (bf16[256,256]{1,0:T(8,128)(2,1)}, bf16[256,256]{1,0:T(8,128)(2,1)S(1)}, u32[]{:S(2)}) copy-start(bf16[256,256]{1,0:T(8,128)(2,1)S(1)} %collective-permute-done.refs_0_.r0.refs_2_) | copy-start | bytes 393220
  19.4 13.7 %copy-start.5 = (bf16[256,256]{1,0:T(8,128)(2,1)}, bf16[256,256]{1,0:T(8,128)(2,1)S(1)}, u32[]{:S(2)}) copy-start(bf16[256,256]{1,0:T(8,128)(2,1)S(1)} %collective-permute-done.1.refs_2_.r2.refs_1_) | copy-start | bytes 393220
  20.1 1.6 %collective-permute-start.8 = (bf16[512,256]{1,0:T(8,128)(2,1)S(1)}, bf16[512,256]{1,0:T(8,128)(2,1)S(1)}, u32[]{:S(2)}, u32[]{:S(2)}) collective-permute-start(bf16[512,256]{1,0:T(8,128)(2,1)S(1)} %get-tuple-element.26), channel_id=1, source_target_pairs={{0,1},{1,0},{2,3},{3,2},{4,5},{5,4},{6,7},{7,6},{8,9},{9,8},{10,11... | collective-permute-start | bytes 786440 | tf_op jit(solution)/shard_map/ppermute | solution.py:386
  20.2 12.9 %copy-start.11 = (f32[3,256]{1,0:T(4,128)S(1)}, f32[3,256]{1,0:T(4,128)}, u32[]{:S(2)}) copy-start(f32[3,256]{1,0:T(4,128)} %get-tuple-element.18.refs_4_.p1.refs_0_) | copy-start | bytes 9220
  20.2 26.5 %copy-start.8 = (s32[3,2048]{1,0:T(4,128)S(1)}, s32[3,2048]{1,0:T(4,128)}, u32[]{:S(2)}) copy-start(s32[3,2048]{1,0:T(4,128)} %wave_ref.1) | copy-start | bytes 73732
  20.2 26.5 %copy-start.14 = (f32[256]{0:T(256)S(1)}, f32[256]{0:T(256)}, u32[]{:S(2)}) copy-start(f32[256]{0:T(256)} %param.17) | copy-start | bytes 3076
  22.5 24.2 %all-to-all-start = ((bf16[32,16,256]{2,1,0:T(8,128)(2,1)}), bf16[32,16,256]{2,1,0:T(8,128)(2,1)S(1)}, u32[]{:S(2)}, u32[]{:S(2)}) async-start(bf16[32,16,256]{2,1,0:T(8,128)(2,1)} %bitcast.5), calls=%async_computation | async-start | bytes 524288 | tf_op jit(solution)/shard_map/all_to_all | solution.py:408
  33.2 20.5 %collective-permute-start.4 = (bf16[3,288,256]{2,1,0:T(8,128)(2,1)S(1)}, bf16[3,288,256]{2,1,0:T(8,128)(2,1)}, u32[]{:S(2)}, u32[]{:S(2)}) collective-permute-start(bf16[3,288,256]{2,1,0:T(8,128)(2,1)S(1)} %shard_map.119), channel_id=1, source_target_pairs={{63,0},{0,1},{1,2},{2,3},{3,4},{4,5},{5,6},{6,7},{7,8},{8,9},{9,10... | collective-permute-start | bytes 1327112 | tf_op jit(solution)/shard_map/ppermute | solution.py:346
  33.3 20.4 %collective-permute-start.5 = (bf16[3,288,256]{2,1,0:T(8,128)(2,1)S(1)}, bf16[3,288,256]{2,1,0:T(8,128)(2,1)}, u32[]{:S(2)}, u32[]{:S(2)}) collective-permute-start(bf16[3,288,256]{2,1,0:T(8,128)(2,1)S(1)} %shard_map.119), channel_id=1, source_target_pairs={{1,0},{2,1},{3,2},{4,3},{5,4},{6,5},{7,6},{8,7},{9,8},{10,9},{11,1... | collective-permute-start | bytes 1327112 | tf_op jit(solution)/shard_map/ppermute | solution.py:346
  47.5 15.7 %all-to-all-start.1 = ((bf16[32,16,256]{2,1,0:T(8,128)(2,1)}), bf16[32,16,256]{2,1,0:T(8,128)(2,1)S(1)}, u32[]{:S(2)}, u32[]{:S(2)}) async-start(bf16[32,16,256]{2,1,0:T(8,128)(2,1)} %shard_map.129), calls=%async_computation.1 | async-start | bytes 524288 | tf_op jit(solution)/shard_map/all_to_all | solution.py:416
  52.3 1.4 %copy-start = (bf16[1024,1024]{1,0:T(8,128)(2,1)}, bf16[1024,1024]{1,0:T(8,128)(2,1)S(1)}, u32[]{:S(2)}) copy-start(bf16[1024,1024]{1,0:T(8,128)(2,1)S(1)} %shard_map.125.table_ref) | copy-start | bytes 6291460
  63.3 9.5 %collective-permute-start.9 = (bf16[512,256]{1,0:T(8,128)(2,1)S(1)}, bf16[512,256]{1,0:T(8,128)(2,1)S(1)}, u32[]{:S(2)}, u32[]{:S(2)}) collective-permute-start(bf16[512,256]{1,0:T(8,128)(2,1)S(1)} %bitcast.16), channel_id=1, source_target_pairs={{0,1},{1,0},{2,3},{3,2},{4,5},{5,4},{6,7},{7,6},{8,9},{9,8},{10,11... | collective-permute-start | bytes 786440 | tf_op jit(solution)/shard_map/ppermute | solution.py:419
  72.8 1.6 %copy-start.1 = (bf16[1024,1024]{1,0:T(8,128)(2,1)S(1)}, bf16[1024,1024]{1,0:T(8,128)(2,1)}, u32[]{:S(2)}) copy-start(bf16[1024,1024]{1,0:T(8,128)(2,1)} %copy-done) | copy-start | bytes 6291460
  74.4 5.8 %copy-start.15 = (bf16[2304,256]{1,0:T(8,128)(2,1)S(1)}, bf16[2304,256]{1,0:T(8,128)(2,1)}, u32[]{:S(2)}) copy-start(bf16[2304,256]{1,0:T(8,128)(2,1)} %get-tuple-element.20.hidden) | copy-start | bytes 3538948
  74.4 5.8 %copy-start.16 = (bf16[128,512]{1,0:T(8,128)(2,1)S(1)}, bf16[128,512]{1,0:T(8,128)(2,1)}, u32[]{:S(2)}) copy-start(bf16[128,512]{1,0:T(8,128)(2,1)} %get-tuple-element.21.pairs) | copy-start | bytes 393220
  74.4 5.8 %copy-start.17 = (bf16[256,256]{1,0:T(8,128)(2,1)S(1)}, bf16[256,256]{1,0:T(8,128)(2,1)}, u32[]{:S(2)}) copy-start(bf16[256,256]{1,0:T(8,128)(2,1)} %get-tuple-element.23.wf_ref) | copy-start | bytes 393220
  74.4 5.8 %copy-start.18 = (bf16[256,128]{1,0:T(8,128)(2,1)S(1)}, bf16[256,128]{1,0:T(8,128)(2,1)}, u32[]{:S(2)}) copy-start(bf16[256,128]{1,0:T(8,128)(2,1)} %get-tuple-element.19.cols_ref) | copy-start | bytes 196612
  74.4 5.8 %copy-start.19 = (f32[1,512]{1,0:T(1,128)S(1)}, f32[1,512]{1,0:T(1,128)}, u32[]{:S(2)}) copy-start(f32[1,512]{1,0:T(1,128)} %get-tuple-element.22.bias) | copy-start | bytes 6148
  74.4 5.8 %copy-start.20 = (f32[256,256]{1,0:T(8,128)S(1)}, f32[256,256]{1,0:T(8,128)}, u32[]{:S(2)}) copy-start(f32[256,256]{1,0:T(8,128)} %shard_map.122.refs_0_) | copy-start | bytes 786436
  75.1 8.8 %collective-permute-start.10 = (bf16[256,256]{1,0:T(8,128)(2,1)S(1)}, bf16[256,256]{1,0:T(8,128)(2,1)S(1)}, u32[]{:S(2)}, u32[]{:S(2)}) collective-permute-start(bf16[256,256]{1,0:T(8,128)(2,1)S(1)} %get-tuple-element.28), channel_id=1, source_target_pairs={{192,0},{0,64},{64,128},{128,192},{193,1},{1,65},{65,129},{129,193... | collective-permute-start | bytes 393224 | tf_op jit(solution)/shard_map/ppermute | solution.py:343
  78.6 9.6 %collective-permute-start.11 = (bf16[256,256]{1,0:T(8,128)(2,1)S(1)}, bf16[256,256]{1,0:T(8,128)(2,1)S(1)}, u32[]{:S(2)}, u32[]{:S(2)}) collective-permute-start(bf16[256,256]{1,0:T(8,128)(2,1)S(1)} %get-tuple-element.29), channel_id=1, source_target_pairs={{64,0},{128,64},{192,128},{0,192},{65,1},{129,65},{193,129},{1,193... | collective-permute-start | bytes 393224 | tf_op jit(solution)/shard_map/ppermute | solution.py:343
  78.6 9.6 %copy-start.3 = (bf16[1,1,256,256]{3,2,1,0:T(8,128)(2,1)S(1)}, bf16[1,1,256,256]{3,2,1,0:T(8,128)(2,1)}, u32[]{:S(2)}) copy-start(bf16[1,1,256,256]{3,2,1,0:T(8,128)(2,1)} %param.12) | copy-start | bytes 393220
  78.6 9.6 %copy-start.6 = (bf16[256,256]{1,0:T(8,128)(2,1)S(1)}, bf16[256,256]{1,0:T(8,128)(2,1)}, u32[]{:S(2)}) copy-start(bf16[256,256]{1,0:T(8,128)(2,1)} %wout_ref.1) | copy-start | bytes 393220
  78.6 9.6 %collective-permute-start.12 = (bf16[256,256]{1,0:T(8,128)(2,1)S(1)}, bf16[256,256]{1,0:T(8,128)(2,1)S(1)}, u32[]{:S(2)}, u32[]{:S(2)}) collective-permute-start(bf16[256,256]{1,0:T(8,128)(2,1)S(1)} %get-tuple-element.30), channel_id=1, source_target_pairs={{128,0},{192,64},{0,128},{64,192},{129,1},{193,65},{1,129},{65,193... | collective-permute-start | bytes 393224 | tf_op jit(solution)/shard_map/ppermute | solution.py:343

commit v5 on v4

--- a/solution.py
+++ b/solution.py
@@ -32,12 +32,12 @@
 HBM = pl.BlockSpec(memory_space=pltpu.HBM)
 
 
-def call(body, out, ins, scratch=(), flops=0, nbytes=0, trans=0, grant=16, spec=VMEM):
+def call(body, out, ins, scratch=(), flops=0, nbytes=0, trans=0, grant=16, spec=None):
     multiple = isinstance(out, (list, tuple))
     return pl.pallas_call(
         body,
         out_shape=out,
-        in_specs=[spec] * len(ins),
+        in_specs=spec or [VMEM] * len(ins),
         out_specs=[VMEM] * len(out) if multiple else VMEM,
         scratch_shapes=list(scratch),
         compiler_params=pltpu.CompilerParams(vmem_limit_bytes=int(grant * (1 << 20))),
@@ -193,8 +193,8 @@
 
 
 def prepare_kernel(
-    r0, r1, r2, low_ref, high_ref, p0, p1, p2, slots_ref, images_ref, win_ref, wrbf_ref, brbf_ref, wf_ref,
-    hidden, cols, pairs, bias, wf_out, pos, turned,
+    r0, r1, r2, low_ref, high_ref, p0, p1, p2, slots_ref, images_ref, win_ref, wrbf_ref, brbf_ref,
+    table, cols, pairs, bias, row_at, pos, turned,
 ):
     basis_count, width = wrbf_ref.shape
     pairs[...] = jnp.zeros_like(pairs)
@@ -202,7 +202,8 @@
     pairs[basis_count:, width:] = wrbf_ref[...]
     bias[:, 0:width] = brbf_ref[...] * math.log2(math.e)
     bias[:, width:] = brbf_ref[...] * math.log2(math.e)
-    wf_out[...] = wf_ref[...]
+    lane = 128
+    halves = width // lane
     slots, atoms = slots_ref.shape
     weight = win_ref[...]
     own = (r0, r1, r2)
@@ -216,9 +217,14 @@
                 rows = ref[p, 0:atoms, :]
                 parts = ref[p, atoms:, :].astype(jnp.float32)
                 place = (parts[0:3, :] + parts[8:11, :]) + parts[16:19, :]
-            hidden[brick * atoms : (brick + 1) * atoms, :] = dot(rows, weight).astype(jnp.bfloat16)
+            hidden = dot(rows, weight).astype(jnp.bfloat16).astype(jnp.float32)
+            for h in range(halves):
+                table[pl.ds(halves * brick * atoms + h, atoms, stride=halves), :] = hidden[
+                    :, h * lane : (h + 1) * lane
+                ]
             pos[0:3, brick * atoms : (brick + 1) * atoms] = place
-    lane = 128
+    row_at[...] = slots_ref[...] * halves
+    table[halves * 9 * atoms :, :] = jnp.zeros((table.shape[0] - halves * 9 * atoms, lane), jnp.float32)
     for half in range(atoms // lane):
         cut = slice(half * lane, (half + 1) * lane)
         index = slots_ref[:, cut]
@@ -245,72 +251,79 @@
             rounded = rest.astype(jnp.bfloat16).astype(jnp.float32)
             turned[k * slots : (k + 1) * slots, cut] = rounded
             rest = rest - rounded
-        turned[3 * slots : 4 * slots, cut] = ((lane + place) << group).astype(jnp.float32)
+        turned[3 * slots : 4 * slots, cut] = jnp.zeros((slots, lane), jnp.float32)
     cols[...] = turned[...].T.astype(jnp.bfloat16)
 
 
-def short_kernel(first, count, scale, cols_ref, hidden, pairs, bias, wf_ref, *refs):
+def short_kernel(
+    scale, cols_ref, table, row_at, pairs, bias, wf_ref, out_ref, near_a, near_b, at_a, at_b, sems
+):
     lane = 128
     atoms = cols_ref.shape[0]
     slots = cols_ref.shape[1] // 4
     basis_count, width = pairs.shape[0] // 2, wf_ref.shape[1]
-    out_ref = refs[-1]
-    out_ref[...] = refs[0][...] if len(refs) > 1 else jnp.zeros_like(out_ref)
-    row = lax.broadcasted_iota(jnp.int32, (lane, 6 * lane), 0)
-    column = lax.broadcasted_iota(jnp.int32, (lane, 6 * lane), 1)
-    code_slot = jnp.where(row >= 3 * slots, row - 3 * slots - (column >> 7), -lane)
-    dist_slot = jnp.where(row < 3 * slots, (row & (slots - 1)) - ((column - 4 * lane) >> 6), -lane)
-    source = jnp.where(column < 4 * lane, code_slot, dist_slot)
+    halves = width // lane
+    group = near_a.shape[0] // (halves * atoms)
+    ahead = at_a.shape[0]
+    wide_lanes = group // 2 * lane
+    out_ref[...] = jnp.zeros_like(out_ref)
+    row = lax.broadcasted_iota(jnp.int32, (lane, wide_lanes), 0)
+    column = lax.broadcasted_iota(jnp.int32, (lane, wide_lanes), 1)
+    source = jnp.where(row < 3 * slots, (row & (slots - 1)) - (column >> 6), -lane)
     centers = (
         (lax.broadcasted_iota(jnp.int32, (1, lane), 1) & (basis_count - 1)).astype(jnp.float32)
         * (4.0 / (basis_count - 1))
         * ZOOM
     )
-    lanes = lax.broadcasted_iota(jnp.int32, (16, lane), 1) + lane
-    groups = 9 * atoms // lane
-
-    def spread(j):
-        select = (source == 4 * j).astype(jnp.float32).astype(jnp.bfloat16)
-        return dot(cols_ref[...], select)
-
-    def hot_of(wide):
-        codes = [
-            wide[:, i * lane : (i + 1) * lane].astype(jnp.bfloat16) for i in range(4)
-        ]
-        code = jnp.concatenate(codes, axis=0)
-        parts = []
-        for g in range(groups):
-            number = jnp.broadcast_to(
-                (lanes << g).astype(jnp.float32).astype(jnp.bfloat16)[None],
-                (4 * atoms // 16, 16, lane),
-            ).reshape(4 * atoms, lane)
-            parts.append(jnp.where(code == number, jnp.bfloat16(1), jnp.bfloat16(0)))
-        return jnp.concatenate(parts, axis=1)
-
-    def filters_of(wide):
+
+    def fetch(first, buffer, sem):
+        rows = pl.ds(pl.multiple_of(first, ahead), ahead)
+        return pltpu.make_async_copy(row_at.at[rows, :], buffer, sem)
+
+    def one_group(first, buffer, offset, near):
+        for i in range(group):
+            for k in range(atoms):
+                to = (i * atoms + k) * halves
+                near[to : to + halves, :] = table[pl.ds(buffer[offset + i, k], halves), :]
+        select = (source == first).astype(jnp.float32).astype(jnp.bfloat16)
+        wide = dot(cols_ref[...], select)
         inner = []
-        for p in range(2):
-            offset = wide[:, (4 + p) * lane : (5 + p) * lane] - centers
+        for p in range(group // 2):
+            offset = wide[:, p * lane : (p + 1) * lane] - centers
             basis = jnp.exp2(-(offset * offset)).astype(jnp.bfloat16)
             value = dot(basis, pairs[...]) * math.log2(math.e) + bias[...]
             both = (jnp.log(1.0 + jnp.exp2(value)) - math.log(2.0)).astype(jnp.bfloat16)
             inner += [both[:, :width], both[:, width:]]
-        return dot(jnp.concatenate(inner, axis=0), wf_ref[...])
-
-    def add(filters, gathered):
-        product = filters * gathered
-        total = product[0:atoms]
-        for i in range(1, 4):
-            total = total + product[i * atoms : (i + 1) * atoms]
-        out_ref[...] += total
+        filters = dot(jnp.concatenate(inner, axis=0), wf_ref[...])
+        for h in range(halves):
+            cut = slice(h * lane, (h + 1) * lane)
+            total = out_ref[:, cut]
+            for i in range(group):
+                gathered = near[pl.ds(i * atoms * halves + h, atoms, stride=halves), :]
+                total = total + filters[i * atoms : (i + 1) * atoms, cut] * gathered
+            out_ref[:, cut] = total
+
+    def both_groups(first, buffer):
+        one_group(first, buffer, 0, near_a)
+        one_group(first + group, buffer, group, near_b)
+
+    fetch(0, at_a, sems.at[0]).start()
 
     def body(j, carry):
-        wide = spread(first + j)
-        gathered = dot(hot_of(wide), hidden[...])
-        add(filters_of(wide), gathered)
+        first = 2 * ahead * j
+        fetch(first, at_a, sems.at[0]).wait()
+        fetch(first + ahead, at_b, sems.at[1]).start()
+        both_groups(first, at_a)
+        fetch(first + ahead, at_b, sems.at[1]).wait()
+
+        @pl.when(first + 2 * ahead < slots)
+        def _():
+            fetch(first + 2 * ahead, at_a, sems.at[0]).start()
+
+        both_groups(first + ahead, at_b)
         return carry
 
-    lax.fori_loop(0, count, body, 0)
+    lax.fori_loop(0, slots // (2 * ahead), body, 0)
     out_ref[...] = out_ref[...] * scale
 
 
@@ -361,7 +374,7 @@
         ],
         nbytes=1 << 19,
         grant=63.25,
-        spec=HBM,
+        spec=[HBM] * 2,
     )
     place_of = {0: place, **{d: from_role(place, d) for d in shifts}}
     rows_of = {0: rows, **{d: from_role(rows, d) for d in shifts}}
@@ -427,39 +440,34 @@
         nbytes=1 << 20,
     )
     low, high = from_column(bundle, columns - 1), from_column(bundle, 1)
-    hidden, cols, pairs, bias, filter_weight = call(
+    table, cols, pairs, bias, row_at = call(
         prepare_kernel,
         [
-            jax.ShapeDtypeStruct((9 * atoms, width), bf16),
+            jax.ShapeDtypeStruct((9 * atoms * width // 128 + 16, 128), f32),
             jax.ShapeDtypeStruct((atoms, 4 * slots), bf16),
             jax.ShapeDtypeStruct((2 * w_rbf.shape[0], 2 * width), bf16),
             jax.ShapeDtypeStruct((1, 2 * width), f32),
-            jax.ShapeDtypeStruct((width, width), bf16),
+            jax.ShapeDtypeStruct((slots, atoms), jnp.int32),
         ],
         [rows_of[d] for d in triple]
         + [low, high]
         + [place_of[d] for d in triple]
-        + [neighbours[0, 0], images[0, 0], w_in, w_rbf, b_rbf[None, :], w_filter],
+        + [neighbours[0, 0], images[0, 0], w_in, w_rbf, b_rbf[None, :]],
         scratch=[pltpu.VMEM((8, 9 * atoms), f32), pltpu.VMEM((4 * slots, atoms), f32)],
         flops=2 * 9 * atoms * width * width,
         nbytes=4 << 20,
-        grant=63.25,
-    )
-    short = ()
-    ends = (0, 2, 6, slots // 4)
-    for i in range(3):
-        count = ends[i + 1] - ends[i]
-        short = (
-            call(
-                functools.partial(short_kernel, ends[i], count, 1.0 if i < 2 else slots ** (-0.5)),
-                jax.ShapeDtypeStruct((atoms, width), f32),
-                [cols, hidden, pairs, bias, filter_weight, *short],
-                flops=2 * 4 * count * atoms * 9 * atoms * width,
-                nbytes=4 << 20,
-                grant=63.25 if i < 2 else 16,
-            ),
-        )
-    short = short[0]
+    )
+    near = pltpu.VMEM((4 * atoms * width // 128, 128), f32)
+    short = call(
+        functools.partial(short_kernel, slots ** (-0.5)),
+        jax.ShapeDtypeStruct((atoms, width), f32),
+        [cols, table, row_at, pairs, bias, w_filter],
+        scratch=[near, near]
+        + [pltpu.SMEM((8, atoms), jnp.int32)] * 2
+        + [pltpu.SemaphoreType.DMA((2,))],
+        flops=4 * slots * atoms * width * width,
+        nbytes=4 << 20,
+    )
     parts = call(
         ewald_kernel,
         [jax.ShapeDtypeStruct((atoms, width), bf16)] * roles,

time: 90.1 us -> 88.8 us (0.986)
  the two profiles are of different devices: /device:TPU:24 before, /device:TPU:16 now
where the time goes in v5:
time: 88.8 us; the launch traced here: 88.5 us
  starting transfers between devices  25.1 us (28%)
  Pallas kernels  23.1 us (26%)
  blocking collectives  22.1 us (25%)
  waiting for transfers between devices  16.2 us (18%)
  local copies, waits for them, and re-layouts  1.63 us (2%)
    pallas_call x12, Pallas kernels, call(): pl.pallas_call(body, out_shape=out, in_specs=spec or [VMEM] * len(ins), o...  23.1 us
    all_to_all x1, blocking collectives, block(): lax.all_to_all(kept.reshape(chunks), 'atoms', 0, 0, axis_index_groups=sam...  22.1 us
    ppermute x9, starting transfers between devices, from_role(): lax.ppermute(block, 'role', [((i + shift) % roles, i) for i in range(role...  15.4 us
    all_to_all x1, waiting for transfers between devices, block(): lax.all_to_all(copies, 'atoms', 0, 0, axis_index_groups=same_core)  7.97 us
    ppermute x9, waiting for transfers between devices, from_role(): lax.ppermute(block, 'role', [((i + shift) % roles, i) for i in range(role...  5.64 us
    ppermute x2, starting transfers between devices, from_column(): lax.ppermute(block, 'atoms', [((i + shift) % columns, i) for i in range(c...  5.13 us
    all_to_all x1, starting transfers between devices, block(): lax.all_to_all(copies, 'atoms', 0, 0, axis_index_groups=same_core)  4.43 us
  transfers between devices with their start and end apart: 14, of which 5 were waited for; matrix products, arithmetic and copies ran while one was open for 0% of the time, Pallas kernels for 23%

profile of v5, /device:TPU:16, one launch (start us, length us, event | category | flops | bytes accessed | tf_op | source)
XLA Modules:
  0.0 88.5 jit_solution(1269238483065196348)
XLA Ops:
  0.0 0.0 copy-start
  0.0 1.3 %collective-permute-start = (bf16[256,256]{1,0:T(8,128)(2,1)}, bf16[256,256]{1,0:T(8,128)(2,1)S(1)}, u32[]{:S(2)}, u32[]{:S(2)}) collective-permute-start(bf16[256,256]{1,0:T(8,128)(2,1)} %bitcast.9), channel_id=1, source_target_pairs={{192,0},{0,64},{64,128},{128,192},{193,1},{1,65},{65,129},{129,193... | collective-permute-start | bytes 393224 | tf_op jit(solution)/shard_map/ppermute | solution.py:356
  1.3 0.7 collective-permute-start.1
  2.0 3.3 %collective-permute-start.7 = (bf16[256,256]{1,0:T(8,128)(2,1)}, bf16[256,256]{1,0:T(8,128)(2,1)S(1)}, u32[]{:S(2)}, u32[]{:S(2)}) collective-permute-start(bf16[256,256]{1,0:T(8,128)(2,1)} %bitcast.11), channel_id=1, source_target_pairs={{128,0},{192,64},{0,128},{64,192},{129,1},{193,65},{1,129},{65,193... | collective-permute-start | bytes 393224 | tf_op jit(solution)/shard_map/ppermute | solution.py:356
  5.3 1.5 %shard_map.118 = (bf16[512,128]{1,0:T(8,128)(2,1)}, f32[3,256]{1,0:T(4,128)}) custom-call(s32[3,2048]{1,0:T(4,128)} %wave_ref.1, f32[3,1,256]{2,1,0:T(1,128)} %bitcast.23), custom_call_target="tpu_custom_call" | custom-call | bytes 524288 | tf_op jit(solution)/shard_map/pallas_call | solution.py:37
  6.8 0.1 collective-permute-start.2
  6.9 2.0 %collective-permute-start.3 = (f32[3,256]{1,0:T(4,128)}, f32[3,256]{1,0:T(4,128)S(1)}, u32[]{:S(2)}, u32[]{:S(2)}) collective-permute-start(f32[3,256]{1,0:T(4,128)} %get-tuple-element.18.refs_4_.p1.refs_0_), channel_id=1, source_target_pairs={{64,0},{128,64},{192,128},{0,192},{65,1},{129,65},{193,129},{1,193... | collective-permute-start | bytes 9224 | tf_op jit(solution)/shard_map/ppermute | solution.py:356
  8.9 1.8 %collective-permute-done.2.refs_3_.p0.refs_2_ = f32[3,256]{1,0:T(4,128)S(1)} collective-permute-done((f32[3,256]{1,0:T(4,128)}, f32[3,256]{1,0:T(4,128)S(1)}, u32[]{:S(2)}, u32[]{:S(2)}) %collective-permute-start.2) | collective-permute-done | bytes 3104 | tf_op jit(solution)/shard_map/ppermute | solution.py:356
  10.7 1.5 %collective-permute-start.6 = (f32[3,256]{1,0:T(4,128)}, f32[3,256]{1,0:T(4,128)S(1)}, u32[]{:S(2)}, u32[]{:S(2)}) collective-permute-start(f32[3,256]{1,0:T(4,128)} %get-tuple-element.18.refs_4_.p1.refs_0_), channel_id=1, source_target_pairs={{128,0},{192,64},{0,128},{64,192},{129,1},{193,65},{1,129},{65,193... | collective-permute-start | bytes 9224 | tf_op jit(solution)/shard_map/ppermute | solution.py:356
  12.2 0.0 collective-permute-done.3.refs_5_.p2.refs_1_
  12.2 3.8 %collective-permute-done.6.refs_3_ = f32[3,256]{1,0:T(4,128)S(1)} collective-permute-done((f32[3,256]{1,0:T(4,128)}, f32[3,256]{1,0:T(4,128)S(1)}, u32[]{:S(2)}, u32[]{:S(2)}) %collective-permute-start.6) | collective-permute-done | bytes 3104 | tf_op jit(solution)/shard_map/ppermute | solution.py:356
  16.0 0.0 copy-start.2
  16.0 0.9 %copy-done.2 = bf16[512,128]{1,0:T(8,128)(2,1)S(1)} copy-done((bf16[512,128]{1,0:T(8,128)(2,1)S(1)}, bf16[512,128]{1,0:T(8,128)(2,1)}, u32[]{:S(2)}) %copy-start.2) | copy-done | bytes 131096
  16.9 0.0 copy-start.6
  16.9 0.7 copy-done.6
  17.6 0.0 copy-start.5
  17.6 3.0 %shard_map.122.by_wave.refs_5_.table = bf16[1024,1024]{1,0:T(8,128)(2,1)S(1)} custom-call(f32[3,256]{1,0:T(4,128)S(1)} %copy-done.6, f32[3,256]{1,0:T(4,128)S(1)} %collective-permute-done.3.refs_5_.p2.refs_1_, f32[3,256]{1,0:T(4,128)S(1)} %collective-permute-done.2.refs_3_.p0.refs_2_, f32[3,256]{1,0:T(4,128)S(1)} %collective-permute-done.6.refs_3_, ...), custom_call_target="tpu_custom_call" | custom-call | flops 20971520 | bytes 4194304 | tf_op jit(solution)/shard_map/pallas_call | solution.py:37
  20.6 0.0 collective-permute-done.refs_0_.r0.refs_2_
  20.6 0.0 collective-permute-done.1.refs_2_.r2.refs_1_
  20.6 0.0 collective-permute-done.7.refs_3_
  20.6 0.0 copy-done
  20.7 0.0 copy-done.5
  20.7 0.7 shard_map.124
  21.4 0.1 collective-permute-start.8
  21.5 0.0 copy-start.3
  21.5 0.0 copy-start.11
  21.5 0.4 shard_map.125.own_ref
  21.9 0.0 copy-start.7
  21.9 1.0 %collective-permute-done.8.got_ref = bf16[512,256]{1,0:T(8,128)(2,1)S(1)} collective-permute-done((bf16[512,256]{1,0:T(8,128)(2,1)S(1)}, bf16[512,256]{1,0:T(8,128)(2,1)S(1)}, u32[]{:S(2)}, u32[]{:S(2)}) %collective-permute-start.8) | collective-permute-done | bytes 262176 | tf_op jit(solution)/shard_map/ppermute | solution.py:399
  23.0 22.1 %all_to_all.10.mine_ref = bf16[32,16,256]{2,1,0:T(8,128)(2,1)S(1)} all-to-all(bf16[32,16,256]{2,1,0:T(8,128)(2,1)S(1)} %bitcast.18), channel_id=1, replica_groups={{0,2,4,6,8,10,12,14,16,18,20,22,24,26,28,30,32,34,36,38,40,42,44,46,48,..., dimensions={0} | all-to-all | bytes 524288 | tf_op jit(solution)/shard_map/all_to_all | solution.py:421
  45.2 0.0 copy-done.3
  45.2 0.0 copy-done.11
  45.2 0.8 shard_map.127
  46.0 4.4 %all-to-all-start.1 = ((bf16[32,16,256]{2,1,0:T(8,128)(2,1)}), bf16[32,16,256]{2,1,0:T(8,128)(2,1)S(1)}, u32[]{:S(2)}, u32[]{:S(2)}) async-start(bf16[32,16,256]{2,1,0:T(8,128)(2,1)} %shard_map.127), calls=%async_computation.1 | async-start | bytes 524288 | tf_op jit(solution)/shard_map/all_to_all | solution.py:429
  50.4 0.0 copy-done.7
  50.4 0.1 shard_map.119
  50.5 0.1 collective-permute-start.4
  50.6 5.1 %collective-permute-start.5 = (bf16[3,288,256]{2,1,0:T(8,128)(2,1)S(1)}, bf16[3,288,256]{2,1,0:T(8,128)(2,1)}, u32[]{:S(2)}, u32[]{:S(2)}) collective-permute-start(bf16[3,288,256]{2,1,0:T(8,128)(2,1)S(1)} %shard_map.119), channel_id=1, source_target_pairs={{1,0},{2,1},{3,2},{4,3},{5,4},{6,5},{7,6},{8,7},{9,8},{10,9},{11,1... | collective-permute-start | bytes 1327112 | tf_op jit(solution)/shard_map/ppermute | solution.py:359
  55.6 8.0 %all-to-all-done.1 = bf16[32,16,256]{2,1,0:T(8,128)(2,1)S(1)} async-done(((bf16[32,16,256]{2,1,0:T(8,128)(2,1)}), bf16[32,16,256]{2,1,0:T(8,128)(2,1)S(1)}, u32[]{:S(2)}, u32[]{:S(2)}) %all-to-all-start.1) | async-done | bytes 262176 | tf_op jit(solution)/shard_map/all_to_all | solution.py:429
  63.6 0.0 copy-start.4
  63.6 0.0 copy-start.12
  63.6 0.1 collective-permute-start.9
  63.7 0.7 shard_map.123.table_ref
  64.4 0.0 copy-start.13
  64.4 1.5 %collective-permute-done.4.low_ref = bf16[3,288,256]{2,1,0:T(8,128)(2,1)} collective-permute-done((bf16[3,288,256]{2,1,0:T(8,128)(2,1)S(1)}, bf16[3,288,256]{2,1,0:T(8,128)(2,1)}, u32[]{:S(2)}, u32[]{:S(2)}) %collective-permute-start.4) | collective-permute-done | bytes 442400 | tf_op jit(solution)/shard_map/ppermute | solution.py:359
  65.9 0.0 collective-permute-done.5.high_ref
  66.0 0.0 copy-done.4
  66.0 0.0 copy-done.8
  66.0 0.0 copy-done.9
  66.0 0.0 copy-done.10
  66.0 0.0 copy-done.12
  66.0 2.6 %shard_map.120 = (f32[4624,128]{1,0:T(8,128)S(1)}, bf16[256,128]{1,0:T(8,128)(2,1)S(1)}, bf16[128,512]{1,0:T(8,128)(2,1)S(1)}, f32[1,512]{1,0:T(1,128)S(1)}, s32[32,256]{1,0:T(8,128)S(1)}) custom-call(bf16[256,256]{1,0:T(8,128)(2,1)S(1)} %collective-permute-done.refs_0_.r0.refs_2_, bf16[256,256]{1,0:T(8,128)(2,1)S(1)} %bitcast.14, ...), custom_call_target="tpu_custom_call" | custom-call | flops 301989888 | bytes 4194304 | tf_op jit(solution)/shard_map/pallas_call | solution.py:37
  68.6 0.0 collective-permute-done.9.other_ref
  68.6 0.7 shard_map.128
  69.3 1.0 %collective-permute-start.10 = (bf16[256,256]{1,0:T(8,128)(2,1)S(1)}, bf16[256,256]{1,0:T(8,128)(2,1)S(1)}, u32[]{:S(2)}, u32[]{:S(2)}) collective-permute-start(bf16[256,256]{1,0:T(8,128)(2,1)S(1)} %get-tuple-element.28), channel_id=1, source_target_pairs={{192,0},{0,64},{64,128},{128,192},{193,1},{1,65},{65,129},{129,193... | collective-permute-start | bytes 393224 | tf_op jit(solution)/shard_map/ppermute | solution.py:356
  70.4 1.1 %collective-permute-start.11 = (bf16[256,256]{1,0:T(8,128)(2,1)S(1)}, bf16[256,256]{1,0:T(8,128)(2,1)S(1)}, u32[]{:S(2)}, u32[]{:S(2)}) collective-permute-start(bf16[256,256]{1,0:T(8,128)(2,1)S(1)} %get-tuple-element.29), channel_id=1, source_target_pairs={{64,0},{128,64},{192,128},{0,192},{65,1},{129,65},{193,129},{1,193... | collective-permute-start | bytes 393224 | tf_op jit(solution)/shard_map/ppermute | solution.py:356
  71.4 4.4 %collective-permute-start.12 = (bf16[256,256]{1,0:T(8,128)(2,1)S(1)}, bf16[256,256]{1,0:T(8,128)(2,1)S(1)}, u32[]{:S(2)}, u32[]{:S(2)}) collective-permute-start(bf16[256,256]{1,0:T(8,128)(2,1)S(1)} %get-tuple-element.30), channel_id=1, source_target_pairs={{128,0},{192,64},{0,128},{64,192},{129,1},{193,65},{1,129},{65,193... | collective-permute-start | bytes 393224 | tf_op jit(solution)/shard_map/ppermute | solution.py:356
  75.8 0.0 copy-done.13
  75.8 11.7 %shard_map.121.short_ref = f32[256,256]{1,0:T(8,128)S(1)} custom-call(bf16[256,128]{1,0:T(8,128)(2,1)S(1)} %get-tuple-element.19.cols_ref, f32[4624,128]{1,0:T(8,128)S(1)} %get-tuple-element.20.table, s32[32,256]{1,0:T(8,128)S(1)} %get-tuple-element.21.row_at, bf16[128,512]{1,0:T(8,128)(2,1)S(1)} %get-tuple-element.22.pairs, ...), custom_call_target="tpu_custom_call" | custom-call | flops 2147483648 | bytes 4194304 | tf_op jit(solution)/shard_map/pallas_call | solution.py:37
  87.5 0.0 collective-permute-done.10.e1_ref
  87.5 0.0 collective-permute-done.11.e2_ref
  87.5 0.0 collective-permute-done.12.e3_ref
  87.6 0.0 copy-done.1
  87.6 0.9 shard_map.129
  (5 shorter events, 0.1 us)
Async XLA Ops:
  0.0 20.6 %copy-start = (bf16[1,1,256,256]{3,2,1,0:T(8,128)(2,1)S(1)}, bf16[1,1,256,256]{3,2,1,0:T(8,128)(2,1)}, u32[]{:S(2)}) copy-start(bf16[1,1,256,256]{3,2,1,0:T(8,128)(2,1)} %param.12) | copy-start | bytes 393220
  0.0 20.6 %collective-permute-start = (bf16[256,256]{1,0:T(8,128)(2,1)}, bf16[256,256]{1,0:T(8,128)(2,1)S(1)}, u32[]{:S(2)}, u32[]{:S(2)}) collective-permute-start(bf16[256,256]{1,0:T(8,128)(2,1)} %bitcast.9), channel_id=1, source_target_pairs={{192,0},{0,64},{64,128},{128,192},{193,1},{1,65},{65,129},{129,193... | collective-permute-start | bytes 393224 | tf_op jit(solution)/shard_map/ppermute | solution.py:356
  1.3 19.3 %collective-permute-start.1 = (bf16[256,256]{1,0:T(8,128)(2,1)}, bf16[256,256]{1,0:T(8,128)(2,1)S(1)}, u32[]{:S(2)}, u32[]{:S(2)}) collective-permute-start(bf16[256,256]{1,0:T(8,128)(2,1)} %bitcast.10), channel_id=1, source_target_pairs={{64,0},{128,64},{192,128},{0,192},{65,1},{129,65},{193,129},{1,193... | collective-permute-start | bytes 393224 | tf_op jit(solution)/shard_map/ppermute | solution.py:356
  2.0 18.6 %collective-permute-start.7 = (bf16[256,256]{1,0:T(8,128)(2,1)}, bf16[256,256]{1,0:T(8,128)(2,1)S(1)}, u32[]{:S(2)}, u32[]{:S(2)}) collective-permute-start(bf16[256,256]{1,0:T(8,128)(2,1)} %bitcast.11), channel_id=1, source_target_pairs={{128,0},{192,64},{0,128},{64,192},{129,1},{193,65},{1,129},{65,193... | collective-permute-start | bytes 393224 | tf_op jit(solution)/shard_map/ppermute | solution.py:356
  6.8 3.9 %collective-permute-start.2 = (f32[3,256]{1,0:T(4,128)}, f32[3,256]{1,0:T(4,128)S(1)}, u32[]{:S(2)}, u32[]{:S(2)}) collective-permute-start(f32[3,256]{1,0:T(4,128)} %get-tuple-element.18.refs_4_.p1.refs_0_), channel_id=1, source_target_pairs={{192,0},{0,64},{64,128},{128,192},{193,1},{1,65},{65,129},{129,193... | collective-permute-start | bytes 9224 | tf_op jit(solution)/shard_map/ppermute | solution.py:356
  6.9 5.3 %collective-permute-start.3 = (f32[3,256]{1,0:T(4,128)}, f32[3,256]{1,0:T(4,128)S(1)}, u32[]{:S(2)}, u32[]{:S(2)}) collective-permute-start(f32[3,256]{1,0:T(4,128)} %get-tuple-element.18.refs_4_.p1.refs_0_), channel_id=1, source_target_pairs={{64,0},{128,64},{192,128},{0,192},{65,1},{129,65},{193,129},{1,193... | collective-permute-start | bytes 9224 | tf_op jit(solution)/shard_map/ppermute | solution.py:356
  10.7 5.3 %collective-permute-start.6 = (f32[3,256]{1,0:T(4,128)}, f32[3,256]{1,0:T(4,128)S(1)}, u32[]{:S(2)}, u32[]{:S(2)}) collective-permute-start(f32[3,256]{1,0:T(4,128)} %get-tuple-element.18.refs_4_.p1.refs_0_), channel_id=1, source_target_pairs={{128,0},{192,64},{0,128},{64,192},{129,1},{193,65},{1,129},{65,193... | collective-permute-start | bytes 9224 | tf_op jit(solution)/shard_map/ppermute | solution.py:356
  16.0 0.9 %copy-start.2 = (bf16[512,128]{1,0:T(8,128)(2,1)S(1)}, bf16[512,128]{1,0:T(8,128)(2,1)}, u32[]{:S(2)}) copy-start(bf16[512,128]{1,0:T(8,128)(2,1)} %get-tuple-element.24.refs_4_) | copy-start | bytes 393220
  16.9 0.7 copy-start.6
  17.6 3.1 %copy-start.5 = (bf16[256,256]{1,0:T(8,128)(2,1)S(1)}, bf16[256,256]{1,0:T(8,128)(2,1)}, u32[]{:S(2)}) copy-start(bf16[256,256]{1,0:T(8,128)(2,1)} %refs_4_.1) | copy-start | bytes 393220
  21.4 1.6 %collective-permute-start.8 = (bf16[512,256]{1,0:T(8,128)(2,1)S(1)}, bf16[512,256]{1,0:T(8,128)(2,1)S(1)}, u32[]{:S(2)}, u32[]{:S(2)}) collective-permute-start(bf16[512,256]{1,0:T(8,128)(2,1)S(1)} %get-tuple-element.26), channel_id=1, source_target_pairs={{0,1},{1,0},{2,3},{3,2},{4,5},{5,4},{6,7},{7,6},{8,9},{9,8},{10,11... | collective-permute-start | bytes 786440 | tf_op jit(solution)/shard_map/ppermute | solution.py:399
  21.5 23.7 %copy-start.3 = (s32[3,2048]{1,0:T(4,128)S(1)}, s32[3,2048]{1,0:T(4,128)}, u32[]{:S(2)}) copy-start(s32[3,2048]{1,0:T(4,128)} %wave_ref.1) | copy-start | bytes 73732
  21.5 23.7 %copy-start.11 = (f32[256]{0:T(256)S(1)}, f32[256]{0:T(256)}, u32[]{:S(2)}) copy-start(f32[256]{0:T(256)} %param.17) | copy-start | bytes 3076
  21.9 28.5 %copy-start.7 = (f32[3,256]{1,0:T(4,128)S(1)}, f32[3,256]{1,0:T(4,128)}, u32[]{:S(2)}) copy-start(f32[3,256]{1,0:T(4,128)} %get-tuple-element.18.refs_4_.p1.refs_0_) | copy-start | bytes 9220
  46.0 17.6 %all-to-all-start.1 = ((bf16[32,16,256]{2,1,0:T(8,128)(2,1)}), bf16[32,16,256]{2,1,0:T(8,128)(2,1)S(1)}, u32[]{:S(2)}, u32[]{:S(2)}) async-start(bf16[32,16,256]{2,1,0:T(8,128)(2,1)} %shard_map.127), calls=%async_computation.1 | async-start | bytes 524288 | tf_op jit(solution)/shard_map/all_to_all | solution.py:429
  50.5 15.4 %collective-permute-start.4 = (bf16[3,288,256]{2,1,0:T(8,128)(2,1)S(1)}, bf16[3,288,256]{2,1,0:T(8,128)(2,1)}, u32[]{:S(2)}, u32[]{:S(2)}) collective-permute-start(bf16[3,288,256]{2,1,0:T(8,128)(2,1)S(1)} %shard_map.119), channel_id=1, source_target_pairs={{63,0},{0,1},{1,2},{2,3},{3,4},{4,5},{5,6},{6,7},{7,8},{8,9},{9,10... | collective-permute-start | bytes 1327112 | tf_op jit(solution)/shard_map/ppermute | solution.py:359
  50.6 15.4 %collective-permute-start.5 = (bf16[3,288,256]{2,1,0:T(8,128)(2,1)S(1)}, bf16[3,288,256]{2,1,0:T(8,128)(2,1)}, u32[]{:S(2)}, u32[]{:S(2)}) collective-permute-start(bf16[3,288,256]{2,1,0:T(8,128)(2,1)S(1)} %shard_map.119), channel_id=1, source_target_pairs={{1,0},{2,1},{3,2},{4,3},{5,4},{6,5},{7,6},{8,7},{9,8},{10,9},{11,1... | collective-permute-start | bytes 1327112 | tf_op jit(solution)/shard_map/ppermute | solution.py:359
  63.6 2.3 %copy-start.4 = (bf16[256,256]{1,0:T(8,128)(2,1)S(1)}, bf16[256,256]{1,0:T(8,128)(2,1)}, u32[]{:S(2)}) copy-start(bf16[256,256]{1,0:T(8,128)(2,1)} %win_ref.1) | copy-start | bytes 393220
  63.6 2.3 %copy-start.8 = (s32[1,1,32,256]{3,2,1,0:T(8,128)S(1)}, s32[1,1,32,256]{3,2,1,0:T(8,128)}, u32[]{:S(2)}) copy-start(s32[1,1,32,256]{3,2,1,0:T(8,128)} %param.14) | copy-start | bytes 98308
  63.6 2.3 %copy-start.9 = (s32[1,1,32,256]{3,2,1,0:T(8,128)S(1)}, s32[1,1,32,256]{3,2,1,0:T(8,128)}, u32[]{:S(2)}) copy-start(s32[1,1,32,256]{3,2,1,0:T(8,128)} %param.15) | copy-start | bytes 98308
  63.6 2.3 %copy-start.10 = (bf16[64,256]{1,0:T(8,128)(2,1)S(1)}, bf16[64,256]{1,0:T(8,128)(2,1)}, u32[]{:S(2)}) copy-start(bf16[64,256]{1,0:T(8,128)(2,1)} %wrbf_ref.1) | copy-start | bytes 98308
  63.6 2.3 %copy-start.12 = (f32[256]{0:T(256)S(1)}, f32[256]{0:T(256)}, u32[]{:S(2)}) copy-start(f32[256]{0:T(256)} %param.21) | copy-start | bytes 3076
  63.6 4.9 %collective-permute-start.9 = (bf16[512,256]{1,0:T(8,128)(2,1)S(1)}, bf16[512,256]{1,0:T(8,128)(2,1)S(1)}, u32[]{:S(2)}, u32[]{:S(2)}) collective-permute-start(bf16[512,256]{1,0:T(8,128)(2,1)S(1)} %bitcast.16), channel_id=1, source_target_pairs={{0,1},{1,0},{2,3},{3,2},{4,5},{5,4},{6,7},{7,6},{8,9},{9,8},{10,11... | collective-permute-start | bytes 786440 | tf_op jit(solution)/shard_map/ppermute | solution.py:432
  64.4 11.4 %copy-start.13 = (bf16[256,256]{1,0:T(8,128)(2,1)S(1)}, bf16[256,256]{1,0:T(8,128)(2,1)}, u32[]{:S(2)}) copy-start(bf16[256,256]{1,0:T(8,128)(2,1)} %wf_ref.1) | copy-start | bytes 393220
  69.3 18.2 %collective-permute-start.10 = (bf16[256,256]{1,0:T(8,128)(2,1)S(1)}, bf16[256,256]{1,0:T(8,128)(2,1)S(1)}, u32[]{:S(2)}, u32[]{:S(2)}) collective-permute-start(bf16[256,256]{1,0:T(8,128)(2,1)S(1)} %get-tuple-element.28), channel_id=1, source_target_pairs={{192,0},{0,64},{64,128},{128,192},{193,1},{1,65},{65,129},{129,193... | collective-permute-start | bytes 393224 | tf_op jit(solution)/shard_map/ppermute | solution.py:356
  70.4 17.2 %collective-permute-start.11 = (bf16[256,256]{1,0:T(8,128)(2,1)S(1)}, bf16[256,256]{1,0:T(8,128)(2,1)S(1)}, u32[]{:S(2)}, u32[]{:S(2)}) collective-permute-start(bf16[256,256]{1,0:T(8,128)(2,1)S(1)} %get-tuple-element.29), channel_id=1, source_target_pairs={{64,0},{128,64},{192,128},{0,192},{65,1},{129,65},{193,129},{1,193... | collective-permute-start | bytes 393224 | tf_op jit(solution)/shard_map/ppermute | solution.py:356
  71.4 16.1 %collective-permute-start.12 = (bf16[256,256]{1,0:T(8,128)(2,1)S(1)}, bf16[256,256]{1,0:T(8,128)(2,1)S(1)}, u32[]{:S(2)}, u32[]{:S(2)}) collective-permute-start(bf16[256,256]{1,0:T(8,128)(2,1)S(1)} %get-tuple-element.30), channel_id=1, source_target_pairs={{128,0},{192,64},{0,128},{64,192},{129,1},{193,65},{1,129},{65,193... | collective-permute-start | bytes 393224 | tf_op jit(solution)/shard_map/ppermute | solution.py:356
  75.8 11.7 %copy-start.1 = (bf16[256,256]{1,0:T(8,128)(2,1)S(1)}, bf16[256,256]{1,0:T(8,128)(2,1)}, u32[]{:S(2)}) copy-start(bf16[256,256]{1,0:T(8,128)(2,1)} %wout_ref.1) | copy-start | bytes 393220

commit v6 on v5

--- a/solution.py
+++ b/solution.py
@@ -13,13 +13,7 @@
 soft_sq = 0.01
 damping = 64.0
 ewald_scale = 0.25
-SINE = (
-    3.1415925800428712,
-    -5.16770687881004,
-    2.550031375353375,
-    -0.5980451625033413,
-    0.07722010591476362,
-)
+SINE = (3.1415820220239103, -5.167142791318864, 2.541898979237898, -0.5546360684015085)
 COSINE = (
     0.9999999534655706,
     -4.934792858503339,
@@ -193,8 +187,8 @@
 
 
 def prepare_kernel(
-    r0, r1, r2, low_ref, high_ref, p0, p1, p2, slots_ref, images_ref, win_ref, wrbf_ref, brbf_ref,
-    table, cols, pairs, bias, row_at, pos, turned,
+    r0, r1, r2, low_ref, high_ref, p0, p1, p2, slots_ref, images_ref, win_ref, wrbf_ref, brbf_ref, wf_ref,
+    table, cols, pairs, bias, row_at, wf_out, pos, turned,
 ):
     basis_count, width = wrbf_ref.shape
     pairs[...] = jnp.zeros_like(pairs)
@@ -224,6 +218,7 @@
                 ]
             pos[0:3, brick * atoms : (brick + 1) * atoms] = place
     row_at[...] = slots_ref[...] * halves
+    wf_out[...] = wf_ref[...]
     table[halves * 9 * atoms :, :] = jnp.zeros((table.shape[0] - halves * 9 * atoms, lane), jnp.float32)
     for half in range(atoms // lane):
         cut = slice(half * lane, (half + 1) * lane)
@@ -255,18 +250,17 @@
     cols[...] = turned[...].T.astype(jnp.bfloat16)
 
 
-def short_kernel(
-    scale, cols_ref, table, row_at, pairs, bias, wf_ref, out_ref, near_a, near_b, at_a, at_b, sems
-):
+def short_kernel(start, count, scale, cols_ref, table, row_at, pairs, bias, wf_ref, *refs):
     lane = 128
     atoms = cols_ref.shape[0]
     slots = cols_ref.shape[1] // 4
     basis_count, width = pairs.shape[0] // 2, wf_ref.shape[1]
     halves = width // lane
+    *before, out_ref, near_a, near_b, at_a, at_b, sems = refs
     group = near_a.shape[0] // (halves * atoms)
     ahead = at_a.shape[0]
     wide_lanes = group // 2 * lane
-    out_ref[...] = jnp.zeros_like(out_ref)
+    out_ref[...] = before[0][...] if before else jnp.zeros_like(out_ref)
     row = lax.broadcasted_iota(jnp.int32, (lane, wide_lanes), 0)
     column = lax.broadcasted_iota(jnp.int32, (lane, wide_lanes), 1)
     source = jnp.where(row < 3 * slots, (row & (slots - 1)) - (column >> 6), -lane)
@@ -307,23 +301,23 @@
         one_group(first, buffer, 0, near_a)
         one_group(first + group, buffer, group, near_b)
 
-    fetch(0, at_a, sems.at[0]).start()
+    fetch(start, at_a, sems.at[0]).start()
 
     def body(j, carry):
-        first = 2 * ahead * j
+        first = start + 2 * ahead * j
         fetch(first, at_a, sems.at[0]).wait()
         fetch(first + ahead, at_b, sems.at[1]).start()
         both_groups(first, at_a)
         fetch(first + ahead, at_b, sems.at[1]).wait()
 
-        @pl.when(first + 2 * ahead < slots)
+        @pl.when(first + 2 * ahead < start + count)
         def _():
             fetch(first + 2 * ahead, at_a, sems.at[0]).start()
 
         both_groups(first + ahead, at_b)
         return carry
 
-    lax.fori_loop(0, slots // (2 * ahead), body, 0)
+    lax.fori_loop(0, count // (2 * ahead), body, 0)
     out_ref[...] = out_ref[...] * scale
 
 
@@ -373,11 +367,12 @@
             pltpu.SemaphoreType.DMA((2,)),
         ],
         nbytes=1 << 19,
-        grant=63.25,
         spec=[HBM] * 2,
     )
     place_of = {0: place, **{d: from_role(place, d) for d in shifts}}
-    rows_of = {0: rows, **{d: from_role(rows, d) for d in shifts}}
+    rows_of = {0: rows}
+    for d in shifts:
+        rows_of[d] = from_role(rows, d)
     by_wave = call(
         tables_kernel,
         jax.ShapeDtypeStruct((2 * share, roles * atoms), bf16),
@@ -440,7 +435,7 @@
         nbytes=1 << 20,
     )
     low, high = from_column(bundle, columns - 1), from_column(bundle, 1)
-    table, cols, pairs, bias, row_at = call(
+    table, cols, pairs, bias, row_at, filter_weight = call(
         prepare_kernel,
         [
             jax.ShapeDtypeStruct((9 * atoms * width // 128 + 16, 128), f32),
@@ -448,26 +443,34 @@
             jax.ShapeDtypeStruct((2 * w_rbf.shape[0], 2 * width), bf16),
             jax.ShapeDtypeStruct((1, 2 * width), f32),
             jax.ShapeDtypeStruct((slots, atoms), jnp.int32),
+            jax.ShapeDtypeStruct((width, width), bf16),
         ],
         [rows_of[d] for d in triple]
         + [low, high]
         + [place_of[d] for d in triple]
-        + [neighbours[0, 0], images[0, 0], w_in, w_rbf, b_rbf[None, :]],
+        + [neighbours[0, 0], images[0, 0], w_in, w_rbf, b_rbf[None, :], w_filter],
         scratch=[pltpu.VMEM((8, 9 * atoms), f32), pltpu.VMEM((4 * slots, atoms), f32)],
         flops=2 * 9 * atoms * width * width,
         nbytes=4 << 20,
     )
     near = pltpu.VMEM((4 * atoms * width // 128, 128), f32)
-    short = call(
-        functools.partial(short_kernel, slots ** (-0.5)),
-        jax.ShapeDtypeStruct((atoms, width), f32),
-        [cols, table, row_at, pairs, bias, w_filter],
-        scratch=[near, near]
-        + [pltpu.SMEM((8, atoms), jnp.int32)] * 2
-        + [pltpu.SemaphoreType.DMA((2,))],
-        flops=4 * slots * atoms * width * width,
-        nbytes=4 << 20,
-    )
+    short = ()
+    for i in range(2):
+        short = (
+            call(
+                functools.partial(
+                    short_kernel, i * slots // 2, slots // 2, slots ** (-0.5) if i else 1.0
+                ),
+                jax.ShapeDtypeStruct((atoms, width), f32),
+                [cols, table, row_at, pairs, bias, filter_weight, *short],
+                scratch=[near, near]
+                + [pltpu.SMEM((8, atoms), jnp.int32)] * 2
+                + [pltpu.SemaphoreType.DMA((2,))],
+                flops=2 * slots * atoms * width * width,
+                nbytes=4 << 20,
+            ),
+        )
+    short = short[0]
     parts = call(
         ewald_kernel,
         [jax.ShapeDtypeStruct((atoms, width), bf16)] * roles,

time: 88.8 us -> 86.7 us (0.976)
  waiting for transfers between devices: 16.2 us -> 15.1 us
    all_to_all x1, waiting for transfers between devices: 7.97 us -> 6.78 us  [block(): lax.all_to_all(copies, 'atoms', 0, 0, axis_index_groups=same_core)]
    pallas_call x12 -> x13, Pallas kernels: 23.1 us -> 22.3 us  [call(): pl.pallas_call(body, out_shape=out, in_specs=spec or [VMEM] * len(ins), o...]
  transfers between devices with their start and end apart: 14 -> 14, of which waited for: 5 -> 5; matrix products, arithmetic and copies ran while one was open for 0% -> 0% of each run, Pallas kernels for 23% -> 22%
where the time goes in v6:
time: 86.7 us; the launch traced here: 86.3 us
  starting transfers between devices  25 us (29%)
  Pallas kernels  22.3 us (26%)
  blocking collectives  22.1 us (25%)
  waiting for transfers between devices  15.1 us (17%)
  local copies, waits for them, and re-layouts  1.49 us (2%)
    pallas_call x13, Pallas kernels, call(): pl.pallas_call(body, out_shape=out, in_specs=spec or [VMEM] * len(ins), o...  22.3 us
    all_to_all x1, blocking collectives, block(): lax.all_to_all(kept.reshape(chunks), 'atoms', 0, 0, axis_index_groups=sam...  22.1 us
    ppermute x9, starting transfers between devices, from_role(): lax.ppermute(block, 'role', [((i + shift) % roles, i) for i in range(role...  15.4 us
    all_to_all x1, waiting for transfers between devices, block(): lax.all_to_all(copies, 'atoms', 0, 0, axis_index_groups=same_core)  6.78 us
    ppermute x9, waiting for transfers between devices, from_role(): lax.ppermute(block, 'role', [((i + shift) % roles, i) for i in range(role...  5.22 us
    ppermute x2, starting transfers between devices, from_column(): lax.ppermute(block, 'atoms', [((i + shift) % columns, i) for i in range(c...  5.07 us
    all_to_all x1, starting transfers between devices, block(): lax.all_to_all(copies, 'atoms', 0, 0, axis_index_groups=same_core)  4.43 us
    ppermute x2, waiting for transfers between devices, from_column(): lax.ppermute(block, 'atoms', [((i + shift) % columns, i) for i in range(c...  2.02 us
  transfers between devices with their start and end apart: 14, of which 5 were waited for; matrix products, arithmetic and copies ran while one was open for 0% of the time, Pallas kernels for 22%

profile of v6, /device:TPU:16, one launch (start us, length us, event | category | flops | bytes accessed | tf_op | source)
XLA Modules:
  0.0 86.3 jit_solution(7939552761610903072)
XLA Ops:
  0.0 0.0 copy-start
  0.0 1.3 %collective-permute-start = (bf16[256,256]{1,0:T(8,128)(2,1)}, bf16[256,256]{1,0:T(8,128)(2,1)S(1)}, u32[]{:S(2)}, u32[]{:S(2)}) collective-permute-start(bf16[256,256]{1,0:T(8,128)(2,1)} %bitcast.9), channel_id=1, source_target_pairs={{192,0},{0,64},{64,128},{128,192},{193,1},{1,65},{65,129},{129,193... | collective-permute-start | bytes 393224 | tf_op jit(solution)/shard_map/ppermute | solution.py:350
  1.3 0.7 collective-permute-start.1
  2.0 3.3 %collective-permute-start.7 = (bf16[256,256]{1,0:T(8,128)(2,1)}, bf16[256,256]{1,0:T(8,128)(2,1)S(1)}, u32[]{:S(2)}, u32[]{:S(2)}) collective-permute-start(bf16[256,256]{1,0:T(8,128)(2,1)} %bitcast.11), channel_id=1, source_target_pairs={{128,0},{192,64},{0,128},{64,192},{129,1},{193,65},{1,129},{65,193... | collective-permute-start | bytes 393224 | tf_op jit(solution)/shard_map/ppermute | solution.py:350
  5.3 0.0 copy-start.4
  5.3 0.8 copy-done.4
  6.0 0.0 copy-start.10
  6.0 0.7 copy-done.10
  6.7 0.0 copy-start.6
  6.7 0.2 shard_map.118
  6.9 0.1 collective-permute-start.2
  7.0 2.0 %collective-permute-start.3 = (f32[3,256]{1,0:T(4,128)S(1)}, f32[3,256]{1,0:T(4,128)S(1)}, u32[]{:S(2)}, u32[]{:S(2)}) collective-permute-start(f32[3,256]{1,0:T(4,128)S(1)} %get-tuple-element.19.refs_4_.p1.refs_0_), channel_id=1, source_target_pairs={{64,0},{128,64},{192,128},{0,192},{65,1},{129,65},{193,129},{1,193... | collective-permute-start | bytes 9224 | tf_op jit(solution)/shard_map/ppermute | solution.py:350
  9.0 1.6 %collective-permute-done.2.refs_3_.p0.refs_2_ = f32[3,256]{1,0:T(4,128)S(1)} collective-permute-done((f32[3,256]{1,0:T(4,128)S(1)}, f32[3,256]{1,0:T(4,128)S(1)}, u32[]{:S(2)}, u32[]{:S(2)}) %collective-permute-start.2) | collective-permute-done | bytes 3104 | tf_op jit(solution)/shard_map/ppermute | solution.py:350
  10.6 1.5 %collective-permute-start.6 = (f32[3,256]{1,0:T(4,128)S(1)}, f32[3,256]{1,0:T(4,128)S(1)}, u32[]{:S(2)}, u32[]{:S(2)}) collective-permute-start(f32[3,256]{1,0:T(4,128)S(1)} %get-tuple-element.19.refs_4_.p1.refs_0_), channel_id=1, source_target_pairs={{128,0},{192,64},{0,128},{64,192},{129,1},{193,65},{1,129},{65,193... | collective-permute-start | bytes 9224 | tf_op jit(solution)/shard_map/ppermute | solution.py:350
  12.1 0.0 collective-permute-done.3.refs_5_.p2.refs_1_
  12.1 3.6 %collective-permute-done.6.refs_3_ = f32[3,256]{1,0:T(4,128)S(1)} collective-permute-done((f32[3,256]{1,0:T(4,128)S(1)}, f32[3,256]{1,0:T(4,128)S(1)}, u32[]{:S(2)}, u32[]{:S(2)}) %collective-permute-start.6) | collective-permute-done | bytes 3104 | tf_op jit(solution)/shard_map/ppermute | solution.py:350
  15.7 2.9 %shard_map.123.by_wave.refs_5_.table = bf16[1024,1024]{1,0:T(8,128)(2,1)S(1)} custom-call(f32[3,256]{1,0:T(4,128)S(1)} %get-tuple-element.19.refs_4_.p1.refs_0_, f32[3,256]{1,0:T(4,128)S(1)} %collective-permute-done.3.refs_5_.p2.refs_1_, f32[3,256]{1,0:T(4,128)S(1)} %collective-permute-done.2.refs_3_.p0.refs_2_, ...), custom_call_target="tpu_custom_call" | custom-call | flops 20971520 | bytes 4194304 | tf_op jit(solution)/shard_map/pallas_call | solution.py:31
  18.6 0.0 collective-permute-done.refs_0_.r0.refs_2_
  18.6 0.0 collective-permute-done.1.refs_2_.r2.refs_1_
  18.6 0.0 collective-permute-done.7.refs_3_
  18.6 0.0 copy-done
  18.6 0.0 copy-done.6
  18.6 0.7 shard_map.125
  19.3 0.1 collective-permute-start.8
  19.4 0.0 copy-start.5
  19.5 0.0 copy-start.11
  19.5 0.4 shard_map.126.own_ref
  19.9 1.1 %collective-permute-done.8.got_ref = bf16[512,256]{1,0:T(8,128)(2,1)S(1)} collective-permute-done((bf16[512,256]{1,0:T(8,128)(2,1)S(1)}, bf16[512,256]{1,0:T(8,128)(2,1)S(1)}, u32[]{:S(2)}, u32[]{:S(2)}) %collective-permute-start.8) | collective-permute-done | bytes 262176 | tf_op jit(solution)/shard_map/ppermute | solution.py:394
  21.0 22.1 %all_to_all.10.mine_ref = bf16[32,16,256]{2,1,0:T(8,128)(2,1)S(1)} all-to-all(bf16[32,16,256]{2,1,0:T(8,128)(2,1)S(1)} %bitcast.18), channel_id=1, replica_groups={{0,2,4,6,8,10,12,14,16,18,20,22,24,26,28,30,32,34,36,38,40,42,44,46,48,..., dimensions={0} | all-to-all | bytes 524288 | tf_op jit(solution)/shard_map/all_to_all | solution.py:416
  43.1 0.0 copy-done.5
  43.1 0.0 copy-done.11
  43.1 0.8 shard_map.128
  44.0 4.4 %all-to-all-start.1 = ((bf16[32,16,256]{2,1,0:T(8,128)(2,1)}), bf16[32,16,256]{2,1,0:T(8,128)(2,1)S(1)}, u32[]{:S(2)}, u32[]{:S(2)}) async-start(bf16[32,16,256]{2,1,0:T(8,128)(2,1)} %shard_map.128), calls=%async_computation.1 | async-start | bytes 524288 | tf_op jit(solution)/shard_map/all_to_all | solution.py:424
  48.4 0.8 shard_map.119
  49.2 0.0 collective-permute-start.4
  49.2 5.1 %collective-permute-start.5 = (bf16[3,288,256]{2,1,0:T(8,128)(2,1)}, bf16[3,288,256]{2,1,0:T(8,128)(2,1)}, u32[]{:S(2)}, u32[]{:S(2)}) collective-permute-start(bf16[3,288,256]{2,1,0:T(8,128)(2,1)} %shard_map.119), channel_id=1, source_target_pairs={{1,0},{2,1},{3,2},{4,3},{5,4},{6,5},{7,6},{8,7},{9,8},{10,9},{11,1... | collective-permute-start | bytes 1327112 | tf_op jit(solution)/shard_map/ppermute | solution.py:353
  54.3 6.8 %all-to-all-done.1 = bf16[32,16,256]{2,1,0:T(8,128)(2,1)S(1)} async-done(((bf16[32,16,256]{2,1,0:T(8,128)(2,1)}), bf16[32,16,256]{2,1,0:T(8,128)(2,1)S(1)}, u32[]{:S(2)}, u32[]{:S(2)}) %all-to-all-start.1) | async-done | bytes 262176 | tf_op jit(solution)/shard_map/all_to_all | solution.py:424
  61.1 0.0 copy-start.1
  61.1 0.0 copy-start.9
  61.1 0.0 copy-start.12
  61.1 0.1 collective-permute-start.9
  61.2 0.7 shard_map.124.table_ref
  61.9 2.0 %collective-permute-done.4.low_ref = bf16[3,288,256]{2,1,0:T(8,128)(2,1)S(1)} collective-permute-done((bf16[3,288,256]{2,1,0:T(8,128)(2,1)}, bf16[3,288,256]{2,1,0:T(8,128)(2,1)S(1)}, u32[]{:S(2)}, u32[]{:S(2)}) %collective-permute-start.4) | collective-permute-done | bytes 442400 | tf_op jit(solution)/shard_map/ppermute | solution.py:353
  63.9 0.0 collective-permute-done.5.high_ref
  63.9 0.0 copy-done.1
  63.9 0.0 copy-done.2
  63.9 0.0 copy-done.7
  63.9 0.0 copy-done.8
  64.0 0.0 copy-done.9
  64.0 0.0 copy-done.12
  64.0 2.5 %shard_map.120 = (f32[4624,128]{1,0:T(8,128)S(1)}, bf16[256,128]{1,0:T(8,128)(2,1)S(1)}, bf16[128,512]{1,0:T(8,128)(2,1)S(1)}, f32[1,512]{1,0:T(1,128)S(1)}, s32...) custom-call(bf16[256,256]{1,0:T(8,128)(2,1)S(1)} %collective-permute-done.refs_0_.r0.refs_2_, ...), custom_call_target="tpu_custom_call" | custom-call | flops 301989888 | bytes 4194304 | tf_op jit(solution)/shard_map/pallas_call | solution.py:31
  66.4 0.0 collective-permute-done.9.other_ref
  66.4 0.7 shard_map.129
  67.2 1.0 %collective-permute-start.10 = (bf16[256,256]{1,0:T(8,128)(2,1)S(1)}, bf16[256,256]{1,0:T(8,128)(2,1)S(1)}, u32[]{:S(2)}, u32[]{:S(2)}) collective-permute-start(bf16[256,256]{1,0:T(8,128)(2,1)S(1)} %get-tuple-element.30), channel_id=1, source_target_pairs={{192,0},{0,64},{64,128},{128,192},{193,1},{1,65},{65,129},{129,193... | collective-permute-start | bytes 393224 | tf_op jit(solution)/shard_map/ppermute | solution.py:350
  68.2 1.1 %collective-permute-start.11 = (bf16[256,256]{1,0:T(8,128)(2,1)S(1)}, bf16[256,256]{1,0:T(8,128)(2,1)S(1)}, u32[]{:S(2)}, u32[]{:S(2)}) collective-permute-start(bf16[256,256]{1,0:T(8,128)(2,1)S(1)} %get-tuple-element.31), channel_id=1, source_target_pairs={{64,0},{128,64},{192,128},{0,192},{65,1},{129,65},{193,129},{1,193... | collective-permute-start | bytes 393224 | tf_op jit(solution)/shard_map/ppermute | solution.py:350
  69.3 4.4 %collective-permute-start.12 = (bf16[256,256]{1,0:T(8,128)(2,1)S(1)}, bf16[256,256]{1,0:T(8,128)(2,1)S(1)}, u32[]{:S(2)}, u32[]{:S(2)}) collective-permute-start(bf16[256,256]{1,0:T(8,128)(2,1)S(1)} %get-tuple-element.32), channel_id=1, source_target_pairs={{128,0},{192,64},{0,128},{64,192},{129,1},{193,65},{1,129},{65,193... | collective-permute-start | bytes 393224 | tf_op jit(solution)/shard_map/ppermute | solution.py:350
  73.7 5.8 %shard_map.121.refs_0_ = f32[256,256]{1,0:T(8,128)S(1)} custom-call(bf16[256,128]{1,0:T(8,128)(2,1)S(1)} %get-tuple-element.20.cols_ref, f32[4624,128]{1,0:T(8,128)S(1)} %get-tuple-element.21.table, s32[32,256]{1,0:T(8,128)S(1)} %get-tuple-element.22.row_at, bf16[128,512]{1,0:T(8,128)(2,1)S(1)} %get-tuple-element.23.pairs, ...), custom_call_target="tpu_custom_call" | custom-call | flops 1073741824 | bytes 4194304 | tf_op jit(solution)/shard_map/pallas_call | solution.py:31
  79.5 0.0 copy-start.3
  79.5 5.9 %shard_map.122.short_ref = f32[256,256]{1,0:T(8,128)S(1)} custom-call(bf16[256,128]{1,0:T(8,128)(2,1)S(1)} %get-tuple-element.20.cols_ref, f32[4624,128]{1,0:T(8,128)S(1)} %get-tuple-element.21.table, s32[32,256]{1,0:T(8,128)S(1)} %get-tuple-element.22.row_at, bf16[128,512]{1,0:T(8,128)(2,1)S(1)} %get-tuple-element.23.pairs, ...), custom_call_target="tpu_custom_call" | custom-call | flops 1073741824 | bytes 4194304 | tf_op jit(solution)/shard_map/pallas_call | solution.py:31
  85.4 0.0 collective-permute-done.10.e1_ref
  85.4 0.0 collective-permute-done.11.e2_ref
  85.4 0.0 collective-permute-done.12.e3_ref
  85.4 0.0 copy-done.3
  85.5 0.9 %shard_map.130 = bf16[256,256]{1,0:T(8,128)(2,1)} custom-call(bf16[256,256]{1,0:T(8,128)(2,1)S(1)} %bitcast.15, f32[256,256]{1,0:T(8,128)S(1)} %shard_map.122.short_ref, bf16[256,256]{1,0:T(8,128)(2,1)S(1)} %get-tuple-element.29.e0_ref, bf16[256,256]{1,0:T(8,128)(2,1)S(1)} %collective-permute-done.10.e1_ref, ...), custom_call_target="tpu_custom_call" | custom-call | flops 33554432 | bytes 1048576 | tf_op jit(solution)/shard_map/pallas_call | solution.py:31
  (4 shorter events, 0.1 us)
Async XLA Ops:
  0.0 18.6 %copy-start = (bf16[1,1,256,256]{3,2,1,0:T(8,128)(2,1)S(1)}, bf16[1,1,256,256]{3,2,1,0:T(8,128)(2,1)}, u32[]{:S(2)}) copy-start(bf16[1,1,256,256]{3,2,1,0:T(8,128)(2,1)} %param.12) | copy-start | bytes 393220
  0.0 18.6 %collective-permute-start = (bf16[256,256]{1,0:T(8,128)(2,1)}, bf16[256,256]{1,0:T(8,128)(2,1)S(1)}, u32[]{:S(2)}, u32[]{:S(2)}) collective-permute-start(bf16[256,256]{1,0:T(8,128)(2,1)} %bitcast.9), channel_id=1, source_target_pairs={{192,0},{0,64},{64,128},{128,192},{193,1},{1,65},{65,129},{129,193... | collective-permute-start | bytes 393224 | tf_op jit(solution)/shard_map/ppermute | solution.py:350
  1.3 17.3 %collective-permute-start.1 = (bf16[256,256]{1,0:T(8,128)(2,1)}, bf16[256,256]{1,0:T(8,128)(2,1)S(1)}, u32[]{:S(2)}, u32[]{:S(2)}) collective-permute-start(bf16[256,256]{1,0:T(8,128)(2,1)} %bitcast.10), channel_id=1, source_target_pairs={{64,0},{128,64},{192,128},{0,192},{65,1},{129,65},{193,129},{1,193... | collective-permute-start | bytes 393224 | tf_op jit(solution)/shard_map/ppermute | solution.py:350
  2.0 16.6 %collective-permute-start.7 = (bf16[256,256]{1,0:T(8,128)(2,1)}, bf16[256,256]{1,0:T(8,128)(2,1)S(1)}, u32[]{:S(2)}, u32[]{:S(2)}) collective-permute-start(bf16[256,256]{1,0:T(8,128)(2,1)} %bitcast.11), channel_id=1, source_target_pairs={{128,0},{192,64},{0,128},{64,192},{129,1},{193,65},{1,129},{65,193... | collective-permute-start | bytes 393224 | tf_op jit(solution)/shard_map/ppermute | solution.py:350
  5.3 0.8 copy-start.4
  6.0 0.7 copy-start.10
  6.7 11.9 %copy-start.6 = (bf16[256,256]{1,0:T(8,128)(2,1)S(1)}, bf16[256,256]{1,0:T(8,128)(2,1)}, u32[]{:S(2)}) copy-start(bf16[256,256]{1,0:T(8,128)(2,1)} %refs_4_.1) | copy-start | bytes 393220
  6.9 3.7 %collective-permute-start.2 = (f32[3,256]{1,0:T(4,128)S(1)}, f32[3,256]{1,0:T(4,128)S(1)}, u32[]{:S(2)}, u32[]{:S(2)}) collective-permute-start(f32[3,256]{1,0:T(4,128)S(1)} %get-tuple-element.19.refs_4_.p1.refs_0_), channel_id=1, source_target_pairs={{192,0},{0,64},{64,128},{128,192},{193,1},{1,65},{65,129},{129,193... | collective-permute-start | bytes 9224 | tf_op jit(solution)/shard_map/ppermute | solution.py:350
  7.0 5.1 %collective-permute-start.3 = (f32[3,256]{1,0:T(4,128)S(1)}, f32[3,256]{1,0:T(4,128)S(1)}, u32[]{:S(2)}, u32[]{:S(2)}) collective-permute-start(f32[3,256]{1,0:T(4,128)S(1)} %get-tuple-element.19.refs_4_.p1.refs_0_), channel_id=1, source_target_pairs={{64,0},{128,64},{192,128},{0,192},{65,1},{129,65},{193,129},{1,193... | collective-permute-start | bytes 9224 | tf_op jit(solution)/shard_map/ppermute | solution.py:350
  10.6 5.1 %collective-permute-start.6 = (f32[3,256]{1,0:T(4,128)S(1)}, f32[3,256]{1,0:T(4,128)S(1)}, u32[]{:S(2)}, u32[]{:S(2)}) collective-permute-start(f32[3,256]{1,0:T(4,128)S(1)} %get-tuple-element.19.refs_4_.p1.refs_0_), channel_id=1, source_target_pairs={{128,0},{192,64},{0,128},{64,192},{129,1},{193,65},{1,129},{65,193... | collective-permute-start | bytes 9224 | tf_op jit(solution)/shard_map/ppermute | solution.py:350
  19.3 1.6 %collective-permute-start.8 = (bf16[512,256]{1,0:T(8,128)(2,1)S(1)}, bf16[512,256]{1,0:T(8,128)(2,1)S(1)}, u32[]{:S(2)}, u32[]{:S(2)}) collective-permute-start(bf16[512,256]{1,0:T(8,128)(2,1)S(1)} %get-tuple-element.28), channel_id=1, source_target_pairs={{0,1},{1,0},{2,3},{3,2},{4,5},{5,4},{6,7},{7,6},{8,9},{9,8},{10,11... | collective-permute-start | bytes 786440 | tf_op jit(solution)/shard_map/ppermute | solution.py:394
  19.4 23.7 %copy-start.5 = (s32[3,2048]{1,0:T(4,128)S(1)}, s32[3,2048]{1,0:T(4,128)}, u32[]{:S(2)}) copy-start(s32[3,2048]{1,0:T(4,128)} %wave_ref.1) | copy-start | bytes 73732
  19.5 23.7 %copy-start.11 = (f32[256]{0:T(256)S(1)}, f32[256]{0:T(256)}, u32[]{:S(2)}) copy-start(f32[256]{0:T(256)} %param.17) | copy-start | bytes 3076
  44.0 17.1 %all-to-all-start.1 = ((bf16[32,16,256]{2,1,0:T(8,128)(2,1)}), bf16[32,16,256]{2,1,0:T(8,128)(2,1)S(1)}, u32[]{:S(2)}, u32[]{:S(2)}) async-start(bf16[32,16,256]{2,1,0:T(8,128)(2,1)} %shard_map.128), calls=%async_computation.1 | async-start | bytes 524288 | tf_op jit(solution)/shard_map/all_to_all | solution.py:424
  49.2 14.7 %collective-permute-start.4 = (bf16[3,288,256]{2,1,0:T(8,128)(2,1)}, bf16[3,288,256]{2,1,0:T(8,128)(2,1)S(1)}, u32[]{:S(2)}, u32[]{:S(2)}) collective-permute-start(bf16[3,288,256]{2,1,0:T(8,128)(2,1)} %shard_map.119), channel_id=1, source_target_pairs={{63,0},{0,1},{1,2},{2,3},{3,4},{4,5},{5,6},{6,7},{7,8},{8,9},{9,10... | collective-permute-start | bytes 1327112 | tf_op jit(solution)/shard_map/ppermute | solution.py:353
  49.2 14.7 %collective-permute-start.5 = (bf16[3,288,256]{2,1,0:T(8,128)(2,1)}, bf16[3,288,256]{2,1,0:T(8,128)(2,1)}, u32[]{:S(2)}, u32[]{:S(2)}) collective-permute-start(bf16[3,288,256]{2,1,0:T(8,128)(2,1)} %shard_map.119), channel_id=1, source_target_pairs={{1,0},{2,1},{3,2},{4,3},{5,4},{6,5},{7,6},{8,7},{9,8},{10,9},{11,1... | collective-permute-start | bytes 1327112 | tf_op jit(solution)/shard_map/ppermute | solution.py:353
  61.1 2.8 %copy-start.1 = (bf16[256,256]{1,0:T(8,128)(2,1)S(1)}, bf16[256,256]{1,0:T(8,128)(2,1)}, u32[]{:S(2)}) copy-start(bf16[256,256]{1,0:T(8,128)(2,1)} %win_ref.1) | copy-start | bytes 393220
  61.1 2.8 %copy-start.2 = (bf16[256,256]{1,0:T(8,128)(2,1)S(1)}, bf16[256,256]{1,0:T(8,128)(2,1)}, u32[]{:S(2)}) copy-start(bf16[256,256]{1,0:T(8,128)(2,1)} %wf_ref.1) | copy-start | bytes 393220
  61.1 2.8 %copy-start.7 = (s32[1,1,32,256]{3,2,1,0:T(8,128)S(1)}, s32[1,1,32,256]{3,2,1,0:T(8,128)}, u32[]{:S(2)}) copy-start(s32[1,1,32,256]{3,2,1,0:T(8,128)} %param.14) | copy-start | bytes 98308
  61.1 2.9 %copy-start.8 = (s32[1,1,32,256]{3,2,1,0:T(8,128)S(1)}, s32[1,1,32,256]{3,2,1,0:T(8,128)}, u32[]{:S(2)}) copy-start(s32[1,1,32,256]{3,2,1,0:T(8,128)} %param.15) | copy-start | bytes 98308
  61.1 2.9 %copy-start.9 = (bf16[64,256]{1,0:T(8,128)(2,1)S(1)}, bf16[64,256]{1,0:T(8,128)(2,1)}, u32[]{:S(2)}) copy-start(bf16[64,256]{1,0:T(8,128)(2,1)} %wrbf_ref.1) | copy-start | bytes 98308
  61.1 2.9 %copy-start.12 = (f32[256]{0:T(256)S(1)}, f32[256]{0:T(256)}, u32[]{:S(2)}) copy-start(f32[256]{0:T(256)} %param.21) | copy-start | bytes 3076
  61.1 5.3 %collective-permute-start.9 = (bf16[512,256]{1,0:T(8,128)(2,1)S(1)}, bf16[512,256]{1,0:T(8,128)(2,1)S(1)}, u32[]{:S(2)}, u32[]{:S(2)}) collective-permute-start(bf16[512,256]{1,0:T(8,128)(2,1)S(1)} %bitcast.16), channel_id=1, source_target_pairs={{0,1},{1,0},{2,3},{3,2},{4,5},{5,4},{6,7},{7,6},{8,9},{9,8},{10,11... | collective-permute-start | bytes 786440 | tf_op jit(solution)/shard_map/ppermute | solution.py:427
  67.2 18.2 %collective-permute-start.10 = (bf16[256,256]{1,0:T(8,128)(2,1)S(1)}, bf16[256,256]{1,0:T(8,128)(2,1)S(1)}, u32[]{:S(2)}, u32[]{:S(2)}) collective-permute-start(bf16[256,256]{1,0:T(8,128)(2,1)S(1)} %get-tuple-element.30), channel_id=1, source_target_pairs={{192,0},{0,64},{64,128},{128,192},{193,1},{1,65},{65,129},{129,193... | collective-permute-start | bytes 393224 | tf_op jit(solution)/shard_map/ppermute | solution.py:350
  68.2 17.2 %collective-permute-start.11 = (bf16[256,256]{1,0:T(8,128)(2,1)S(1)}, bf16[256,256]{1,0:T(8,128)(2,1)S(1)}, u32[]{:S(2)}, u32[]{:S(2)}) collective-permute-start(bf16[256,256]{1,0:T(8,128)(2,1)S(1)} %get-tuple-element.31), channel_id=1, source_target_pairs={{64,0},{128,64},{192,128},{0,192},{65,1},{129,65},{193,129},{1,193... | collective-permute-start | bytes 393224 | tf_op jit(solution)/shard_map/ppermute | solution.py:350
  69.3 16.2 %collective-permute-start.12 = (bf16[256,256]{1,0:T(8,128)(2,1)S(1)}, bf16[256,256]{1,0:T(8,128)(2,1)S(1)}, u32[]{:S(2)}, u32[]{:S(2)}) collective-permute-start(bf16[256,256]{1,0:T(8,128)(2,1)S(1)} %get-tuple-element.32), channel_id=1, source_target_pairs={{128,0},{192,64},{0,128},{64,192},{129,1},{193,65},{1,129},{65,193... | collective-permute-start | bytes 393224 | tf_op jit(solution)/shard_map/ppermute | solution.py:350
  79.5 5.9 %copy-start.3 = (bf16[256,256]{1,0:T(8,128)(2,1)S(1)}, bf16[256,256]{1,0:T(8,128)(2,1)}, u32[]{:S(2)}) copy-start(bf16[256,256]{1,0:T(8,128)(2,1)} %wout_ref.1) | copy-start | bytes 393220

commit v7 on v6

--- a/solution.py
+++ b/solution.py
@@ -105,10 +105,49 @@
     lax.fori_loop(0, share // step, block, 0)
 
 
-def flip_kernel(by_wave, by_atom):
-    for j in range(by_wave.shape[0] // 128):
-        part = slice(j * 128, (j + 1) * 128)
-        by_atom[:, part] = by_wave[part, :].T
+def again_kernel(*refs):
+    pos_refs, (wave_ref, by_atom, flat, pos, parts) = refs[:4], refs[4:]
+    atoms = pos_refs[0].shape[1]
+    columns = by_atom.shape[1]
+    share = columns // 2
+    first = pl.multiple_of(lax.axis_index("role") * share, 128)
+    waves = wave_ref[:, pl.ds(first, share)].astype(jnp.float32)
+    flat[...] = jnp.zeros_like(flat)
+    pos[...] = jnp.zeros_like(pos)
+    for k in range(3):
+        flat[3 * k : 3 * k + 3, :] = waves
+    pos[9:10, :] = jnp.ones((1, pos.shape[1]), jnp.float32)
+    for i, ref in enumerate(pos_refs):
+        rest = ref[...]
+        for k in range(3):
+            rounded = rest.astype(jnp.bfloat16).astype(jnp.float32)
+            pos[3 * k : 3 * k + 3, i * atoms : (i + 1) * atoms] = rounded
+            rest = rest - rounded
+    for i in range(pos.shape[1] // 128):
+        part = slice(i * 128, (i + 1) * 128)
+        parts[part, :] = pos[:, part].T.astype(jnp.bfloat16)
+    row = lax.broadcasted_iota(jnp.int32, (share, columns), 0)
+    lane = lax.broadcasted_iota(jnp.int32, (share, columns), 1)
+    pick = (row == (lane >> 4) * 8 + (lane & 7)).astype(jnp.float32).astype(jnp.bfloat16)
+    spread = dot(flat[...].astype(jnp.bfloat16), pick)
+    row = lax.broadcasted_iota(jnp.int32, spread.shape, 0)
+    lane = lax.broadcasted_iota(jnp.int32, spread.shape, 1)
+    spread = jnp.where((row == 9) & ((lane & 8) != 0), -0.25, spread).astype(jnp.bfloat16)
+    step = 128
+
+    def block(j, carry):
+        part = pl.ds(pl.multiple_of(j * step, step), step)
+        turns = dot(parts[part, :], spread)
+        rest = turns - jnp.round(turns)
+        square = rest * rest
+        odd = SINE[-1]
+        for coef in SINE[-2::-1]:
+            odd = odd * square + coef
+        half = odd * rest
+        by_atom[part, :] = (1.0 - 2.0 * (half * half)).astype(jnp.bfloat16)
+        return carry
+
+    lax.fori_loop(0, pos.shape[1] // step, block, 0)
 
 
 def core_half(size, other):
@@ -188,14 +227,11 @@
 
 def prepare_kernel(
     r0, r1, r2, low_ref, high_ref, p0, p1, p2, slots_ref, images_ref, win_ref, wrbf_ref, brbf_ref, wf_ref,
-    table, cols, pairs, bias, row_at, wf_out, pos, turned,
+    table, cols, row_at, wrbf_out, brbf_out, wf_out, pos, turned,
 ):
-    basis_count, width = wrbf_ref.shape
-    pairs[...] = jnp.zeros_like(pairs)
-    pairs[0:basis_count, 0:width] = wrbf_ref[...]
-    pairs[basis_count:, width:] = wrbf_ref[...]
-    bias[:, 0:width] = brbf_ref[...] * math.log2(math.e)
-    bias[:, width:] = brbf_ref[...] * math.log2(math.e)
+    width = wf_ref.shape[1]
+    wrbf_out[...] = wrbf_ref[...]
+    brbf_out[...] = brbf_ref[...]
     lane = 128
     halves = width // lane
     slots, atoms = slots_ref.shape
@@ -250,13 +286,18 @@
     cols[...] = turned[...].T.astype(jnp.bfloat16)
 
 
-def short_kernel(start, count, scale, cols_ref, table, row_at, pairs, bias, wf_ref, *refs):
+def short_kernel(start, count, scale, cols_ref, table, row_at, wrbf_ref, brbf_ref, wf_ref, *refs):
     lane = 128
     atoms = cols_ref.shape[0]
     slots = cols_ref.shape[1] // 4
-    basis_count, width = pairs.shape[0] // 2, wf_ref.shape[1]
+    basis_count, width = wrbf_ref.shape
     halves = width // lane
-    *before, out_ref, near_a, near_b, at_a, at_b, sems = refs
+    *before, out_ref, near_a, near_b, at_a, at_b, pairs, bias, sems = refs
+    pairs[...] = jnp.zeros_like(pairs)
+    pairs[0:basis_count, 0:width] = wrbf_ref[...]
+    pairs[basis_count:, width:] = wrbf_ref[...]
+    bias[:, 0:width] = brbf_ref[...] * math.log2(math.e)
+    bias[:, width:] = brbf_ref[...] * math.log2(math.e)
     group = near_a.shape[0] // (halves * atoms)
     ahead = at_a.shape[0]
     wide_lanes = group // 2 * lane
@@ -407,10 +448,16 @@
         nbytes=1 << 20,
     )
     by_atom = call(
-        flip_kernel,
+        again_kernel,
         jax.ShapeDtypeStruct((roles * atoms, 2 * share), bf16),
-        [by_wave],
-        nbytes=4 << 20,
+        [place_of[d] for d in order] + [wave],
+        scratch=[
+            pltpu.VMEM((128, share), f32),
+            pltpu.VMEM((128, roles * atoms), f32),
+            pltpu.VMEM((roles * atoms, 128), bf16),
+        ],
+        flops=40 * share * roles * atoms,
+        nbytes=2 << 20,
     )
     chunks = (columns // 2, 2 * piece, width)
     mine = lax.all_to_all(kept.reshape(chunks), "atoms", 0, 0, axis_index_groups=same_core)
@@ -435,14 +482,14 @@
         nbytes=1 << 20,
     )
     low, high = from_column(bundle, columns - 1), from_column(bundle, 1)
-    table, cols, pairs, bias, row_at, filter_weight = call(
+    table, cols, row_at, *held = call(
         prepare_kernel,
         [
             jax.ShapeDtypeStruct((9 * atoms * width // 128 + 16, 128), f32),
             jax.ShapeDtypeStruct((atoms, 4 * slots), bf16),
-            jax.ShapeDtypeStruct((2 * w_rbf.shape[0], 2 * width), bf16),
-            jax.ShapeDtypeStruct((1, 2 * width), f32),
             jax.ShapeDtypeStruct((slots, atoms), jnp.int32),
+            jax.ShapeDtypeStruct(w_rbf.shape, bf16),
+            jax.ShapeDtypeStruct((1, width), f32),
             jax.ShapeDtypeStruct((width, width), bf16),
         ],
         [rows_of[d] for d in triple]
@@ -462,9 +509,15 @@
                     short_kernel, i * slots // 2, slots // 2, slots ** (-0.5) if i else 1.0
                 ),
                 jax.ShapeDtypeStruct((atoms, width), f32),
-                [cols, table, row_at, pairs, bias, filter_weight, *short],
+                [cols, table, row_at]
+                + ([w_rbf, b_rbf[None, :], w_filter] if i else held)
+                + [*short],
                 scratch=[near, near]
                 + [pltpu.SMEM((8, atoms), jnp.int32)] * 2
+                + [
+                    pltpu.VMEM((2 * w_rbf.shape[0], 2 * width), bf16),
+                    pltpu.VMEM((1, 2 * width), f32),
+                ]
                 + [pltpu.SemaphoreType.DMA((2,))],
                 flops=2 * slots * atoms * width * width,
                 nbytes=4 << 20,

time: 86.7 us -> 87.4 us (level)
  the two profiles are of different devices: /device:TPU:16 before, /device:TPU:1 now
where the time goes in v7:
time: 87.4 us; the launch traced here: 87.1 us
  starting transfers between devices  29.7 us (34%)
  Pallas kernels  23.3 us (27%)
  blocking collectives  20.5 us (23%)
  waiting for transfers between devices  11.8 us (14%)
  local copies, waits for them, and re-layouts  1.49 us (2%)
    pallas_call x13, Pallas kernels, call(): pl.pallas_call(body, out_shape=out, in_specs=spec or [VMEM] * len(ins), o...  23.3 us
    all_to_all x1, blocking collectives, block(): lax.all_to_all(kept.reshape(chunks), 'atoms', 0, 0, axis_index_groups=sam...  20.5 us
    ppermute x9, starting transfers between devices, from_role(): lax.ppermute(block, 'role', [((i + shift) % roles, i) for i in range(role...  11.2 us
    all_to_all x1, starting transfers between devices, block(): lax.all_to_all(copies, 'atoms', 0, 0, axis_index_groups=same_core)  6.71 us
    all_to_all x1, waiting for transfers between devices, block(): lax.all_to_all(copies, 'atoms', 0, 0, axis_index_groups=same_core)  6.61 us
    ppermute x1, starting transfers between devices, block(): half_other = lax.ppermute(half_own, 'atoms', partner)  4.96 us
    ppermute x9, waiting for transfers between devices, from_role(): lax.ppermute(block, 'role', [((i + shift) % roles, i) for i in range(role...  4.5 us
    ppermute x1, starting transfers between devices, block(): got = lax.ppermute(sent, 'atoms', partner)  3.86 us
  transfers between devices with their start and end apart: 14, of which 4 were waited for; matrix products, arithmetic and copies ran while one was open for 0% of the time, Pallas kernels for 23%

profile of v7, /device:TPU:1, one launch (start us, length us, event | category | flops | bytes accessed | tf_op | source)
XLA Modules:
  0.0 87.1 jit_solution(7980466102558143495)
XLA Ops:
  0.0 0.0 copy-start
  0.0 3.7 %collective-permute-start.7 = (bf16[256,256]{1,0:T(8,128)(2,1)}, bf16[256,256]{1,0:T(8,128)(2,1)S(1)}, u32[]{:S(2)}, u32[]{:S(2)}) collective-permute-start(bf16[256,256]{1,0:T(8,128)(2,1)} %bitcast.9), channel_id=1, source_target_pairs={{128,0},{192,64},{0,128},{64,192},{129,1},{193,65},{1,129},{65,193... | collective-permute-start | bytes 393224 | tf_op jit(solution)/shard_map/ppermute | solution.py:391
  3.7 0.8 collective-permute-start.1
  4.5 0.7 collective-permute-start
  5.2 0.0 copy-start.1
  5.2 0.8 copy-done.1
  6.0 0.0 copy-start.10
  6.0 0.7 copy-done.10
  6.6 0.0 copy-start.6
  6.6 0.2 shard_map.118
  6.8 0.8 collective-permute-start.6
  7.6 2.1 %collective-permute-start.3 = (f32[3,256]{1,0:T(4,128)S(1)}, f32[3,256]{1,0:T(4,128)S(1)}, u32[]{:S(2)}, u32[]{:S(2)}) collective-permute-start(f32[3,256]{1,0:T(4,128)S(1)} %get-tuple-element.19.refs_4_.p1.refs_0_), channel_id=1, source_target_pairs={{64,0},{128,64},{192,128},{0,192},{65,1},{129,65},{193,129},{1,193... | collective-permute-start | bytes 9224 | tf_op jit(solution)/shard_map/ppermute | solution.py:391
  9.7 1.2 %collective-permute-done.6.refs_3_ = f32[3,256]{1,0:T(4,128)S(1)} collective-permute-done((f32[3,256]{1,0:T(4,128)S(1)}, f32[3,256]{1,0:T(4,128)S(1)}, u32[]{:S(2)}, u32[]{:S(2)}) %collective-permute-start.6) | collective-permute-done | bytes 3104 | tf_op jit(solution)/shard_map/ppermute | solution.py:391
  10.9 0.4 collective-permute-start.2
  11.3 0.0 collective-permute-done.3.refs_5_.p2.refs_1_
  11.3 3.3 %collective-permute-done.2.refs_3_.p0.refs_2_ = f32[3,256]{1,0:T(4,128)S(1)} collective-permute-done((f32[3,256]{1,0:T(4,128)S(1)}, f32[3,256]{1,0:T(4,128)S(1)}, u32[]{:S(2)}, u32[]{:S(2)}) %collective-permute-start.2) | collective-permute-done | bytes 3104 | tf_op jit(solution)/shard_map/ppermute | solution.py:391
  14.6 2.9 %shard_map.124.refs_5_.table = bf16[1024,1024]{1,0:T(8,128)(2,1)S(1)} custom-call(f32[3,256]{1,0:T(4,128)S(1)} %get-tuple-element.19.refs_4_.p1.refs_0_, f32[3,256]{1,0:T(4,128)S(1)} %collective-permute-done.3.refs_5_.p2.refs_1_, f32[3,256]{1,0:T(4,128)S(1)} %collective-permute-done.2.refs_3_.p0.refs_2_, f32[3,256]{1,0:T(4,128)S(1)} %collective-permute-done.6.refs_3_, ...), custom_call_target="tpu_custom_call" | custom-call | flops 20971520 | bytes 4194304 | tf_op jit(solution)/shard_map/pallas_call | solution.py:31
  17.5 0.0 collective-permute-done.7.refs_3_
  17.5 0.0 collective-permute-done.1.refs_2_.r2.refs_1_
  17.5 0.0 collective-permute-done.refs_0_.r0.refs_2_
  17.5 0.0 copy-done
  17.5 0.0 copy-done.6
  17.5 0.7 shard_map.125
  18.2 3.9 %collective-permute-start.8 = (bf16[512,256]{1,0:T(8,128)(2,1)S(1)}, bf16[512,256]{1,0:T(8,128)(2,1)S(1)}, u32[]{:S(2)}, u32[]{:S(2)}) collective-permute-start(bf16[512,256]{1,0:T(8,128)(2,1)S(1)} %get-tuple-element.28), channel_id=1, source_target_pairs={{0,1},{1,0},{2,3},{3,2},{4,5},{5,4},{6,7},{7,6},{8,9},{9,8},{10,11... | collective-permute-start | bytes 786440 | tf_op jit(solution)/shard_map/ppermute | solution.py:435
  22.1 0.0 copy-start.2
  22.1 0.0 copy-start.11
  22.1 0.4 shard_map.126.own_ref
  22.5 0.7 collective-permute-done.8.got_ref
  23.3 20.5 %all_to_all.10.mine_ref = bf16[32,16,256]{2,1,0:T(8,128)(2,1)S(1)} all-to-all(bf16[32,16,256]{2,1,0:T(8,128)(2,1)S(1)} %bitcast.18), channel_id=1, replica_groups={{0,2,4,6,8,10,12,14,16,18,20,22,24,26,28,30,32,34,36,38,40,42,44,46,48,..., dimensions={0} | all-to-all | bytes 524288 | tf_op jit(solution)/shard_map/all_to_all | solution.py:463
  43.8 0.0 copy-start.3
  43.8 0.0 copy-start.9
  43.8 0.0 copy-start.12
  43.8 0.0 copy-done.2
  43.8 0.0 copy-done.11
  43.9 0.8 shard_map.128
  44.7 6.7 %all-to-all-start.1 = ((bf16[32,16,256]{2,1,0:T(8,128)(2,1)}), bf16[32,16,256]{2,1,0:T(8,128)(2,1)S(1)}, u32[]{:S(2)}, u32[]{:S(2)}) async-start(bf16[32,16,256]{2,1,0:T(8,128)(2,1)} %shard_map.128), calls=%async_computation.1 | async-start | bytes 524288 | tf_op jit(solution)/shard_map/all_to_all | solution.py:471
  51.4 0.1 shard_map.119
  51.5 1.5 %collective-permute-start.5 = (bf16[3,288,256]{2,1,0:T(8,128)(2,1)S(1)}, bf16[3,288,256]{2,1,0:T(8,128)(2,1)S(1)}, u32[]{:S(2)}, u32[]{:S(2)}) collective-permute-start(bf16[3,288,256]{2,1,0:T(8,128)(2,1)S(1)} %shard_map.119), channel_id=1, source_target_pairs={{1,0},{2,1},{3,2},{4,3},{5,4},{6,5},{7,6},{8,7},{9,8},{10,9},{11,1... | collective-permute-start | bytes 1327112 | tf_op jit(solution)/shard_map/ppermute | solution.py:394
  53.0 1.5 %collective-permute-start.4 = (bf16[3,288,256]{2,1,0:T(8,128)(2,1)S(1)}, bf16[3,288,256]{2,1,0:T(8,128)(2,1)S(1)}, u32[]{:S(2)}, u32[]{:S(2)}) collective-permute-start(bf16[3,288,256]{2,1,0:T(8,128)(2,1)S(1)} %shard_map.119), channel_id=1, source_target_pairs={{63,0},{0,1},{1,2},{2,3},{3,4},{4,5},{5,6},{6,7},{7,8},{8,9},{9,10... | collective-permute-start | bytes 1327112 | tf_op jit(solution)/shard_map/ppermute | solution.py:394
  54.5 6.6 %all-to-all-done.1 = bf16[32,16,256]{2,1,0:T(8,128)(2,1)S(1)} async-done(((bf16[32,16,256]{2,1,0:T(8,128)(2,1)}), bf16[32,16,256]{2,1,0:T(8,128)(2,1)S(1)}, u32[]{:S(2)}, u32[]{:S(2)}) %all-to-all-start.1) | async-done | bytes 262176 | tf_op jit(solution)/shard_map/all_to_all | solution.py:471
  61.1 5.0 %collective-permute-start.9 = (bf16[512,256]{1,0:T(8,128)(2,1)S(1)}, bf16[512,256]{1,0:T(8,128)(2,1)S(1)}, u32[]{:S(2)}, u32[]{:S(2)}) collective-permute-start(bf16[512,256]{1,0:T(8,128)(2,1)S(1)} %bitcast.16), channel_id=1, source_target_pairs={{0,1},{1,0},{2,3},{3,2},{4,5},{5,4},{6,7},{7,6},{8,9},{9,8},{10,11... | collective-permute-start | bytes 786440 | tf_op jit(solution)/shard_map/ppermute | solution.py:474
  66.0 3.4 %shard_map.123.table_ref = bf16[1024,1024]{1,0:T(8,128)(2,1)S(1)} custom-call(f32[3,256]{1,0:T(4,128)S(1)} %get-tuple-element.19.refs_4_.p1.refs_0_, f32[3,256]{1,0:T(4,128)S(1)} %collective-permute-done.3.refs_5_.p2.refs_1_, f32[3,256]{1,0:T(4,128)S(1)} %collective-permute-done.2.refs_3_.p0.refs_2_, f32[3,256]{1,0:T(4,128)S(1)} %collective-permute-done.6.refs_3_, ...), custom_call_target="tpu_custom_call" | custom-call | flops 20971520 | bytes 2097152 | tf_op jit(solution)/shard_map/pallas_call | solution.py:31
  69.4 0.0 collective-permute-done.5.high_ref
  69.4 0.0 collective-permute-done.4.low_ref
  69.4 0.0 copy-done.3
  69.4 0.0 copy-done.4
  69.4 0.0 copy-done.7
  69.4 0.0 copy-done.8
  69.5 0.0 copy-done.9
  69.5 0.0 copy-done.12
  69.5 1.4 %shard_map.120 = (f32[4624,128]{1,0:T(8,128)S(1)}, bf16[256,128]{1,0:T(8,128)(2,1)S(1)}, s32[32,256]{1,0:T(8,128)S(1)}, bf16[64,256]{1,0:T(8,128)(2,1)S(1)}, f32...) custom-call(bf16[256,256]{1,0:T(8,128)(2,1)S(1)} %collective-permute-done.refs_0_.r0.refs_2_, ...), custom_call_target="tpu_custom_call" | custom-call | flops 301989888 | bytes 4194304 | tf_op jit(solution)/shard_map/pallas_call | solution.py:31
  70.9 0.0 collective-permute-done.9.other_ref
  70.9 0.7 shard_map.129
  71.6 0.1 collective-permute-start.10
  71.7 2.7 %collective-permute-start.11 = (bf16[256,256]{1,0:T(8,128)(2,1)S(1)}, bf16[256,256]{1,0:T(8,128)(2,1)S(1)}, u32[]{:S(2)}, u32[]{:S(2)}) collective-permute-start(bf16[256,256]{1,0:T(8,128)(2,1)S(1)} %get-tuple-element.31), channel_id=1, source_target_pairs={{64,0},{128,64},{192,128},{0,192},{65,1},{129,65},{193,129},{1,193... | collective-permute-start | bytes 393224 | tf_op jit(solution)/shard_map/ppermute | solution.py:391
  74.4 0.0 collective-permute-start.12
  74.4 5.9 %shard_map.121.refs_0_ = f32[256,256]{1,0:T(8,128)S(1)} custom-call(bf16[256,128]{1,0:T(8,128)(2,1)S(1)} %get-tuple-element.20.cols_ref, f32[4624,128]{1,0:T(8,128)S(1)} %get-tuple-element.21.table, s32[32,256]{1,0:T(8,128)S(1)} %get-tuple-element.22.row_at, bf16[64,256]{1,0:T(8,128)(2,1)S(1)} %get-tuple-element.23.wrbf_ref, ...), custom_call_target="tpu_custom_call" | custom-call | flops 1073741824 | bytes 4194304 | tf_op jit(solution)/shard_map/pallas_call | solution.py:31
  80.3 0.0 copy-start.5
  80.3 5.9 %shard_map.122.short_ref = f32[256,256]{1,0:T(8,128)S(1)} custom-call(bf16[256,128]{1,0:T(8,128)(2,1)S(1)} %get-tuple-element.20.cols_ref, f32[4624,128]{1,0:T(8,128)S(1)} %get-tuple-element.21.table, s32[32,256]{1,0:T(8,128)S(1)} %get-tuple-element.22.row_at, bf16[64,256]{1,0:T(8,128)(2,1)S(1)} %copy-done.9, f32[1,256]{1,0:T(1,128)S(1)} %bitcast.24, ...), custom_call_target="tpu_custom_call" | custom-call | flops 1073741824 | bytes 4194304 | tf_op jit(solution)/shard_map/pallas_call | solution.py:31
  86.2 0.0 collective-permute-done.10.e1_ref
  86.2 0.0 collective-permute-done.11.e2_ref
  86.2 0.0 collective-permute-done.12.e3_ref
  86.2 0.0 copy-done.5
  86.2 0.9 %shard_map.130 = bf16[256,256]{1,0:T(8,128)(2,1)} custom-call(bf16[256,256]{1,0:T(8,128)(2,1)S(1)} %bitcast.15, f32[256,256]{1,0:T(8,128)S(1)} %shard_map.122.short_ref, bf16[256,256]{1,0:T(8,128)(2,1)S(1)} %get-tuple-element.29.e0_ref, bf16[256,256]{1,0:T(8,128)(2,1)S(1)} %collective-permute-done.10.e1_ref, ...), custom_call_target="tpu_custom_call" | custom-call | flops 33554432 | bytes 1048576 | tf_op jit(solution)/shard_map/pallas_call | solution.py:31
  (4 shorter events, 0.1 us)
Async XLA Ops:
  0.0 17.5 %copy-start = (bf16[1,1,256,256]{3,2,1,0:T(8,128)(2,1)S(1)}, bf16[1,1,256,256]{3,2,1,0:T(8,128)(2,1)}, u32[]{:S(2)}) copy-start(bf16[1,1,256,256]{3,2,1,0:T(8,128)(2,1)} %param.12) | copy-start | bytes 393220
  0.0 17.5 %collective-permute-start.7 = (bf16[256,256]{1,0:T(8,128)(2,1)}, bf16[256,256]{1,0:T(8,128)(2,1)S(1)}, u32[]{:S(2)}, u32[]{:S(2)}) collective-permute-start(bf16[256,256]{1,0:T(8,128)(2,1)} %bitcast.9), channel_id=1, source_target_pairs={{128,0},{192,64},{0,128},{64,192},{129,1},{193,65},{1,129},{65,193... | collective-permute-start | bytes 393224 | tf_op jit(solution)/shard_map/ppermute | solution.py:391
  3.7 13.7 %collective-permute-start.1 = (bf16[256,256]{1,0:T(8,128)(2,1)}, bf16[256,256]{1,0:T(8,128)(2,1)S(1)}, u32[]{:S(2)}, u32[]{:S(2)}) collective-permute-start(bf16[256,256]{1,0:T(8,128)(2,1)} %bitcast.10), channel_id=1, source_target_pairs={{64,0},{128,64},{192,128},{0,192},{65,1},{129,65},{193,129},{1,193... | collective-permute-start | bytes 393224 | tf_op jit(solution)/shard_map/ppermute | solution.py:391
  4.5 13.0 %collective-permute-start = (bf16[256,256]{1,0:T(8,128)(2,1)}, bf16[256,256]{1,0:T(8,128)(2,1)S(1)}, u32[]{:S(2)}, u32[]{:S(2)}) collective-permute-start(bf16[256,256]{1,0:T(8,128)(2,1)} %bitcast.11), channel_id=1, source_target_pairs={{192,0},{0,64},{64,128},{128,192},{193,1},{1,65},{65,129},{129,193... | collective-permute-start | bytes 393224 | tf_op jit(solution)/shard_map/ppermute | solution.py:391
  5.2 0.8 copy-start.1
  6.0 0.7 copy-start.10
  6.6 10.9 %copy-start.6 = (bf16[256,256]{1,0:T(8,128)(2,1)S(1)}, bf16[256,256]{1,0:T(8,128)(2,1)}, u32[]{:S(2)}) copy-start(bf16[256,256]{1,0:T(8,128)(2,1)} %refs_4_.3) | copy-start | bytes 393220
  6.8 4.1 %collective-permute-start.6 = (f32[3,256]{1,0:T(4,128)S(1)}, f32[3,256]{1,0:T(4,128)S(1)}, u32[]{:S(2)}, u32[]{:S(2)}) collective-permute-start(f32[3,256]{1,0:T(4,128)S(1)} %get-tuple-element.19.refs_4_.p1.refs_0_), channel_id=1, source_target_pairs={{128,0},{192,64},{0,128},{64,192},{129,1},{193,65},{1,129},{65,193... | collective-permute-start | bytes 9224 | tf_op jit(solution)/shard_map/ppermute | solution.py:391
  7.6 3.7 %collective-permute-start.3 = (f32[3,256]{1,0:T(4,128)S(1)}, f32[3,256]{1,0:T(4,128)S(1)}, u32[]{:S(2)}, u32[]{:S(2)}) collective-permute-start(f32[3,256]{1,0:T(4,128)S(1)} %get-tuple-element.19.refs_4_.p1.refs_0_), channel_id=1, source_target_pairs={{64,0},{128,64},{192,128},{0,192},{65,1},{129,65},{193,129},{1,193... | collective-permute-start | bytes 9224 | tf_op jit(solution)/shard_map/ppermute | solution.py:391
  10.9 3.7 %collective-permute-start.2 = (f32[3,256]{1,0:T(4,128)S(1)}, f32[3,256]{1,0:T(4,128)S(1)}, u32[]{:S(2)}, u32[]{:S(2)}) collective-permute-start(f32[3,256]{1,0:T(4,128)S(1)} %get-tuple-element.19.refs_4_.p1.refs_0_), channel_id=1, source_target_pairs={{192,0},{0,64},{64,128},{128,192},{193,1},{1,65},{65,129},{129,193... | collective-permute-start | bytes 9224 | tf_op jit(solution)/shard_map/ppermute | solution.py:391
  18.2 5.0 %collective-permute-start.8 = (bf16[512,256]{1,0:T(8,128)(2,1)S(1)}, bf16[512,256]{1,0:T(8,128)(2,1)S(1)}, u32[]{:S(2)}, u32[]{:S(2)}) collective-permute-start(bf16[512,256]{1,0:T(8,128)(2,1)S(1)} %get-tuple-element.28), channel_id=1, source_target_pairs={{0,1},{1,0},{2,3},{3,2},{4,5},{5,4},{6,7},{7,6},{8,9},{9,8},{10,11... | collective-permute-start | bytes 786440 | tf_op jit(solution)/shard_map/ppermute | solution.py:435
  22.1 21.8 %copy-start.2 = (s32[3,2048]{1,0:T(4,128)S(1)}, s32[3,2048]{1,0:T(4,128)}, u32[]{:S(2)}) copy-start(s32[3,2048]{1,0:T(4,128)} %wave_ref.1) | copy-start | bytes 73732
  22.1 21.8 %copy-start.11 = (f32[256]{0:T(256)S(1)}, f32[256]{0:T(256)}, u32[]{:S(2)}) copy-start(f32[256]{0:T(256)} %param.17) | copy-start | bytes 3076
  43.8 25.6 %copy-start.3 = (bf16[256,256]{1,0:T(8,128)(2,1)S(1)}, bf16[256,256]{1,0:T(8,128)(2,1)}, u32[]{:S(2)}) copy-start(bf16[256,256]{1,0:T(8,128)(2,1)} %win_ref.1) | copy-start | bytes 393220
  43.8 25.6 %copy-start.4 = (bf16[256,256]{1,0:T(8,128)(2,1)S(1)}, bf16[256,256]{1,0:T(8,128)(2,1)}, u32[]{:S(2)}) copy-start(bf16[256,256]{1,0:T(8,128)(2,1)} %wf_ref.3) | copy-start | bytes 393220
  43.8 25.6 %copy-start.7 = (s32[1,1,32,256]{3,2,1,0:T(8,128)S(1)}, s32[1,1,32,256]{3,2,1,0:T(8,128)}, u32[]{:S(2)}) copy-start(s32[1,1,32,256]{3,2,1,0:T(8,128)} %param.14) | copy-start | bytes 98308
  43.8 25.6 %copy-start.8 = (s32[1,1,32,256]{3,2,1,0:T(8,128)S(1)}, s32[1,1,32,256]{3,2,1,0:T(8,128)}, u32[]{:S(2)}) copy-start(s32[1,1,32,256]{3,2,1,0:T(8,128)} %param.15) | copy-start | bytes 98308
  43.8 25.6 %copy-start.9 = (bf16[64,256]{1,0:T(8,128)(2,1)S(1)}, bf16[64,256]{1,0:T(8,128)(2,1)}, u32[]{:S(2)}) copy-start(bf16[64,256]{1,0:T(8,128)(2,1)} %wrbf_ref.3) | copy-start | bytes 98308
  43.8 25.6 %copy-start.12 = (f32[256]{0:T(256)S(1)}, f32[256]{0:T(256)}, u32[]{:S(2)}) copy-start(f32[256]{0:T(256)} %param.21) | copy-start | bytes 3076
  44.7 16.4 %all-to-all-start.1 = ((bf16[32,16,256]{2,1,0:T(8,128)(2,1)}), bf16[32,16,256]{2,1,0:T(8,128)(2,1)S(1)}, u32[]{:S(2)}, u32[]{:S(2)}) async-start(bf16[32,16,256]{2,1,0:T(8,128)(2,1)} %shard_map.128), calls=%async_computation.1 | async-start | bytes 524288 | tf_op jit(solution)/shard_map/all_to_all | solution.py:471
  51.5 17.9 %collective-permute-start.5 = (bf16[3,288,256]{2,1,0:T(8,128)(2,1)S(1)}, bf16[3,288,256]{2,1,0:T(8,128)(2,1)S(1)}, u32[]{:S(2)}, u32[]{:S(2)}) collective-permute-start(bf16[3,288,256]{2,1,0:T(8,128)(2,1)S(1)} %shard_map.119), channel_id=1, source_target_pairs={{1,0},{2,1},{3,2},{4,3},{5,4},{6,5},{7,6},{8,7},{9,8},{10,9},{11,1... | collective-permute-start | bytes 1327112 | tf_op jit(solution)/shard_map/ppermute | solution.py:394
  53.0 16.4 %collective-permute-start.4 = (bf16[3,288,256]{2,1,0:T(8,128)(2,1)S(1)}, bf16[3,288,256]{2,1,0:T(8,128)(2,1)S(1)}, u32[]{:S(2)}, u32[]{:S(2)}) collective-permute-start(bf16[3,288,256]{2,1,0:T(8,128)(2,1)S(1)} %shard_map.119), channel_id=1, source_target_pairs={{63,0},{0,1},{1,2},{2,3},{3,4},{4,5},{5,6},{6,7},{7,8},{8,9},{9,10... | collective-permute-start | bytes 1327112 | tf_op jit(solution)/shard_map/ppermute | solution.py:394
  61.1 9.9 %collective-permute-start.9 = (bf16[512,256]{1,0:T(8,128)(2,1)S(1)}, bf16[512,256]{1,0:T(8,128)(2,1)S(1)}, u32[]{:S(2)}, u32[]{:S(2)}) collective-permute-start(bf16[512,256]{1,0:T(8,128)(2,1)S(1)} %bitcast.16), channel_id=1, source_target_pairs={{0,1},{1,0},{2,3},{3,2},{4,5},{5,4},{6,7},{7,6},{8,9},{9,8},{10,11... | collective-permute-start | bytes 786440 | tf_op jit(solution)/shard_map/ppermute | solution.py:474
  71.6 14.6 %collective-permute-start.10 = (bf16[256,256]{1,0:T(8,128)(2,1)S(1)}, bf16[256,256]{1,0:T(8,128)(2,1)S(1)}, u32[]{:S(2)}, u32[]{:S(2)}) collective-permute-start(bf16[256,256]{1,0:T(8,128)(2,1)S(1)} %get-tuple-element.30), channel_id=1, source_target_pairs={{192,0},{0,64},{64,128},{128,192},{193,1},{1,65},{65,129},{129,193... | collective-permute-start | bytes 393224 | tf_op jit(solution)/shard_map/ppermute | solution.py:391
  71.7 14.5 %collective-permute-start.11 = (bf16[256,256]{1,0:T(8,128)(2,1)S(1)}, bf16[256,256]{1,0:T(8,128)(2,1)S(1)}, u32[]{:S(2)}, u32[]{:S(2)}) collective-permute-start(bf16[256,256]{1,0:T(8,128)(2,1)S(1)} %get-tuple-element.31), channel_id=1, source_target_pairs={{64,0},{128,64},{192,128},{0,192},{65,1},{129,65},{193,129},{1,193... | collective-permute-start | bytes 393224 | tf_op jit(solution)/shard_map/ppermute | solution.py:391
  74.4 11.8 %collective-permute-start.12 = (bf16[256,256]{1,0:T(8,128)(2,1)S(1)}, bf16[256,256]{1,0:T(8,128)(2,1)S(1)}, u32[]{:S(2)}, u32[]{:S(2)}) collective-permute-start(bf16[256,256]{1,0:T(8,128)(2,1)S(1)} %get-tuple-element.32), channel_id=1, source_target_pairs={{128,0},{192,64},{0,128},{64,192},{129,1},{193,65},{1,129},{65,193... | collective-permute-start | bytes 393224 | tf_op jit(solution)/shard_map/ppermute | solution.py:391
  80.3 6.0 %copy-start.5 = (bf16[256,256]{1,0:T(8,128)(2,1)S(1)}, bf16[256,256]{1,0:T(8,128)(2,1)}, u32[]{:S(2)}) copy-start(bf16[256,256]{1,0:T(8,128)(2,1)} %wout_ref.1) | copy-start | bytes 393220

commit v8 on v7

--- a/solution.py
+++ b/solution.py
@@ -287,19 +287,20 @@
 
 
 def short_kernel(start, count, scale, cols_ref, table, row_at, wrbf_ref, brbf_ref, wf_ref, *refs):
+    copy = pltpu.make_async_copy(row_at.at[start : start + count, :], refs[-4], refs[-1])
+    copy.start()
     lane = 128
     atoms = cols_ref.shape[0]
     slots = cols_ref.shape[1] // 4
     basis_count, width = wrbf_ref.shape
     halves = width // lane
-    *before, out_ref, near_a, near_b, at_a, at_b, pairs, bias, sems = refs
+    *before, out_ref, near_a, near_b, near_at, pairs, bias, sem = refs
     pairs[...] = jnp.zeros_like(pairs)
     pairs[0:basis_count, 0:width] = wrbf_ref[...]
     pairs[basis_count:, width:] = wrbf_ref[...]
     bias[:, 0:width] = brbf_ref[...] * math.log2(math.e)
     bias[:, width:] = brbf_ref[...] * math.log2(math.e)
     group = near_a.shape[0] // (halves * atoms)
-    ahead = at_a.shape[0]
     wide_lanes = group // 2 * lane
     out_ref[...] = before[0][...] if before else jnp.zeros_like(out_ref)
     row = lax.broadcasted_iota(jnp.int32, (lane, wide_lanes), 0)
@@ -311,16 +312,13 @@
         * ZOOM
     )
 
-    def fetch(first, buffer, sem):
-        rows = pl.ds(pl.multiple_of(first, ahead), ahead)
-        return pltpu.make_async_copy(row_at.at[rows, :], buffer, sem)
-
-    def one_group(first, buffer, offset, near):
-        for i in range(group):
-            for k in range(atoms):
-                to = (i * atoms + k) * halves
-                near[to : to + halves, :] = table[pl.ds(buffer[offset + i, k], halves), :]
-        select = (source == first).astype(jnp.float32).astype(jnp.bfloat16)
+    def gather(i, near):
+        for k in range(group * atoms):
+            row = near_at[group * i + k // atoms, k % atoms]
+            near[k * halves : (k + 1) * halves, :] = table[pl.ds(row, halves), :]
+
+    def filters_of(i):
+        select = (source == start + group * i).astype(jnp.float32).astype(jnp.bfloat16)
         wide = dot(cols_ref[...], select)
         inner = []
         for p in range(group // 2):
@@ -329,7 +327,9 @@
             value = dot(basis, pairs[...]) * math.log2(math.e) + bias[...]
             both = (jnp.log(1.0 + jnp.exp2(value)) - math.log(2.0)).astype(jnp.bfloat16)
             inner += [both[:, :width], both[:, width:]]
-        filters = dot(jnp.concatenate(inner, axis=0), wf_ref[...])
+        return dot(jnp.concatenate(inner, axis=0), wf_ref[...])
+
+    def add(filters, near):
         for h in range(halves):
             cut = slice(h * lane, (h + 1) * lane)
             total = out_ref[:, cut]
@@ -338,27 +338,14 @@
                 total = total + filters[i * atoms : (i + 1) * atoms, cut] * gathered
             out_ref[:, cut] = total
 
-    def both_groups(first, buffer):
-        one_group(first, buffer, 0, near_a)
-        one_group(first + group, buffer, group, near_b)
-
-    fetch(start, at_a, sems.at[0]).start()
-
-    def body(j, carry):
-        first = start + 2 * ahead * j
-        fetch(first, at_a, sems.at[0]).wait()
-        fetch(first + ahead, at_b, sems.at[1]).start()
-        both_groups(first, at_a)
-        fetch(first + ahead, at_b, sems.at[1]).wait()
-
-        @pl.when(first + 2 * ahead < start + count)
-        def _():
-            fetch(first + 2 * ahead, at_a, sems.at[0]).start()
-
-        both_groups(first + ahead, at_b)
-        return carry
-
-    lax.fori_loop(0, count // (2 * ahead), body, 0)
+    filters = filters_of(0)
+    copy.wait()
+    for i in range(count // group):
+        near = (near_a, near_b)[i % 2]
+        gather(i, near)
+        following = filters_of(i + 1) if group * (i + 1) < count else None
+        add(filters, near)
+        filters = following
     out_ref[...] = out_ref[...] * scale
 
 
@@ -500,7 +487,7 @@
         flops=2 * 9 * atoms * width * width,
         nbytes=4 << 20,
     )
-    near = pltpu.VMEM((4 * atoms * width // 128, 128), f32)
+    near = pltpu.VMEM((2 * atoms * width // 128, 128), f32)
     short = ()
     for i in range(2):
         short = (
@@ -513,12 +500,12 @@
                 + ([w_rbf, b_rbf[None, :], w_filter] if i else held)
                 + [*short],
                 scratch=[near, near]
-                + [pltpu.SMEM((8, atoms), jnp.int32)] * 2
+                + [pltpu.SMEM((slots // 2, atoms), jnp.int32)]
                 + [
                     pltpu.VMEM((2 * w_rbf.shape[0], 2 * width), bf16),
                     pltpu.VMEM((1, 2 * width), f32),
                 ]
-                + [pltpu.SemaphoreType.DMA((2,))],
+                + [pltpu.SemaphoreType.DMA],
                 flops=2 * slots * atoms * width * width,
                 nbytes=4 << 20,
             ),

time: 87.4 us -> 85.1 us (0.974)
  Pallas kernels: 23.3 us -> 21 us
    pallas_call x13, Pallas kernels: 23.3 us -> 21 us  [call(): pl.pallas_call(body, out_shape=out, in_specs=spec or [VMEM] * len(ins), o...]
  transfers between devices with their start and end apart: 14 -> 14, of which waited for: 4 -> 4; matrix products, arithmetic and copies ran while one was open for 0% -> 0% of each run, Pallas kernels for 23% -> 21%
where the time goes in v8:
time: 85.1 us; the launch traced here: 84.8 us
  starting transfers between devices  29.7 us (35%)
  Pallas kernels  21 us (25%)
  blocking collectives  20.5 us (24%)
  waiting for transfers between devices  11.8 us (14%)
  local copies, waits for them, and re-layouts  1.49 us (2%)
    pallas_call x13, Pallas kernels, call(): pl.pallas_call(body, out_shape=out, in_specs=spec or [VMEM] * len(ins), o...  21 us
    all_to_all x1, blocking collectives, block(): lax.all_to_all(kept.reshape(chunks), 'atoms', 0, 0, axis_index_groups=sam...  20.5 us
    ppermute x9, starting transfers between devices, from_role(): lax.ppermute(block, 'role', [((i + shift) % roles, i) for i in range(role...  11.2 us
    all_to_all x1, starting transfers between devices, block(): lax.all_to_all(copies, 'atoms', 0, 0, axis_index_groups=same_core)  6.71 us
    all_to_all x1, waiting for transfers between devices, block(): lax.all_to_all(copies, 'atoms', 0, 0, axis_index_groups=same_core)  6.61 us
    ppermute x1, starting transfers between devices, block(): half_other = lax.ppermute(half_own, 'atoms', partner)  4.96 us
    ppermute x9, waiting for transfers between devices, from_role(): lax.ppermute(block, 'role', [((i + shift) % roles, i) for i in range(role...  4.5 us
    ppermute x1, starting transfers between devices, block(): got = lax.ppermute(sent, 'atoms', partner)  3.86 us
  transfers between devices with their start and end apart: 14, of which 4 were waited for; matrix products, arithmetic and copies ran while one was open for 0% of the time, Pallas kernels for 21%

profile of v8, /device:TPU:1, one launch (start us, length us, event | category | flops | bytes accessed | tf_op | source)
XLA Modules:
  0.0 84.8 jit_solution(16929911821336258687)
XLA Ops:
  0.0 0.0 copy-start
  0.0 3.7 %collective-permute-start.7 = (bf16[256,256]{1,0:T(8,128)(2,1)}, bf16[256,256]{1,0:T(8,128)(2,1)S(1)}, u32[]{:S(2)}, u32[]{:S(2)}) collective-permute-start(bf16[256,256]{1,0:T(8,128)(2,1)} %bitcast.9), channel_id=1, source_target_pairs={{128,0},{192,64},{0,128},{64,192},{129,1},{193,65},{1,129},{65,193... | collective-permute-start | bytes 393224 | tf_op jit(solution)/shard_map/ppermute | solution.py:378
  3.7 0.8 collective-permute-start.1
  4.5 0.7 collective-permute-start
  5.2 0.0 copy-start.1
  5.2 0.8 copy-done.1
  6.0 0.0 copy-start.10
  6.0 0.7 copy-done.10
  6.6 0.0 copy-start.6
  6.6 0.2 shard_map.118
  6.8 0.8 collective-permute-start.6
  7.6 2.1 %collective-permute-start.3 = (f32[3,256]{1,0:T(4,128)S(1)}, f32[3,256]{1,0:T(4,128)S(1)}, u32[]{:S(2)}, u32[]{:S(2)}) collective-permute-start(f32[3,256]{1,0:T(4,128)S(1)} %get-tuple-element.19.refs_4_.p1.refs_0_), channel_id=1, source_target_pairs={{64,0},{128,64},{192,128},{0,192},{65,1},{129,65},{193,129},{1,193... | collective-permute-start | bytes 9224 | tf_op jit(solution)/shard_map/ppermute | solution.py:378
  9.7 1.2 %collective-permute-done.6.refs_3_ = f32[3,256]{1,0:T(4,128)S(1)} collective-permute-done((f32[3,256]{1,0:T(4,128)S(1)}, f32[3,256]{1,0:T(4,128)S(1)}, u32[]{:S(2)}, u32[]{:S(2)}) %collective-permute-start.6) | collective-permute-done | bytes 3104 | tf_op jit(solution)/shard_map/ppermute | solution.py:378
  10.9 0.4 collective-permute-start.2
  11.3 0.0 collective-permute-done.3.refs_5_.p2.refs_1_
  11.3 3.3 %collective-permute-done.2.refs_3_.p0.refs_2_ = f32[3,256]{1,0:T(4,128)S(1)} collective-permute-done((f32[3,256]{1,0:T(4,128)S(1)}, f32[3,256]{1,0:T(4,128)S(1)}, u32[]{:S(2)}, u32[]{:S(2)}) %collective-permute-start.2) | collective-permute-done | bytes 3104 | tf_op jit(solution)/shard_map/ppermute | solution.py:378
  14.6 2.9 %shard_map.124.refs_5_.table = bf16[1024,1024]{1,0:T(8,128)(2,1)S(1)} custom-call(f32[3,256]{1,0:T(4,128)S(1)} %get-tuple-element.19.refs_4_.p1.refs_0_, f32[3,256]{1,0:T(4,128)S(1)} %collective-permute-done.3.refs_5_.p2.refs_1_, f32[3,256]{1,0:T(4,128)S(1)} %collective-permute-done.2.refs_3_.p0.refs_2_, f32[3,256]{1,0:T(4,128)S(1)} %collective-permute-done.6.refs_3_, ...), custom_call_target="tpu_custom_call" | custom-call | flops 20971520 | bytes 4194304 | tf_op jit(solution)/shard_map/pallas_call | solution.py:31
  17.5 0.0 collective-permute-done.7.refs_3_
  17.5 0.0 collective-permute-done.1.refs_2_.r2.refs_1_
  17.5 0.0 collective-permute-done.refs_0_.r0.refs_2_
  17.5 0.0 copy-done
  17.5 0.0 copy-done.6
  17.5 0.7 shard_map.125
  18.2 3.9 %collective-permute-start.8 = (bf16[512,256]{1,0:T(8,128)(2,1)S(1)}, bf16[512,256]{1,0:T(8,128)(2,1)S(1)}, u32[]{:S(2)}, u32[]{:S(2)}) collective-permute-start(bf16[512,256]{1,0:T(8,128)(2,1)S(1)} %get-tuple-element.28), channel_id=1, source_target_pairs={{0,1},{1,0},{2,3},{3,2},{4,5},{5,4},{6,7},{7,6},{8,9},{9,8},{10,11... | collective-permute-start | bytes 786440 | tf_op jit(solution)/shard_map/ppermute | solution.py:422
  22.1 0.0 copy-start.2
  22.1 0.0 copy-start.11
  22.1 0.4 shard_map.126.own_ref
  22.5 0.7 collective-permute-done.8.got_ref
  23.3 20.5 %all_to_all.10.mine_ref = bf16[32,16,256]{2,1,0:T(8,128)(2,1)S(1)} all-to-all(bf16[32,16,256]{2,1,0:T(8,128)(2,1)S(1)} %bitcast.18), channel_id=1, replica_groups={{0,2,4,6,8,10,12,14,16,18,20,22,24,26,28,30,32,34,36,38,40,42,44,46,48,..., dimensions={0} | all-to-all | bytes 524288 | tf_op jit(solution)/shard_map/all_to_all | solution.py:450
  43.8 0.0 copy-start.3
  43.8 0.0 copy-start.9
  43.8 0.0 copy-start.12
  43.8 0.0 copy-done.2
  43.8 0.0 copy-done.11
  43.9 0.8 shard_map.128
  44.7 6.7 %all-to-all-start.1 = ((bf16[32,16,256]{2,1,0:T(8,128)(2,1)}), bf16[32,16,256]{2,1,0:T(8,128)(2,1)S(1)}, u32[]{:S(2)}, u32[]{:S(2)}) async-start(bf16[32,16,256]{2,1,0:T(8,128)(2,1)} %shard_map.128), calls=%async_computation.1 | async-start | bytes 524288 | tf_op jit(solution)/shard_map/all_to_all | solution.py:458
  51.4 0.1 shard_map.119
  51.5 1.5 %collective-permute-start.5 = (bf16[3,288,256]{2,1,0:T(8,128)(2,1)S(1)}, bf16[3,288,256]{2,1,0:T(8,128)(2,1)S(1)}, u32[]{:S(2)}, u32[]{:S(2)}) collective-permute-start(bf16[3,288,256]{2,1,0:T(8,128)(2,1)S(1)} %shard_map.119), channel_id=1, source_target_pairs={{1,0},{2,1},{3,2},{4,3},{5,4},{6,5},{7,6},{8,7},{9,8},{10,9},{11,1... | collective-permute-start | bytes 1327112 | tf_op jit(solution)/shard_map/ppermute | solution.py:381
  53.0 1.5 %collective-permute-start.4 = (bf16[3,288,256]{2,1,0:T(8,128)(2,1)S(1)}, bf16[3,288,256]{2,1,0:T(8,128)(2,1)S(1)}, u32[]{:S(2)}, u32[]{:S(2)}) collective-permute-start(bf16[3,288,256]{2,1,0:T(8,128)(2,1)S(1)} %shard_map.119), channel_id=1, source_target_pairs={{63,0},{0,1},{1,2},{2,3},{3,4},{4,5},{5,6},{6,7},{7,8},{8,9},{9,10... | collective-permute-start | bytes 1327112 | tf_op jit(solution)/shard_map/ppermute | solution.py:381
  54.5 6.6 %all-to-all-done.1 = bf16[32,16,256]{2,1,0:T(8,128)(2,1)S(1)} async-done(((bf16[32,16,256]{2,1,0:T(8,128)(2,1)}), bf16[32,16,256]{2,1,0:T(8,128)(2,1)S(1)}, u32[]{:S(2)}, u32[]{:S(2)}) %all-to-all-start.1) | async-done | bytes 262176 | tf_op jit(solution)/shard_map/all_to_all | solution.py:458
  61.1 5.0 %collective-permute-start.9 = (bf16[512,256]{1,0:T(8,128)(2,1)S(1)}, bf16[512,256]{1,0:T(8,128)(2,1)S(1)}, u32[]{:S(2)}, u32[]{:S(2)}) collective-permute-start(bf16[512,256]{1,0:T(8,128)(2,1)S(1)} %bitcast.16), channel_id=1, source_target_pairs={{0,1},{1,0},{2,3},{3,2},{4,5},{5,4},{6,7},{7,6},{8,9},{9,8},{10,11... | collective-permute-start | bytes 786440 | tf_op jit(solution)/shard_map/ppermute | solution.py:461
  66.0 3.4 %shard_map.123.table_ref = bf16[1024,1024]{1,0:T(8,128)(2,1)S(1)} custom-call(f32[3,256]{1,0:T(4,128)S(1)} %get-tuple-element.19.refs_4_.p1.refs_0_, f32[3,256]{1,0:T(4,128)S(1)} %collective-permute-done.3.refs_5_.p2.refs_1_, f32[3,256]{1,0:T(4,128)S(1)} %collective-permute-done.2.refs_3_.p0.refs_2_, f32[3,256]{1,0:T(4,128)S(1)} %collective-permute-done.6.refs_3_, ...), custom_call_target="tpu_custom_call" | custom-call | flops 20971520 | bytes 2097152 | tf_op jit(solution)/shard_map/pallas_call | solution.py:31
  69.4 0.0 collective-permute-done.5.high_ref
  69.4 0.0 collective-permute-done.4.low_ref
  69.4 0.0 copy-done.3
  69.4 0.0 copy-done.4
  69.4 0.0 copy-done.7
  69.4 0.0 copy-done.8
  69.5 0.0 copy-done.9
  69.5 0.0 copy-done.12
  69.5 1.4 %shard_map.120 = (f32[4624,128]{1,0:T(8,128)S(1)}, bf16[256,128]{1,0:T(8,128)(2,1)S(1)}, s32[32,256]{1,0:T(8,128)S(1)}, bf16[64,256]{1,0:T(8,128)(2,1)S(1)}, f32...) custom-call(bf16[256,256]{1,0:T(8,128)(2,1)S(1)} %collective-permute-done.refs_0_.r0.refs_2_, ...), custom_call_target="tpu_custom_call" | custom-call | flops 301989888 | bytes 4194304 | tf_op jit(solution)/shard_map/pallas_call | solution.py:31
  70.9 0.0 collective-permute-done.9.other_ref
  70.9 0.7 shard_map.129
  71.6 0.1 collective-permute-start.10
  71.7 2.7 %collective-permute-start.11 = (bf16[256,256]{1,0:T(8,128)(2,1)S(1)}, bf16[256,256]{1,0:T(8,128)(2,1)S(1)}, u32[]{:S(2)}, u32[]{:S(2)}) collective-permute-start(bf16[256,256]{1,0:T(8,128)(2,1)S(1)} %get-tuple-element.31), channel_id=1, source_target_pairs={{64,0},{128,64},{192,128},{0,192},{65,1},{129,65},{193,129},{1,193... | collective-permute-start | bytes 393224 | tf_op jit(solution)/shard_map/ppermute | solution.py:378
  74.4 0.0 collective-permute-start.12
  74.4 4.7 %shard_map.121.refs_0_ = f32[256,256]{1,0:T(8,128)S(1)} custom-call(bf16[256,128]{1,0:T(8,128)(2,1)S(1)} %get-tuple-element.20.cols_ref, f32[4624,128]{1,0:T(8,128)S(1)} %get-tuple-element.21.table, s32[32,256]{1,0:T(8,128)S(1)} %get-tuple-element.22.row_at, bf16[64,256]{1,0:T(8,128)(2,1)S(1)} %get-tuple-element.23.wrbf_ref, ...), custom_call_target="tpu_custom_call" | custom-call | flops 1073741824 | bytes 4194304 | tf_op jit(solution)/shard_map/pallas_call | solution.py:31
  79.1 0.0 copy-start.5
  79.1 4.8 %shard_map.122.short_ref = f32[256,256]{1,0:T(8,128)S(1)} custom-call(bf16[256,128]{1,0:T(8,128)(2,1)S(1)} %get-tuple-element.20.cols_ref, f32[4624,128]{1,0:T(8,128)S(1)} %get-tuple-element.21.table, s32[32,256]{1,0:T(8,128)S(1)} %get-tuple-element.22.row_at, bf16[64,256]{1,0:T(8,128)(2,1)S(1)} %copy-done.9, f32[1,256]{1,0:T(1,128)S(1)} %bitcast.24, ...), custom_call_target="tpu_custom_call" | custom-call | flops 1073741824 | bytes 4194304 | tf_op jit(solution)/shard_map/pallas_call | solution.py:31
  83.9 0.0 collective-permute-done.10.e1_ref
  83.9 0.0 collective-permute-done.11.e2_ref
  83.9 0.0 collective-permute-done.12.e3_ref
  83.9 0.0 copy-done.5
  84.0 0.9 %shard_map.130 = bf16[256,256]{1,0:T(8,128)(2,1)} custom-call(bf16[256,256]{1,0:T(8,128)(2,1)S(1)} %bitcast.15, f32[256,256]{1,0:T(8,128)S(1)} %shard_map.122.short_ref, bf16[256,256]{1,0:T(8,128)(2,1)S(1)} %get-tuple-element.29.e0_ref, bf16[256,256]{1,0:T(8,128)(2,1)S(1)} %collective-permute-done.10.e1_ref, ...), custom_call_target="tpu_custom_call" | custom-call | flops 33554432 | bytes 1048576 | tf_op jit(solution)/shard_map/pallas_call | solution.py:31
  (4 shorter events, 0.1 us)
Async XLA Ops:
  0.0 17.5 %copy-start = (bf16[1,1,256,256]{3,2,1,0:T(8,128)(2,1)S(1)}, bf16[1,1,256,256]{3,2,1,0:T(8,128)(2,1)}, u32[]{:S(2)}) copy-start(bf16[1,1,256,256]{3,2,1,0:T(8,128)(2,1)} %param.12) | copy-start | bytes 393220
  0.0 17.5 %collective-permute-start.7 = (bf16[256,256]{1,0:T(8,128)(2,1)}, bf16[256,256]{1,0:T(8,128)(2,1)S(1)}, u32[]{:S(2)}, u32[]{:S(2)}) collective-permute-start(bf16[256,256]{1,0:T(8,128)(2,1)} %bitcast.9), channel_id=1, source_target_pairs={{128,0},{192,64},{0,128},{64,192},{129,1},{193,65},{1,129},{65,193... | collective-permute-start | bytes 393224 | tf_op jit(solution)/shard_map/ppermute | solution.py:378
  3.7 13.7 %collective-permute-start.1 = (bf16[256,256]{1,0:T(8,128)(2,1)}, bf16[256,256]{1,0:T(8,128)(2,1)S(1)}, u32[]{:S(2)}, u32[]{:S(2)}) collective-permute-start(bf16[256,256]{1,0:T(8,128)(2,1)} %bitcast.10), channel_id=1, source_target_pairs={{64,0},{128,64},{192,128},{0,192},{65,1},{129,65},{193,129},{1,193... | collective-permute-start | bytes 393224 | tf_op jit(solution)/shard_map/ppermute | solution.py:378
  4.5 13.0 %collective-permute-start = (bf16[256,256]{1,0:T(8,128)(2,1)}, bf16[256,256]{1,0:T(8,128)(2,1)S(1)}, u32[]{:S(2)}, u32[]{:S(2)}) collective-permute-start(bf16[256,256]{1,0:T(8,128)(2,1)} %bitcast.11), channel_id=1, source_target_pairs={{192,0},{0,64},{64,128},{128,192},{193,1},{1,65},{65,129},{129,193... | collective-permute-start | bytes 393224 | tf_op jit(solution)/shard_map/ppermute | solution.py:378
  5.2 0.8 copy-start.1
  6.0 0.7 copy-start.10
  6.6 10.9 %copy-start.6 = (bf16[256,256]{1,0:T(8,128)(2,1)S(1)}, bf16[256,256]{1,0:T(8,128)(2,1)}, u32[]{:S(2)}) copy-start(bf16[256,256]{1,0:T(8,128)(2,1)} %refs_4_.3) | copy-start | bytes 393220
  6.8 4.1 %collective-permute-start.6 = (f32[3,256]{1,0:T(4,128)S(1)}, f32[3,256]{1,0:T(4,128)S(1)}, u32[]{:S(2)}, u32[]{:S(2)}) collective-permute-start(f32[3,256]{1,0:T(4,128)S(1)} %get-tuple-element.19.refs_4_.p1.refs_0_), channel_id=1, source_target_pairs={{128,0},{192,64},{0,128},{64,192},{129,1},{193,65},{1,129},{65,193... | collective-permute-start | bytes 9224 | tf_op jit(solution)/shard_map/ppermute | solution.py:378
  7.6 3.7 %collective-permute-start.3 = (f32[3,256]{1,0:T(4,128)S(1)}, f32[3,256]{1,0:T(4,128)S(1)}, u32[]{:S(2)}, u32[]{:S(2)}) collective-permute-start(f32[3,256]{1,0:T(4,128)S(1)} %get-tuple-element.19.refs_4_.p1.refs_0_), channel_id=1, source_target_pairs={{64,0},{128,64},{192,128},{0,192},{65,1},{129,65},{193,129},{1,193... | collective-permute-start | bytes 9224 | tf_op jit(solution)/shard_map/ppermute | solution.py:378
  10.9 3.7 %collective-permute-start.2 = (f32[3,256]{1,0:T(4,128)S(1)}, f32[3,256]{1,0:T(4,128)S(1)}, u32[]{:S(2)}, u32[]{:S(2)}) collective-permute-start(f32[3,256]{1,0:T(4,128)S(1)} %get-tuple-element.19.refs_4_.p1.refs_0_), channel_id=1, source_target_pairs={{192,0},{0,64},{64,128},{128,192},{193,1},{1,65},{65,129},{129,193... | collective-permute-start | bytes 9224 | tf_op jit(solution)/shard_map/ppermute | solution.py:378
  18.2 5.0 %collective-permute-start.8 = (bf16[512,256]{1,0:T(8,128)(2,1)S(1)}, bf16[512,256]{1,0:T(8,128)(2,1)S(1)}, u32[]{:S(2)}, u32[]{:S(2)}) collective-permute-start(bf16[512,256]{1,0:T(8,128)(2,1)S(1)} %get-tuple-element.28), channel_id=1, source_target_pairs={{0,1},{1,0},{2,3},{3,2},{4,5},{5,4},{6,7},{7,6},{8,9},{9,8},{10,11... | collective-permute-start | bytes 786440 | tf_op jit(solution)/shard_map/ppermute | solution.py:422
  22.1 21.8 %copy-start.2 = (s32[3,2048]{1,0:T(4,128)S(1)}, s32[3,2048]{1,0:T(4,128)}, u32[]{:S(2)}) copy-start(s32[3,2048]{1,0:T(4,128)} %wave_ref.1) | copy-start | bytes 73732
  22.1 21.8 %copy-start.11 = (f32[256]{0:T(256)S(1)}, f32[256]{0:T(256)}, u32[]{:S(2)}) copy-start(f32[256]{0:T(256)} %param.17) | copy-start | bytes 3076
  43.8 25.6 %copy-start.3 = (bf16[256,256]{1,0:T(8,128)(2,1)S(1)}, bf16[256,256]{1,0:T(8,128)(2,1)}, u32[]{:S(2)}) copy-start(bf16[256,256]{1,0:T(8,128)(2,1)} %win_ref.1) | copy-start | bytes 393220
  43.8 25.6 %copy-start.4 = (bf16[256,256]{1,0:T(8,128)(2,1)S(1)}, bf16[256,256]{1,0:T(8,128)(2,1)}, u32[]{:S(2)}) copy-start(bf16[256,256]{1,0:T(8,128)(2,1)} %wf_ref.3) | copy-start | bytes 393220
  43.8 25.6 %copy-start.7 = (s32[1,1,32,256]{3,2,1,0:T(8,128)S(1)}, s32[1,1,32,256]{3,2,1,0:T(8,128)}, u32[]{:S(2)}) copy-start(s32[1,1,32,256]{3,2,1,0:T(8,128)} %param.14) | copy-start | bytes 98308
  43.8 25.6 %copy-start.8 = (s32[1,1,32,256]{3,2,1,0:T(8,128)S(1)}, s32[1,1,32,256]{3,2,1,0:T(8,128)}, u32[]{:S(2)}) copy-start(s32[1,1,32,256]{3,2,1,0:T(8,128)} %param.15) | copy-start | bytes 98308
  43.8 25.6 %copy-start.9 = (bf16[64,256]{1,0:T(8,128)(2,1)S(1)}, bf16[64,256]{1,0:T(8,128)(2,1)}, u32[]{:S(2)}) copy-start(bf16[64,256]{1,0:T(8,128)(2,1)} %wrbf_ref.3) | copy-start | bytes 98308
  43.8 25.6 %copy-start.12 = (f32[256]{0:T(256)S(1)}, f32[256]{0:T(256)}, u32[]{:S(2)}) copy-start(f32[256]{0:T(256)} %param.21) | copy-start | bytes 3076
  44.7 16.4 %all-to-all-start.1 = ((bf16[32,16,256]{2,1,0:T(8,128)(2,1)}), bf16[32,16,256]{2,1,0:T(8,128)(2,1)S(1)}, u32[]{:S(2)}, u32[]{:S(2)}) async-start(bf16[32,16,256]{2,1,0:T(8,128)(2,1)} %shard_map.128), calls=%async_computation.1 | async-start | bytes 524288 | tf_op jit(solution)/shard_map/all_to_all | solution.py:458
  51.5 17.9 %collective-permute-start.5 = (bf16[3,288,256]{2,1,0:T(8,128)(2,1)S(1)}, bf16[3,288,256]{2,1,0:T(8,128)(2,1)S(1)}, u32[]{:S(2)}, u32[]{:S(2)}) collective-permute-start(bf16[3,288,256]{2,1,0:T(8,128)(2,1)S(1)} %shard_map.119), channel_id=1, source_target_pairs={{1,0},{2,1},{3,2},{4,3},{5,4},{6,5},{7,6},{8,7},{9,8},{10,9},{11,1... | collective-permute-start | bytes 1327112 | tf_op jit(solution)/shard_map/ppermute | solution.py:381
  53.0 16.4 %collective-permute-start.4 = (bf16[3,288,256]{2,1,0:T(8,128)(2,1)S(1)}, bf16[3,288,256]{2,1,0:T(8,128)(2,1)S(1)}, u32[]{:S(2)}, u32[]{:S(2)}) collective-permute-start(bf16[3,288,256]{2,1,0:T(8,128)(2,1)S(1)} %shard_map.119), channel_id=1, source_target_pairs={{63,0},{0,1},{1,2},{2,3},{3,4},{4,5},{5,6},{6,7},{7,8},{8,9},{9,10... | collective-permute-start | bytes 1327112 | tf_op jit(solution)/shard_map/ppermute | solution.py:381
  61.1 9.9 %collective-permute-start.9 = (bf16[512,256]{1,0:T(8,128)(2,1)S(1)}, bf16[512,256]{1,0:T(8,128)(2,1)S(1)}, u32[]{:S(2)}, u32[]{:S(2)}) collective-permute-start(bf16[512,256]{1,0:T(8,128)(2,1)S(1)} %bitcast.16), channel_id=1, source_target_pairs={{0,1},{1,0},{2,3},{3,2},{4,5},{5,4},{6,7},{7,6},{8,9},{9,8},{10,11... | collective-permute-start | bytes 786440 | tf_op jit(solution)/shard_map/ppermute | solution.py:461
  71.6 12.3 %collective-permute-start.10 = (bf16[256,256]{1,0:T(8,128)(2,1)S(1)}, bf16[256,256]{1,0:T(8,128)(2,1)S(1)}, u32[]{:S(2)}, u32[]{:S(2)}) collective-permute-start(bf16[256,256]{1,0:T(8,128)(2,1)S(1)} %get-tuple-element.30), channel_id=1, source_target_pairs={{192,0},{0,64},{64,128},{128,192},{193,1},{1,65},{65,129},{129,193... | collective-permute-start | bytes 393224 | tf_op jit(solution)/shard_map/ppermute | solution.py:378
  71.7 12.2 %collective-permute-start.11 = (bf16[256,256]{1,0:T(8,128)(2,1)S(1)}, bf16[256,256]{1,0:T(8,128)(2,1)S(1)}, u32[]{:S(2)}, u32[]{:S(2)}) collective-permute-start(bf16[256,256]{1,0:T(8,128)(2,1)S(1)} %get-tuple-element.31), channel_id=1, source_target_pairs={{64,0},{128,64},{192,128},{0,192},{65,1},{129,65},{193,129},{1,193... | collective-permute-start | bytes 393224 | tf_op jit(solution)/shard_map/ppermute | solution.py:378
  74.4 9.5 %collective-permute-start.12 = (bf16[256,256]{1,0:T(8,128)(2,1)S(1)}, bf16[256,256]{1,0:T(8,128)(2,1)S(1)}, u32[]{:S(2)}, u32[]{:S(2)}) collective-permute-start(bf16[256,256]{1,0:T(8,128)(2,1)S(1)} %get-tuple-element.32), channel_id=1, source_target_pairs={{128,0},{192,64},{0,128},{64,192},{129,1},{193,65},{1,129},{65,193... | collective-permute-start | bytes 393224 | tf_op jit(solution)/shard_map/ppermute | solution.py:378
  79.1 4.8 %copy-start.5 = (bf16[256,256]{1,0:T(8,128)(2,1)S(1)}, bf16[256,256]{1,0:T(8,128)(2,1)}, u32[]{:S(2)}) copy-start(bf16[256,256]{1,0:T(8,128)(2,1)} %wout_ref.1) | copy-start | bytes 393220
